TPU v7x, 512 devices: a whole 4x4x16 slice. The times are simulated.
512 devices in a mesh: slab: 32 (over y, z_hi, x), shots: 16 (over z_lo, core).
Axes of the slice: x: 4, y: 4, z: 16 (z_hi: 2, z_lo: 8; z = z_hi * 8 + z_lo), core: 2. Of those that a mesh axis runs over, the one named last changes fastest.
Arguments:
- src_prev: float32 [32, 256, 64, 128], P('shots', 'slab'), may hold values from -6 to 6
- src_cur: float32 [32, 256, 64, 128], P('shots', 'slab'), may hold values from -6 to 6
- rcv_prev: float32 [32, 256, 64, 128], P('shots', 'slab'), may hold values from -6 to 6
- rcv_cur: float32 [32, 256, 64, 128], P('shots', 'slab'), may hold values from -6 to 6
- velocity: float32 [256, 64, 128], P('slab'), may hold values from 0.05 to 0.18
- wavelet: float32 [2, 32], P(None, 'shots'), may hold values from -6 to 6
- residual_traces: float32 [2, 32, 256], P(None, 'shots'), may hold values from -6 to 6
- source_depth: int32 [32], P('shots'), may hold values from 0 to 255
- source_y: int32 [32], P('shots'), may hold values from 21 to 42
- source_x: int32 [32], P('shots'), may hold values from 42 to 85
- half_y: int32 [32], P('shots'), may hold values from 10 to 21
- half_x: int32 [32], P('shots'), may hold values from 21 to 42
- receiver_cell: int32 [32, 256], P('shots'), may hold values from 0 to 2097151
Outputs:
- src_last: float32 [32, 256, 64, 128], P('shots', 'slab')
- rcv_last: float32 [32, 256, 64, 128], P('shots', 'slab')
- image: float32 [256, 64, 128], P('slab')
All inputs are finite; a program needn't handle non-finite values.
Results may differ from a plain program's by a relative error of at most 0.0003.
Values sent between devices are 32-bit elements; how exact they have to be, the bound alone decides.
A program may use at most 64 MiB of HBM per device.

v0:
```python
import jax
import jax.numpy as jnp
from jax import lax
from jax.sharding import PartitionSpec as P

STEPS = 2


COEF = (-205.0 / 72.0, 8.0 / 5.0, -1.0 / 5.0, 8.0 / 315.0, -1.0 / 560.0)


def extended(block, sides, width):
    for axis, dim in sides:
        count = lax.axis_size(axis)
        forward = [(i, i + 1) for i in range(count - 1)]
        backward = [(target, source) for source, target in forward]
        low = lax.ppermute(
            lax.slice_in_dim(block, block.shape[dim] - width, None, axis=dim), axis, forward
        )
        high = lax.ppermute(lax.slice_in_dim(block, 0, width, axis=dim), axis, backward)
        block = jnp.concatenate([low, block, high], axis=dim)
    return block


def laplace(padded):
    axis_z = padded.ndim - 3
    length = padded.shape[axis_z] - 8
    center = lax.slice_in_dim(padded, 4, 4 + length, axis=axis_z)
    total = 3.0 * COEF[0] * center
    for shift_k in range(1, 5):
        upper = lax.slice_in_dim(padded, 4 + shift_k, 4 + shift_k + length, axis=axis_z)
        lower = lax.slice_in_dim(padded, 4 - shift_k, 4 - shift_k + length, axis=axis_z)
        total = total + COEF[shift_k] * (upper + lower)
    widths = [(0, 0)] * (center.ndim - 2) + [(4, 4), (4, 4)]
    plane = jnp.pad(center, widths)
    rows_y = center.shape[-2]
    cols_x = center.shape[-1]
    for shift_k in range(1, 5):
        side_y = (
            plane[..., 4 + shift_k : 4 + shift_k + rows_y, 4 : 4 + cols_x]
            + plane[..., 4 - shift_k : 4 - shift_k + rows_y, 4 : 4 + cols_x]
        )
        side_x = (
            plane[..., 4 : 4 + rows_y, 4 + shift_k : 4 + shift_k + cols_x]
            + plane[..., 4 : 4 + rows_y, 4 - shift_k : 4 - shift_k + cols_x]
        )
        total = total + COEF[shift_k] * (side_y + side_x)
    return total


def band_mask(source_y, source_x, half_y, half_x, rows_y, cols_x):
    grid_y = jnp.arange(rows_y, dtype=jnp.int32)
    grid_x = jnp.arange(cols_x, dtype=jnp.int32)
    inside_y = jnp.abs(grid_y[None, :, None] - source_y[:, None, None]) <= half_y[:, None, None]
    inside_x = jnp.abs(grid_x[None, None, :] - source_x[:, None, None]) <= half_x[:, None, None]
    return (inside_y & inside_x).astype(jnp.float32)


def inject(cells, values, begin, length, rows_y, cols_x):
    plane = rows_y * cols_x
    depth = cells // plane
    rest = cells - depth * plane
    local = depth - begin
    valid = (local >= 0) & (local < length)
    flat = jnp.where(valid, local * plane + rest, 0)
    amounts = jnp.where(valid, values, jnp.zeros_like(values))
    count = cells.shape[0]
    rows = jnp.broadcast_to(jnp.arange(count, dtype=jnp.int32)[:, None], flat.shape)
    field = jnp.zeros((count, length * plane), jnp.float32).at[rows, flat].add(amounts)
    return field.reshape(count, length, rows_y, cols_x)


def per_device(
    src_prev,
    src_cur,
    rcv_prev,
    rcv_cur,
    velocity,
    wavelet,
    residual_traces,
    source_depth,
    source_y,
    source_x,
    half_y,
    half_x,
    receiver_cell,
):
    shot_count, depth, rows_y, cols_x = src_cur.shape
    start = lax.axis_index("slab") * depth
    mask = band_mask(source_y, source_x, half_y, half_x, rows_y, cols_x)[:, None]
    scells = (source_depth * rows_y * cols_x + source_y * cols_x + source_x)[:, None]
    terms = []
    up, u, vp, v = (src_prev, src_cur, rcv_prev, rcv_cur)
    for step in range(STEPS):
        stacked = jnp.stack([u, v])
        padded = extended(stacked, (("slab", 2),), 4)
        lap = laplace(padded)
        sdelta = inject(scells, wavelet[step][:, None], start, depth, rows_y, cols_x)
        rdelta = inject(receiver_cell, residual_traces[step], start, depth, rows_y, cols_x)
        sdelta, rdelta = (sdelta, rdelta)
        unew = mask * (2.0 * u - up + velocity * lap[0] + sdelta)
        vnew = mask * (2.0 * v - vp + velocity * lap[1] + rdelta)
        terms.append(jnp.sum((unew - 2.0 * u + up) * vnew, axis=0))
        up, u, vp, v = (u, unew, v, vnew)
    src_last, rcv_last = (u, v)
    local_sum = terms[0]
    for extra in terms[1:]:
        local_sum = local_sum + extra
    image = lax.psum(local_sum, "shots")
    return (src_last, rcv_last, image)


def solution(mesh):
    return jax.shard_map(
        per_device,
        mesh=mesh,
        in_specs=(
            P("shots", "slab", None, None),
            P("shots", "slab", None, None),
            P("shots", "slab", None, None),
            P("shots", "slab", None, None),
            P("slab", None, None),
            P(None, "shots"),
            P(None, "shots", None),
            P("shots"),
            P("shots"),
            P("shots"),
            P("shots"),
            P("shots"),
            P("shots", None),
        ),
        out_specs=(
            P("shots", "slab", None, None),
            P("shots", "slab", None, None),
            P("slab", None, None),
        ),
        check_vma=False,
    )
```

profile of v0, /device:TPU:25, one launch (start us, length us, event | category | flops | bytes accessed | tf_op | source)
XLA Modules:
  0.0 347.9 jit_solution(7300250642595813293)
XLA Ops:
  7.3 2.3 fusion.58
  9.5 17.8 %collective-permute-start = (f32[2,2,4,64,128]{4,3,2,1,0:T(8,128)}, f32[2,2,4,64,128]{4,3,2,1,0:T(8,128)S(1)}, u32[]{:S(2)}, u32[]{:S(2)}) collective-permute-start(f32[2,2,4,64,128]{4,3,2,1,0:T(8,128)} %get-tuple-element.20), channel_id=1, source_target_pairs={{16,0},{32,16},{48,32},{64,48},{80,64},{96,80},{112,96},{128,112},... | collective-permute-start | bytes 1572872 | tf_op jit(solution)/shard_map/ppermute | solution.py:20
  27.4 1.9 collective-permute-start.1
  29.5 0.1 copy.17
  29.6 0.2 fusion.83
  29.8 0.1 broadcast.180.clone.1
  29.9 0.6 scatter_fusion
  30.6 0.1 broadcast.180.clone
  30.8 24.8 %scatter_fusion.1 = f32[2,65536]{1,0:T(2,128)S(1)} fusion(f32[2,65536]{1,0:T(2,128)S(1)} %broadcast.180.clone, s32[512]{0:T(512)S(1)} %bitcast.87, f32[512]{0:T(512)S(1)} %bitcast.111), kind=kCustom, calls=%fused_computation.1 | custom fusion | flops 512 | bytes 10240 | tf_op jit(solution)/shard_map/scatter-add | solution.py:69
  55.6 0.1 abs_compare_fusion
  55.8 0.4 copy-done.13
  56.3 0.1 and_convert_fusion
  56.4 15.1 %collective-permute-done = f32[2,2,4,64,128]{4,3,2,1,0:T(8,128)S(1)} collective-permute-done((f32[2,2,4,64,128]{4,3,2,1,0:T(8,128)}, f32[2,2,4,64,128]{4,3,2,1,0:T(8,128)S(1)}, u32[]{:S(2)}, u32[]{:S(2)}) %collective-permute-start) | collective-permute-done | bytes 524320 | tf_op jit(solution)/shard_map/ppermute | solution.py:20
  71.5 15.4 %collective-permute-done.1 = f32[2,2,4,64,128]{4,3,2,1,0:T(8,128)S(1)} collective-permute-done((f32[2,2,4,64,128]{4,3,2,1,0:T(8,128)}, f32[2,2,4,64,128]{4,3,2,1,0:T(8,128)S(1)}, u32[]{:S(2)}, u32[]{:S(2)}) %collective-permute-start.1) | collective-permute-done | bytes 524320 | tf_op jit(solution)/shard_map/ppermute | solution.py:17
  86.8 0.4 pad_maximum_fusion
  87.2 2.5 fusion.6
  89.7 0.5 fusion.71
  90.3 1.0 fusion.56
  91.3 1.9 collective-permute-start.2
  93.2 3.4 collective-permute-start.3
  96.6 0.1 broadcast.180.clone.3
  96.7 0.6 scatter_fusion.2
  97.4 0.1 broadcast.180.clone.2
  97.6 24.8 %scatter_fusion.3 = f32[2,65536]{1,0:T(2,128)S(1)} fusion(f32[2,65536]{1,0:T(2,128)S(1)} %broadcast.180.clone.2, s32[512]{0:T(512)S(1)} %bitcast.88, f32[512]{0:T(512)S(1)} %bitcast.110), kind=kCustom, calls=%fused_computation.3 | custom fusion | flops 512 | bytes 10240 | tf_op jit(solution)/shard_map/scatter-add | solution.py:69
  122.5 7.9 %collective-permute-done.2 = f32[2,2,4,64,128]{4,3,2,1,0:T(8,128)} collective-permute-done((f32[2,2,4,64,128]{4,3,2,1,0:T(8,128)}, f32[2,2,4,64,128]{4,3,2,1,0:T(8,128)}, u32[]{:S(2)}, u32[]{:S(2)}) %collective-permute-start.2) | collective-permute-done | bytes 524320 | tf_op jit(solution)/shard_map/ppermute | solution.py:20
  130.4 15.8 %collective-permute-done.3 = f32[2,2,4,64,128]{4,3,2,1,0:T(8,128)} collective-permute-done((f32[2,2,4,64,128]{4,3,2,1,0:T(8,128)}, f32[2,2,4,64,128]{4,3,2,1,0:T(8,128)}, u32[]{:S(2)}, u32[]{:S(2)}) %collective-permute-start.3) | collective-permute-done | bytes 524320 | tf_op jit(solution)/shard_map/ppermute | solution.py:17
  146.3 1.6 pad_maximum_fusion.1
  147.9 2.5 fusion.26
  150.4 1.6 multiply_reduce_fusion
  152.0 0.7 add.287
  152.7 186.7 %all-reduce.4.cloned.1.call-done = f32[8,64,128]{2,1,0:T(8,128)} async-done(((f32[8,64,128]{2,1,0:T(8,128)}), f32[8,64,128]{2,1,0:T(8,128)}) %all-reduce.4.cloned.1.call-update) | async-done | bytes 262160 | tf_op jit(solution)/shard_map/psum | solution.py:109
  339.4 1.7 copy.30
  (47 shorter events, 0.6 us)
Async XLA Ops:
  7.2 22.1 %copy-start.7 = (f32[2,2,256]{2,1,0:T(2,128)S(1)}, f32[2,2,256]{2,1,0:T(2,128)}, u32[]{:S(2)}) copy-start(f32[2,2,256]{2,1,0:T(2,128)} %param.19) | copy-start | bytes 12292
  7.2 22.1 %copy-start.6 = (s32[2,256]{1,0:T(2,128)S(1)}, s32[2,256]{1,0:T(2,128)}, u32[]{:S(2)}) copy-start(s32[2,256]{1,0:T(2,128)} %param.25) | copy-start | bytes 6148
  7.2 22.2 %copy-start.8 = (f32[2,2]{1,0:T(2,128)S(1)}, f32[2,2]{1,0:T(2,128)}, u32[]{:S(2)}) copy-start(f32[2,2]{1,0:T(2,128)} %param.18) | copy-start | bytes 52
  7.2 22.2 %copy-start.9 = (s32[2]{0:T(128)S(1)}, s32[2]{0:T(128)}, u32[]{:S(2)}) copy-start(s32[2]{0:T(128)} %param.20) | copy-start | bytes 28
  7.2 22.2 %copy-start.11 = (s32[2]{0:T(128)S(1)}, s32[2]{0:T(128)}, u32[]{:S(2)}) copy-start(s32[2]{0:T(128)} %param.21) | copy-start | bytes 28
  7.2 22.2 %copy-start.10 = (s32[2]{0:T(128)S(1)}, s32[2]{0:T(128)}, u32[]{:S(2)}) copy-start(s32[2]{0:T(128)} %param.22) | copy-start | bytes 28
  7.2 332.2 %all-reduce.4.cloned.1.call-start = ((), (), s32[]{:S(2)}) async-start(), calls=%async_computation | async-start | bytes 524288 | tf_op jit(solution)/shard_map/psum | solution.py:109
  9.5 61.9 %collective-permute-start = (f32[2,2,4,64,128]{4,3,2,1,0:T(8,128)}, f32[2,2,4,64,128]{4,3,2,1,0:T(8,128)S(1)}, u32[]{:S(2)}, u32[]{:S(2)}) collective-permute-start(f32[2,2,4,64,128]{4,3,2,1,0:T(8,128)} %get-tuple-element.20), channel_id=1, source_target_pairs={{16,0},{32,16},{48,32},{64,48},{80,64},{96,80},{112,96},{128,112},... | collective-permute-start | bytes 1572872 | tf_op jit(solution)/shard_map/ppermute | solution.py:20
  27.4 59.5 %collective-permute-start.1 = (f32[2,2,4,64,128]{4,3,2,1,0:T(8,128)}, f32[2,2,4,64,128]{4,3,2,1,0:T(8,128)S(1)}, u32[]{:S(2)}, u32[]{:S(2)}) collective-permute-start(f32[2,2,4,64,128]{4,3,2,1,0:T(8,128)} %get-tuple-element.21), channel_id=1, source_target_pairs={{0,16},{16,32},{32,48},{48,64},{64,80},{80,96},{96,112},{112,128},... | collective-permute-start | bytes 1572872 | tf_op jit(solution)/shard_map/ppermute | solution.py:17
  30.7 24.9 %copy-start.12 = (s32[2]{0:T(128)S(1)}, s32[2]{0:T(128)}, u32[]{:S(2)}) copy-start(s32[2]{0:T(128)} %param.24) | copy-start | bytes 28
  30.8 25.0 %copy-start = (f32[2,8,64,128]{3,2,1,0:T(8,128)S(1)}, f32[2,8,64,128]{3,2,1,0:T(8,128)}, u32[]{:S(2)}) copy-start(f32[2,8,64,128]{3,2,1,0:T(8,128)} %param.14) | copy-start | bytes 1572868
  30.8 25.0 %copy-start.1 = (f32[2,8,64,128]{3,2,1,0:T(8,128)S(1)}, f32[2,8,64,128]{3,2,1,0:T(8,128)}, u32[]{:S(2)}) copy-start(f32[2,8,64,128]{3,2,1,0:T(8,128)} %param.16) | copy-start | bytes 1572868
  55.6 0.7 copy-start.13
  87.2 2.5 copy-start.2
  87.2 2.5 copy-start.4
  87.2 2.5 copy-start.5
  91.3 39.1 %collective-permute-start.2 = (f32[2,2,4,64,128]{4,3,2,1,0:T(8,128)}, f32[2,2,4,64,128]{4,3,2,1,0:T(8,128)}, u32[]{:S(2)}, u32[]{:S(2)}) collective-permute-start(f32[2,2,4,64,128]{4,3,2,1,0:T(8,128)} %get-tuple-element.16), channel_id=1, source_target_pairs={{16,0},{32,16},{48,32},{64,48},{80,64},{96,80},{112,96},{128,112},... | collective-permute-start | bytes 1572872 | tf_op jit(solution)/shard_map/ppermute | solution.py:20
  93.2 53.0 %collective-permute-start.3 = (f32[2,2,4,64,128]{4,3,2,1,0:T(8,128)}, f32[2,2,4,64,128]{4,3,2,1,0:T(8,128)}, u32[]{:S(2)}, u32[]{:S(2)}) collective-permute-start(f32[2,2,4,64,128]{4,3,2,1,0:T(8,128)} %get-tuple-element.17), channel_id=1, source_target_pairs={{0,16},{16,32},{32,48},{48,64},{64,80},{80,96},{96,112},{112,128},... | collective-permute-start | bytes 1572872 | tf_op jit(solution)/shard_map/ppermute | solution.py:17
  147.9 2.5 copy-start.3
Sparse Core Ops, SparseCore 0:
  152.9 186.5 all-reduce.3
where the time goes:
time: 349 us; the launch traced here: 348 us
  waiting for transfers between devices  241 us (69%)
  other arithmetic  64.6 us (19%)
  starting transfers between devices  25 us (7%)
  between operations  14.5 us (4%)
    psum x1, waiting for transfers between devices, per_device(): image = lax.psum(local_sum, 'shots')  187 us
    scatter-add x4, other arithmetic, inject(): jnp.zeros((count, length * plane), jnp.float32).at[rows, flat].add(amounts)  50.9 us
    ppermute x2, waiting for transfers between devices, extended(): lax.ppermute(lax.slice_in_dim(block, block.shape[dim] - width, None, axis...  31.2 us
    ppermute x2, waiting for transfers between devices, extended(): lax.ppermute(lax.slice_in_dim(block, 0, width, axis=dim), axis, backward)  23 us
    ppermute x2, starting transfers between devices, extended(): lax.ppermute(lax.slice_in_dim(block, 0, width, axis=dim), axis, backward)  19.7 us
  transfers between devices with their start and end apart: 5, of which 5 were waited for; matrix products, arithmetic and copies ran while one was open for 15% of the time, Pallas kernels for 0%

commit v1 on v0

--- a/solution.py
+++ b/solution.py
@@ -56,18 +56,49 @@
     return (inside_y & inside_x).astype(jnp.float32)
 
 
-def inject(cells, values, begin, length, rows_y, cols_x):
+def point_field(depth_local, row, col, values, length, rows_y, cols_x):
+    grid_z = jnp.arange(length, dtype=jnp.int32)[None, :, None, None]
+    grid_y = jnp.arange(rows_y, dtype=jnp.int32)[None, None, :, None]
+    grid_x = jnp.arange(cols_x, dtype=jnp.int32)[None, None, None, :]
+    hit = (
+        (grid_z == depth_local[:, None, None, None])
+        & (grid_y == row[:, None, None, None])
+        & (grid_x == col[:, None, None, None])
+    )
+    return jnp.where(hit, values[:, None, None, None], 0.0)
+
+
+def receiver_field(cells, traces, begin, length, rows_y, cols_x):
     plane = rows_y * cols_x
     depth = cells // plane
     rest = cells - depth * plane
+    row = rest // cols_x
+    col = rest - row * cols_x
     local = depth - begin
-    valid = (local >= 0) & (local < length)
-    flat = jnp.where(valid, local * plane + rest, 0)
-    amounts = jnp.where(valid, values, jnp.zeros_like(values))
-    count = cells.shape[0]
-    rows = jnp.broadcast_to(jnp.arange(count, dtype=jnp.int32)[:, None], flat.shape)
-    field = jnp.zeros((count, length * plane), jnp.float32).at[rows, flat].add(amounts)
-    return field.reshape(count, length, rows_y, cols_x)
+    slab_rows = jnp.arange(length * rows_y, dtype=jnp.int32)
+    key = local * rows_y + row
+    left = jnp.where(slab_rows[None, :, None] == key[:, None, :], traces[:, None, :], 0.0)
+    right = (col[:, :, None] == jnp.arange(cols_x, dtype=jnp.int32)[None, None, :]).astype(
+        jnp.float32
+    )
+    field = jnp.einsum(
+        "szr,srx->szx",
+        left,
+        right,
+        precision=lax.Precision.HIGHEST,
+        preferred_element_type=jnp.float32,
+    )
+    return field.reshape(cells.shape[0], length, rows_y, cols_x)
+
+
+def butterfly_sum(value, axis):
+    count = lax.axis_size(axis)
+    stride = 1
+    while stride < count:
+        pairs = [(i, i ^ stride) for i in range(count)]
+        value = value + lax.ppermute(value, axis, pairs)
+        stride *= 2
+    return value
 
 
 def per_device(
@@ -88,16 +119,16 @@
     shot_count, depth, rows_y, cols_x = src_cur.shape
     start = lax.axis_index("slab") * depth
     mask = band_mask(source_y, source_x, half_y, half_x, rows_y, cols_x)[:, None]
-    scells = (source_depth * rows_y * cols_x + source_y * cols_x + source_x)[:, None]
     terms = []
     up, u, vp, v = (src_prev, src_cur, rcv_prev, rcv_cur)
     for step in range(STEPS):
         stacked = jnp.stack([u, v])
         padded = extended(stacked, (("slab", 2),), 4)
         lap = laplace(padded)
-        sdelta = inject(scells, wavelet[step][:, None], start, depth, rows_y, cols_x)
-        rdelta = inject(receiver_cell, residual_traces[step], start, depth, rows_y, cols_x)
-        sdelta, rdelta = (sdelta, rdelta)
+        sdelta = point_field(
+            source_depth - start, source_y, source_x, wavelet[step], depth, rows_y, cols_x
+        )
+        rdelta = receiver_field(receiver_cell, residual_traces[step], start, depth, rows_y, cols_x)
         unew = mask * (2.0 * u - up + velocity * lap[0] + sdelta)
         vnew = mask * (2.0 * v - vp + velocity * lap[1] + rdelta)
         terms.append(jnp.sum((unew - 2.0 * u + up) * vnew, axis=0))
@@ -106,7 +137,7 @@
     local_sum = terms[0]
     for extra in terms[1:]:
         local_sum = local_sum + extra
-    image = lax.psum(local_sum, "shots")
+    image = butterfly_sum(local_sum, "shots")
     return (src_last, rcv_last, image)
 
 

time: 349 us -> 201 us (0.58)
  waiting for transfers between devices: 241 us -> 150 us
  other arithmetic: 64.6 us -> 10.8 us
  between operations: 14.5 us -> 1.01 us
  starting transfers between devices: 25 us -> 37.6 us
    psum x1 -> x0, waiting for transfers between devices: 187 us -> none  [per_device(): image = lax.psum(local_sum, 'shots')]
    scatter-add x4 -> x0, other arithmetic: 50.9 us -> none  [inject(): jnp.zeros((count, length * plane), jnp.float32).at[rows, flat].add(amounts)]
    ppermute x0 -> x4, waiting for transfers between devices: none -> 46.3 us  [butterfly_sum(): value = value + lax.ppermute(value, axis, pairs)]
    ppermute x2, waiting for transfers between devices: 23 us -> 61.2 us  [extended(): lax.ppermute(lax.slice_in_dim(block, 0, width, axis=dim), axis, backward)]
    ppermute x0 -> x4, starting transfers between devices: none -> 12.6 us  [butterfly_sum(): value = value + lax.ppermute(value, axis, pairs)]
    ppermute x2, waiting for transfers between devices: 31.2 us -> 42.5 us  [extended(): lax.ppermute(lax.slice_in_dim(block, block.shape[dim] - width, None, axis...]
  transfers between devices with their start and end apart: 5 -> 8, of which waited for: 5 -> 8; matrix products, arithmetic and copies ran while one was open for 15% -> 1% of each run, Pallas kernels for 0% -> 0%
where the time goes in v1:
time: 201 us
  waiting for transfers between devices  150 us (75%)
  starting transfers between devices  37.6 us (19%)
  other arithmetic  10.8 us (5%)
    ppermute x2, waiting for transfers between devices, extended(): lax.ppermute(lax.slice_in_dim(block, 0, width, axis=dim), axis, backward)  61.2 us
    ppermute x4, waiting for transfers between devices, butterfly_sum(): value = value + lax.ppermute(value, axis, pairs)  46.3 us
    ppermute x2, waiting for transfers between devices, extended(): lax.ppermute(lax.slice_in_dim(block, block.shape[dim] - width, None, axis...  42.5 us
    ppermute x2, starting transfers between devices, extended(): lax.ppermute(lax.slice_in_dim(block, 0, width, axis=dim), axis, backward)  19.7 us
    ppermute x4, starting transfers between devices, butterfly_sum(): value = value + lax.ppermute(value, axis, pairs)  12.6 us
    ppermute x2, starting transfers between devices, extended(): lax.ppermute(lax.slice_in_dim(block, block.shape[dim] - width, None, axis...  5.28 us
    add x2, other arithmetic, laplace(): total = total + COEF[shift_k] * (side_y + side_x)  4.91 us
  transfers between devices with their start and end apart: 8, of which 8 were waited for; matrix products, arithmetic and copies ran while one was open for 1% of the time, Pallas kernels for 0%

profile of v1, /device:TPU:25, one launch (start us, length us, event | category | flops | bytes accessed | tf_op | source)
XLA Modules:
  0.0 201.1 jit_solution(9378719920602305006)
XLA Ops:
  0.7 1.4 fusion.66
  2.2 17.8 %collective-permute-start = (f32[2,2,4,64,128]{4,3,2,1,0:T(8,128)S(1)}, f32[2,2,4,64,128]{4,3,2,1,0:T(8,128)S(1)}, u32[]{:S(2)}, u32[]{:S(2)}) collective-permute-start(f32[2,2,4,64,128]{4,3,2,1,0:T(8,128)S(1)} %get-tuple-element.18), channel_id=1, source_target_pairs={{16,0},{32,16},{48,32},{64,48},{80,64},{96,80},{112,96},{128,112},... | collective-permute-start | bytes 1572872 | tf_op jit(solution)/shard_map/ppermute | solution.py:20
  20.0 1.9 collective-permute-start.1
  22.1 0.1 iota_compare_fusion.7
  22.2 0.1 iota_compare_fusion.6
  22.3 0.1 broadcast_and_fusion
  22.4 0.1 and_convert_fusion
  22.5 0.8 fusion.58
  23.3 40.5 %collective-permute-done = f32[2,2,4,64,128]{4,3,2,1,0:T(8,128)S(1)} collective-permute-done((f32[2,2,4,64,128]{4,3,2,1,0:T(8,128)S(1)}, f32[2,2,4,64,128]{4,3,2,1,0:T(8,128)S(1)}, u32[]{:S(2)}, u32[]{:S(2)}) %collective-permute-start) | collective-permute-done | bytes 524320 | tf_op jit(solution)/shard_map/ppermute | solution.py:20
  63.8 15.5 %collective-permute-done.1 = f32[2,2,4,64,128]{4,3,2,1,0:T(8,128)S(1)} collective-permute-done((f32[2,2,4,64,128]{4,3,2,1,0:T(8,128)S(1)}, f32[2,2,4,64,128]{4,3,2,1,0:T(8,128)S(1)}, u32[]{:S(2)}, u32[]{:S(2)}) %collective-permute-start.1) | collective-permute-done | bytes 524320 | tf_op jit(solution)/shard_map/ppermute | solution.py:17
  79.2 0.4 pad_maximum_fusion
  79.7 2.5 %fusion.6 = f32[2,2,8,64,128]{4,3,2,1,0:T(8,128)S(1)} fusion(f32[2,2,8,64,128]{4,3,2,1,0:T(8,128)S(1)} %pad_maximum_fusion.2, f32[2,2,12,64,128]{4,3,2,1,0:T(8,128)S(1)} %get-tuple-element.17, f32[2,2,12,64,128]{4,3,2,1,0:T(8,128)S(1)} %get-tuple-element.16), kind=kLoop, calls=%fused_computation.52 | loop fusion | flops 8650752 | bytes 10485760 | tf_op jit(solution)/shard_map/add | solution.py:47
  82.1 0.5 fusion.77
  82.6 0.1 fusion.64
  82.7 1.9 collective-permute-start.2
  84.7 3.4 %collective-permute-start.3 = (f32[2,2,4,64,128]{4,3,2,1,0:T(8,128)S(1)}, f32[2,2,4,64,128]{4,3,2,1,0:T(8,128)S(1)}, u32[]{:S(2)}, u32[]{:S(2)}) collective-permute-start(f32[2,2,4,64,128]{4,3,2,1,0:T(8,128)S(1)} %get-tuple-element.15), channel_id=1, source_target_pairs={{0,16},{16,32},{32,48},{48,64},{64,80},{80,96},{96,112},{112,128},... | collective-permute-start | bytes 1572872 | tf_op jit(solution)/shard_map/ppermute | solution.py:17
  88.0 0.8 fusion.56
  88.8 0.1 pad_maximum_fusion.3
  88.9 20.7 %collective-permute-done.2 = f32[2,2,4,64,128]{4,3,2,1,0:T(8,128)S(1)} collective-permute-done((f32[2,2,4,64,128]{4,3,2,1,0:T(8,128)S(1)}, f32[2,2,4,64,128]{4,3,2,1,0:T(8,128)S(1)}, u32[]{:S(2)}, u32[]{:S(2)}) %collective-permute-start.2) | collective-permute-done | bytes 524320 | tf_op jit(solution)/shard_map/ppermute | solution.py:20
  109.6 27.1 %collective-permute-done.3 = f32[2,2,4,64,128]{4,3,2,1,0:T(8,128)S(1)} collective-permute-done((f32[2,2,4,64,128]{4,3,2,1,0:T(8,128)S(1)}, f32[2,2,4,64,128]{4,3,2,1,0:T(8,128)S(1)}, u32[]{:S(2)}, u32[]{:S(2)}) %collective-permute-start.3) | collective-permute-done | bytes 524320 | tf_op jit(solution)/shard_map/ppermute | solution.py:17
  136.7 0.4 pad_maximum_fusion.1
  137.2 2.5 %fusion.26 = f32[2,2,8,64,128]{4,3,2,1,0:T(8,128)S(1)} fusion(f32[2,2,8,64,128]{4,3,2,1,0:T(8,128)S(1)} %pad_maximum_fusion.3, f32[2,2,12,64,128]{4,3,2,1,0:T(8,128)S(1)} %get-tuple-element.13, f32[2,2,12,64,128]{4,3,2,1,0:T(8,128)S(1)} %get-tuple-element.12), kind=kLoop, calls=%fused_computation.72 | loop fusion | flops 8650752 | bytes 10485760 | tf_op jit(solution)/shard_map/add | solution.py:47
  139.6 1.7 multiply_reduce_fusion
  141.3 2.4 %collective-permute-start.4 = (f32[8,64,128]{2,1,0:T(8,128)S(1)}, f32[8,64,128]{2,1,0:T(8,128)S(1)}, u32[]{:S(2)}, u32[]{:S(2)}) collective-permute-start(f32[8,64,128]{2,1,0:T(8,128)S(1)} %add.258), channel_id=1, source_target_pairs={{0,1},{1,0},{2,3},{3,2},{4,5},{5,4},{6,7},{7,6},{8,9},{9,8},{10,11... | collective-permute-start | bytes 786440 | tf_op jit(solution)/shard_map/ppermute | solution.py:99
  143.7 1.1 collective-permute-done.4
  144.9 2.4 %collective-permute-start.5 = (f32[8,64,128]{2,1,0:T(8,128)S(1)}, f32[8,64,128]{2,1,0:T(8,128)S(1)}, u32[]{:S(2)}, u32[]{:S(2)}) collective-permute-start(f32[8,64,128]{2,1,0:T(8,128)S(1)} %add.259), channel_id=1, source_target_pairs={{0,2},{1,3},{2,0},{3,1},{4,6},{5,7},{6,4},{7,5},{8,10},{9,11},{10,... | collective-permute-start | bytes 786440 | tf_op jit(solution)/shard_map/ppermute | solution.py:99
  147.3 7.0 %collective-permute-done.5 = f32[8,64,128]{2,1,0:T(8,128)S(1)} collective-permute-done((f32[8,64,128]{2,1,0:T(8,128)S(1)}, f32[8,64,128]{2,1,0:T(8,128)S(1)}, u32[]{:S(2)}, u32[]{:S(2)}) %collective-permute-start.5) | collective-permute-done | bytes 262176 | tf_op jit(solution)/shard_map/ppermute | solution.py:99
  154.4 4.6 %collective-permute-start.6 = (f32[8,64,128]{2,1,0:T(8,128)S(1)}, f32[8,64,128]{2,1,0:T(8,128)S(1)}, u32[]{:S(2)}, u32[]{:S(2)}) collective-permute-start(f32[8,64,128]{2,1,0:T(8,128)S(1)} %add.260), channel_id=1, source_target_pairs={{0,4},{1,5},{2,6},{3,7},{4,0},{5,1},{6,2},{7,3},{8,12},{9,13},{10,... | collective-permute-start | bytes 786440 | tf_op jit(solution)/shard_map/ppermute | solution.py:99
  159.0 11.5 %collective-permute-done.6 = f32[8,64,128]{2,1,0:T(8,128)S(1)} collective-permute-done((f32[8,64,128]{2,1,0:T(8,128)S(1)}, f32[8,64,128]{2,1,0:T(8,128)S(1)}, u32[]{:S(2)}, u32[]{:S(2)}) %collective-permute-start.6) | collective-permute-done | bytes 262176 | tf_op jit(solution)/shard_map/ppermute | solution.py:99
  170.5 3.2 %collective-permute-start.7 = (f32[8,64,128]{2,1,0:T(8,128)S(1)}, f32[8,64,128]{2,1,0:T(8,128)S(1)}, u32[]{:S(2)}, u32[]{:S(2)}) collective-permute-start(f32[8,64,128]{2,1,0:T(8,128)S(1)} %add.261), channel_id=1, source_target_pairs={{0,8},{1,9},{2,10},{3,11},{4,12},{5,13},{6,14},{7,15},{8,0},{9,1},... | collective-permute-start | bytes 786440 | tf_op jit(solution)/shard_map/ppermute | solution.py:99
  173.7 26.7 %collective-permute-done.7 = f32[8,64,128]{2,1,0:T(8,128)S(1)} collective-permute-done((f32[8,64,128]{2,1,0:T(8,128)S(1)}, f32[8,64,128]{2,1,0:T(8,128)S(1)}, u32[]{:S(2)}, u32[]{:S(2)}) %collective-permute-start.7) | collective-permute-done | bytes 262176 | tf_op jit(solution)/shard_map/ppermute | solution.py:99
  200.4 0.7 add.262
  (37 shorter events, 0.4 us)
Async XLA Ops:
  0.6 21.7 %copy-start = (f32[2,8,64,128]{3,2,1,0:T(8,128)S(1)}, f32[2,8,64,128]{3,2,1,0:T(8,128)}, u32[]{:S(2)}) copy-start(f32[2,8,64,128]{3,2,1,0:T(8,128)} %param.14) | copy-start | bytes 1572868
  0.6 21.7 %copy-start.1 = (f32[2,8,64,128]{3,2,1,0:T(8,128)S(1)}, f32[2,8,64,128]{3,2,1,0:T(8,128)}, u32[]{:S(2)}) copy-start(f32[2,8,64,128]{3,2,1,0:T(8,128)} %param.16) | copy-start | bytes 1572868
  0.7 21.3 %copy-start.6 = (s32[2,256]{1,0:T(2,128)S(1)}, s32[2,256]{1,0:T(2,128)}, u32[]{:S(2)}) copy-start(s32[2,256]{1,0:T(2,128)} %param.25) | copy-start | bytes 6148
  0.7 21.3 %copy-start.5 = (f32[2,2,256]{2,1,0:T(2,128)S(1)}, f32[2,2,256]{2,1,0:T(2,128)}, u32[]{:S(2)}) copy-start(f32[2,2,256]{2,1,0:T(2,128)} %param.19) | copy-start | bytes 12292
  0.7 21.3 %copy-start.12 = (s32[2]{0:T(128)S(1)}, s32[2]{0:T(128)}, u32[]{:S(2)}) copy-start(s32[2]{0:T(128)} %param.20) | copy-start | bytes 28
  0.7 21.4 %copy-start.7 = (f32[2,2]{1,0:T(2,128)S(1)}, f32[2,2]{1,0:T(2,128)}, u32[]{:S(2)}) copy-start(f32[2,2]{1,0:T(2,128)} %param.18) | copy-start | bytes 52
  0.7 21.4 %copy-start.8 = (s32[2]{0:T(128)S(1)}, s32[2]{0:T(128)}, u32[]{:S(2)}) copy-start(s32[2]{0:T(128)} %param.21) | copy-start | bytes 28
  0.7 21.4 %copy-start.9 = (s32[2]{0:T(128)S(1)}, s32[2]{0:T(128)}, u32[]{:S(2)}) copy-start(s32[2]{0:T(128)} %param.23) | copy-start | bytes 28
  0.7 21.5 %copy-start.10 = (s32[2]{0:T(128)S(1)}, s32[2]{0:T(128)}, u32[]{:S(2)}) copy-start(s32[2]{0:T(128)} %param.22) | copy-start | bytes 28
  0.7 21.5 %copy-start.11 = (s32[2]{0:T(128)S(1)}, s32[2]{0:T(128)}, u32[]{:S(2)}) copy-start(s32[2]{0:T(128)} %param.24) | copy-start | bytes 28
  2.2 61.6 %collective-permute-start = (f32[2,2,4,64,128]{4,3,2,1,0:T(8,128)S(1)}, f32[2,2,4,64,128]{4,3,2,1,0:T(8,128)S(1)}, u32[]{:S(2)}, u32[]{:S(2)}) collective-permute-start(f32[2,2,4,64,128]{4,3,2,1,0:T(8,128)S(1)} %get-tuple-element.18), channel_id=1, source_target_pairs={{16,0},{32,16},{48,32},{64,48},{80,64},{96,80},{112,96},{128,112},... | collective-permute-start | bytes 1572872 | tf_op jit(solution)/shard_map/ppermute | solution.py:20
  20.0 59.3 %collective-permute-start.1 = (f32[2,2,4,64,128]{4,3,2,1,0:T(8,128)S(1)}, f32[2,2,4,64,128]{4,3,2,1,0:T(8,128)S(1)}, u32[]{:S(2)}, u32[]{:S(2)}) collective-permute-start(f32[2,2,4,64,128]{4,3,2,1,0:T(8,128)S(1)} %get-tuple-element.19), channel_id=1, source_target_pairs={{0,16},{16,32},{32,48},{48,64},{64,80},{80,96},{96,112},{112,128},... | collective-permute-start | bytes 1572872 | tf_op jit(solution)/shard_map/ppermute | solution.py:17
  79.6 2.5 %copy-start.2 = (f32[2,8,64,128]{3,2,1,0:T(8,128)S(1)}, f32[2,8,64,128]{3,2,1,0:T(8,128)}, u32[]{:S(2)}) copy-start(f32[2,8,64,128]{3,2,1,0:T(8,128)} %param.13) | copy-start | bytes 1572868
  79.6 2.5 %copy-start.3 = (f32[8,64,128]{2,1,0:T(8,128)S(1)}, f32[8,64,128]{2,1,0:T(8,128)}, u32[]{:S(2)}) copy-start(f32[8,64,128]{2,1,0:T(8,128)} %param.17) | copy-start | bytes 786436
  79.6 2.5 %copy-start.4 = (f32[2,8,64,128]{3,2,1,0:T(8,128)S(1)}, f32[2,8,64,128]{3,2,1,0:T(8,128)}, u32[]{:S(2)}) copy-start(f32[2,8,64,128]{3,2,1,0:T(8,128)} %param.15) | copy-start | bytes 1572868
  82.7 26.9 %collective-permute-start.2 = (f32[2,2,4,64,128]{4,3,2,1,0:T(8,128)S(1)}, f32[2,2,4,64,128]{4,3,2,1,0:T(8,128)S(1)}, u32[]{:S(2)}, u32[]{:S(2)}) collective-permute-start(f32[2,2,4,64,128]{4,3,2,1,0:T(8,128)S(1)} %get-tuple-element.14), channel_id=1, source_target_pairs={{16,0},{32,16},{48,32},{64,48},{80,64},{96,80},{112,96},{128,112},... | collective-permute-start | bytes 1572872 | tf_op jit(solution)/shard_map/ppermute | solution.py:20
  84.7 52.0 %collective-permute-start.3 = (f32[2,2,4,64,128]{4,3,2,1,0:T(8,128)S(1)}, f32[2,2,4,64,128]{4,3,2,1,0:T(8,128)S(1)}, u32[]{:S(2)}, u32[]{:S(2)}) collective-permute-start(f32[2,2,4,64,128]{4,3,2,1,0:T(8,128)S(1)} %get-tuple-element.15), channel_id=1, source_target_pairs={{0,16},{16,32},{32,48},{48,64},{64,80},{80,96},{96,112},{112,128},... | collective-permute-start | bytes 1572872 | tf_op jit(solution)/shard_map/ppermute | solution.py:17
  141.3 3.5 %collective-permute-start.4 = (f32[8,64,128]{2,1,0:T(8,128)S(1)}, f32[8,64,128]{2,1,0:T(8,128)S(1)}, u32[]{:S(2)}, u32[]{:S(2)}) collective-permute-start(f32[8,64,128]{2,1,0:T(8,128)S(1)} %add.258), channel_id=1, source_target_pairs={{0,1},{1,0},{2,3},{3,2},{4,5},{5,4},{6,7},{7,6},{8,9},{9,8},{10,11... | collective-permute-start | bytes 786440 | tf_op jit(solution)/shard_map/ppermute | solution.py:99
  144.9 9.4 %collective-permute-start.5 = (f32[8,64,128]{2,1,0:T(8,128)S(1)}, f32[8,64,128]{2,1,0:T(8,128)S(1)}, u32[]{:S(2)}, u32[]{:S(2)}) collective-permute-start(f32[8,64,128]{2,1,0:T(8,128)S(1)} %add.259), channel_id=1, source_target_pairs={{0,2},{1,3},{2,0},{3,1},{4,6},{5,7},{6,4},{7,5},{8,10},{9,11},{10,... | collective-permute-start | bytes 786440 | tf_op jit(solution)/shard_map/ppermute | solution.py:99
  154.4 16.1 %collective-permute-start.6 = (f32[8,64,128]{2,1,0:T(8,128)S(1)}, f32[8,64,128]{2,1,0:T(8,128)S(1)}, u32[]{:S(2)}, u32[]{:S(2)}) collective-permute-start(f32[8,64,128]{2,1,0:T(8,128)S(1)} %add.260), channel_id=1, source_target_pairs={{0,4},{1,5},{2,6},{3,7},{4,0},{5,1},{6,2},{7,3},{8,12},{9,13},{10,... | collective-permute-start | bytes 786440 | tf_op jit(solution)/shard_map/ppermute | solution.py:99
  170.5 29.9 %collective-permute-start.7 = (f32[8,64,128]{2,1,0:T(8,128)S(1)}, f32[8,64,128]{2,1,0:T(8,128)S(1)}, u32[]{:S(2)}, u32[]{:S(2)}) collective-permute-start(f32[8,64,128]{2,1,0:T(8,128)S(1)} %add.261), channel_id=1, source_target_pairs={{0,8},{1,9},{2,10},{3,11},{4,12},{5,13},{6,14},{7,15},{8,0},{9,1},... | collective-permute-start | bytes 786440 | tf_op jit(solution)/shard_map/ppermute | solution.py:99

commit v2 on v1

--- a/solution.py
+++ b/solution.py
@@ -9,17 +9,54 @@
 COEF = (-205.0 / 72.0, 8.0 / 5.0, -1.0 / 5.0, 8.0 / 315.0, -1.0 / 560.0)
 
 
-def extended(block, sides, width):
-    for axis, dim in sides:
-        count = lax.axis_size(axis)
-        forward = [(i, i + 1) for i in range(count - 1)]
-        backward = [(target, source) for source, target in forward]
-        low = lax.ppermute(
-            lax.slice_in_dim(block, block.shape[dim] - width, None, axis=dim), axis, forward
-        )
-        high = lax.ppermute(lax.slice_in_dim(block, 0, width, axis=dim), axis, backward)
-        block = jnp.concatenate([low, block, high], axis=dim)
-    return block
+WIN_Y = 44
+WIN_X = 88
+
+
+def band_corner(source_y, source_x, half_y, half_x, rows_y, cols_x):
+    row0 = jnp.clip(source_y - half_y, 0, rows_y - WIN_Y)
+    col0 = jnp.clip(source_x - half_x, 0, cols_x - WIN_X)
+    return row0, col0
+
+
+def cut_windows(layers, row0, col0):
+    fields, shots, width = layers.shape[:3]
+    pieces = []
+    for s in range(shots):
+        piece = lax.dynamic_slice(
+            layers[:, s], (0, 0, row0[s], col0[s]), (fields, width, WIN_Y, WIN_X)
+        )
+        pieces.append(piece.reshape(fields, -1, 128))
+    return jnp.stack(pieces, axis=1)
+
+
+def paste_windows(flat, row0, col0, width, rows_y, cols_x):
+    fields, shots = flat.shape[:2]
+    pieces = []
+    for s in range(shots):
+        piece = flat[:, s].reshape(fields, width, WIN_Y, WIN_X)
+        empty = jnp.zeros((fields, width, rows_y, cols_x), flat.dtype)
+        pieces.append(lax.dynamic_update_slice(empty, piece, (0, 0, row0[s], col0[s])))
+    return jnp.stack(pieces, axis=1)
+
+
+def extended(block, row0, col0, width):
+    count = lax.axis_size("slab")
+    forward = [(i, i + 1) for i in range(count - 1)]
+    backward = [(target, source) for source, target in forward]
+    dim = 2
+    rows_y, cols_x = block.shape[-2:]
+    low = lax.ppermute(
+        cut_windows(lax.slice_in_dim(block, block.shape[dim] - width, None, axis=dim), row0, col0),
+        "slab",
+        forward,
+    )
+    high = lax.ppermute(
+        cut_windows(lax.slice_in_dim(block, 0, width, axis=dim), row0, col0), "slab", backward
+    )
+    low = paste_windows(low, row0, col0, width, rows_y, cols_x)
+    high = paste_windows(high, row0, col0, width, rows_y, cols_x)
+    return jnp.concatenate([low, block, high], axis=dim)
 
 
 def laplace(padded):
@@ -91,14 +128,29 @@
     return field.reshape(cells.shape[0], length, rows_y, cols_x)
 
 
-def butterfly_sum(value, axis):
+def tree_sum(value, axis):
     count = lax.axis_size(axis)
+    me = lax.axis_index(axis)
+    shape = value.shape
+    piece = value.reshape(-1)
+    bits = []
     stride = 1
     while stride < count:
+        bits.append(stride)
+        stride *= 2
+    for stride in bits:
+        upper = (me // stride) % 2 == 1
+        halves = piece.reshape(2, -1)
+        send = jnp.where(upper, halves[0], halves[1])
+        keep = jnp.where(upper, halves[1], halves[0])
         pairs = [(i, i ^ stride) for i in range(count)]
-        value = value + lax.ppermute(value, axis, pairs)
-        stride *= 2
-    return value
+        piece = keep + lax.ppermute(send, axis, pairs)
+    for stride in reversed(bits):
+        upper = (me // stride) % 2 == 1
+        pairs = [(i, i ^ stride) for i in range(count)]
+        other = lax.ppermute(piece, axis, pairs)
+        piece = jnp.where(upper, jnp.concatenate([other, piece]), jnp.concatenate([piece, other]))
+    return piece.reshape(shape)
 
 
 def per_device(
@@ -119,11 +171,12 @@
     shot_count, depth, rows_y, cols_x = src_cur.shape
     start = lax.axis_index("slab") * depth
     mask = band_mask(source_y, source_x, half_y, half_x, rows_y, cols_x)[:, None]
+    row0, col0 = band_corner(source_y, source_x, half_y, half_x, rows_y, cols_x)
     terms = []
     up, u, vp, v = (src_prev, src_cur, rcv_prev, rcv_cur)
     for step in range(STEPS):
         stacked = jnp.stack([u, v])
-        padded = extended(stacked, (("slab", 2),), 4)
+        padded = extended(stacked, row0, col0, 4)
         lap = laplace(padded)
         sdelta = point_field(
             source_depth - start, source_y, source_x, wavelet[step], depth, rows_y, cols_x
@@ -137,7 +190,7 @@
     local_sum = terms[0]
     for extra in terms[1:]:
         local_sum = local_sum + extra
-    image = butterfly_sum(local_sum, "shots")
+    image = tree_sum(local_sum, "shots")
     return (src_last, rcv_last, image)
 
 

time: 201 us -> 213 us (1.060)
  the two profiles are of different devices: /device:TPU:25 before, /device:TPU:7 now
where the time goes in v2:
time: 213 us; the launch traced here: 211 us
  starting transfers between devices  78.1 us (37%)
  local copies, waits for them, and re-layouts  52.9 us (25%)
  waiting for transfers between devices  49.9 us (23%)
  other arithmetic  18.2 us (9%)
  between operations  9.03 us (4%)
  matrix products  3.11 us (1%)
    ppermute x4, starting transfers between devices, tree_sum(): piece = keep + lax.ppermute(send, axis, pairs)  40.2 us
    dynamic_update_slice x8, local copies, waits for them, and re-layouts, paste_windows(): lax.dynamic_update_slice(empty, piece, (0, 0, row0[s], col0[s]))  29.5 us
    ppermute x2, waiting for transfers between devices, extended(): lax.ppermute(cut_windows(lax.slice_in_dim(block, 0, width, axis=dim), row...  23.4 us
    ppermute x2, starting transfers between devices, extended(): lax.ppermute(cut_windows(lax.slice_in_dim(block, block.shape[dim] - width...  17.3 us
    ppermute x4, starting transfers between devices, tree_sum(): other = lax.ppermute(piece, axis, pairs)  15 us
    ppermute x4, waiting for transfers between devices, tree_sum(): other = lax.ppermute(piece, axis, pairs)  13.4 us
    ppermute x4, waiting for transfers between devices, tree_sum(): piece = keep + lax.ppermute(send, axis, pairs)  13.1 us
    another operation x16, local copies, waits for them, and re-layouts, paste_windows(): return jnp.stack(pieces, axis=1)  10.5 us
  transfers between devices with their start and end apart: 12, of which 10 were waited for; matrix products, arithmetic and copies ran while one was open for 6% of the time, Pallas kernels for 0%

profile of v2, /device:TPU:7, one launch (start us, length us, event | category | flops | bytes accessed | tf_op | source)
XLA Modules:
  0.0 211.2 jit_solution(12121517892576642330)
XLA Ops:
  12.3 15.4 %collective-permute-start.1 = (f32[2,2,121,128]{3,2,0,1:T(8,128)S(1)}, f32[2,2,121,128]{3,2,0,1:T(8,128)S(1)}, u32[]{:S(2)}, u32[]{:S(2)}) collective-permute-start(f32[2,2,121,128]{3,2,0,1:T(8,128)S(1)} %pad_maximum_fusion.3), channel_id=1, source_target_pairs={{0,16},{16,32},{32,48},{48,64},{64,80},{80,96},{96,112},{112,128},... | collective-permute-start | bytes 743432 | tf_op jit(solution)/shard_map/ppermute | solution.py:49
  28.4 2.1 collective-permute-start
  34.6 13.5 %collective-permute-done = f32[2,2,121,128]{3,2,0,1:T(8,128)S(1)} collective-permute-done((f32[2,2,121,128]{3,2,0,1:T(8,128)S(1)}, f32[2,2,121,128]{3,2,0,1:T(8,128)S(1)}, u32[]{:S(2)}, u32[]{:S(2)}) %collective-permute-start) | collective-permute-done | bytes 247840 | tf_op jit(solution)/shard_map/ppermute | solution.py:54
  48.5 3.3 %dynamic_update_slice.34 = f32[2,1,4,64,128]{4,3,2,1,0:T(8,128)S(1)} dynamic-update-slice(f32[2,1,4,64,128]{4,3,2,1,0:T(8,128)S(1)} %stack.71.clone.3, f32[2,1,4,44,88]{4,3,2,1,0:T(8,128)S(1)} %bitcast.101, s32[]{:T(128)} %constant.140.clone.1, s32[]{:T(128)} %constant.140.clone.1, s32[]{:T(128)} %constant.140.clone.1, s32[]{:T(128)S(6)} %select_n.201, s32[]{:T(128)S(6)} %select_n.202) | dynamic-update-slice | bytes 247812 | tf_op jit(solution)/shard_map/dynamic_update_slice | solution.py:39
  51.8 3.4 %dynamic_update_slice.35 = f32[2,1,4,64,128]{4,3,2,1,0:T(8,128)S(1)} dynamic-update-slice(f32[2,1,4,64,128]{4,3,2,1,0:T(8,128)S(1)} %stack.71.clone.2, f32[2,1,4,44,88]{4,3,2,1,0:T(8,128)S(1)} %bitcast.98, s32[]{:T(128)} %constant.140.clone.1, s32[]{:T(128)} %constant.140.clone.1, s32[]{:T(128)} %constant.140.clone.1, s32[]{:T(128)S(6)} %select_n.203, s32[]{:T(128)S(6)} %select_n.204) | dynamic-update-slice | bytes 247812 | tf_op jit(solution)/shard_map/dynamic_update_slice | solution.py:39
  55.2 3.3 %dynamic_update_slice.32 = f32[2,1,4,64,128]{4,3,2,1,0:T(8,128)S(1)} dynamic-update-slice(f32[2,1,4,64,128]{4,3,2,1,0:T(8,128)S(1)} %stack.71.clone.1, f32[2,1,4,44,88]{4,3,2,1,0:T(8,128)S(1)} %bitcast.105, s32[]{:T(128)} %constant.140.clone.1, s32[]{:T(128)} %constant.140.clone.1, s32[]{:T(128)} %constant.140.clone.1, s32[]{:T(128)S(6)} %select_n.201, s32[]{:T(128)S(6)} %select_n.202) | dynamic-update-slice | bytes 247812 | tf_op jit(solution)/shard_map/dynamic_update_slice | solution.py:39
  58.5 3.4 %dynamic_update_slice.33 = f32[2,1,4,64,128]{4,3,2,1,0:T(8,128)S(1)} dynamic-update-slice(f32[2,1,4,64,128]{4,3,2,1,0:T(8,128)S(1)} %stack.71.clone, f32[2,1,4,44,88]{4,3,2,1,0:T(8,128)S(1)} %bitcast.104, s32[]{:T(128)} %constant.140.clone.1, s32[]{:T(128)} %constant.140.clone.1, s32[]{:T(128)} %constant.140.clone.1, s32[]{:T(128)S(6)} %select_n.203, s32[]{:T(128)S(6)} %select_n.204) | dynamic-update-slice | bytes 247812 | tf_op jit(solution)/shard_map/dynamic_update_slice | solution.py:39
  62.3 2.5 %fusion.6 = f32[2,2,8,64,128]{4,3,2,1,0:T(8,128)S(1)} fusion(f32[2,2,8,64,128]{4,3,2,1,0:T(8,128)S(1)} %pad_maximum_fusion, f32[2,2,12,64,128]{4,3,2,1,0:T(8,128)S(1)} %get-tuple-element.15, f32[2,2,12,64,128]{4,3,2,1,0:T(8,128)S(1)} %get-tuple-element.14), kind=kLoop, calls=%fused_computation.60 | loop fusion | flops 8650752 | bytes 10485760 | tf_op jit(solution)/shard_map/add | solution.py:84
  69.5 1.9 dynamic-slice_maximum_fusion
  74.8 1.9 collective-permute-start.3
  79.6 3.5 %collective-permute-start.2 = (f32[2,2,121,128]{3,2,0,1:T(8,128)}, f32[2,2,121,128]{3,2,0,1:T(8,128)}, u32[]{:S(2)}, u32[]{:S(2)}) collective-permute-start(f32[2,2,121,128]{3,2,0,1:T(8,128)} %pad_maximum_fusion.4), channel_id=1, source_target_pairs={{16,0},{32,16},{48,32},{64,48},{80,64},{96,80},{112,96},{128,112},... | collective-permute-start | bytes 743432 | tf_op jit(solution)/shard_map/ppermute | solution.py:54
  88.4 9.9 %collective-permute-done.2 = f32[2,2,121,128]{3,2,0,1:T(8,128)} collective-permute-done((f32[2,2,121,128]{3,2,0,1:T(8,128)}, f32[2,2,121,128]{3,2,0,1:T(8,128)}, u32[]{:S(2)}, u32[]{:S(2)}) %collective-permute-start.2) | collective-permute-done | bytes 247840 | tf_op jit(solution)/shard_map/ppermute | solution.py:54
  101.7 1.7 stack.85
  104.2 4.0 %dynamic_update_slice.38 = f32[2,1,4,64,128]{4,3,2,1,0:T(8,128)} dynamic-update-slice(f32[2,1,4,64,128]{4,3,2,1,0:T(8,128)} %stack.71.clone.7, f32[2,1,4,44,88]{4,3,2,1,0:T(8,128)} %bitcast.102, s32[]{:T(128)} %constant.140.clone.1, s32[]{:T(128)} %constant.140.clone.1, s32[]{:T(128)} %constant.140.clone.1, s32[]{:T(128)S(6)} %select_n.201, s32[]{:T(128)S(6)} %select_n.202) | dynamic-update-slice | bytes 247812 | tf_op jit(solution)/shard_map/dynamic_update_slice | solution.py:39
  108.9 4.1 %dynamic_update_slice.39 = f32[2,1,4,64,128]{4,3,2,1,0:T(8,128)} dynamic-update-slice(f32[2,1,4,64,128]{4,3,2,1,0:T(8,128)} %stack.71.clone.6, f32[2,1,4,44,88]{4,3,2,1,0:T(8,128)} %bitcast.99, s32[]{:T(128)} %constant.140.clone.1, s32[]{:T(128)} %constant.140.clone.1, s32[]{:T(128)} %constant.140.clone.1, s32[]{:T(128)S(6)} %select_n.203, s32[]{:T(128)S(6)} %select_n.204) | dynamic-update-slice | bytes 247812 | tf_op jit(solution)/shard_map/dynamic_update_slice | solution.py:39
  113.7 4.0 %dynamic_update_slice.36 = f32[2,1,4,64,128]{4,3,2,1,0:T(8,128)} dynamic-update-slice(f32[2,1,4,64,128]{4,3,2,1,0:T(8,128)} %stack.71.clone.5, f32[2,1,4,44,88]{4,3,2,1,0:T(8,128)} %bitcast.103, s32[]{:T(128)} %constant.140.clone.1, s32[]{:T(128)} %constant.140.clone.1, s32[]{:T(128)} %constant.140.clone.1, s32[]{:T(128)S(6)} %select_n.201, s32[]{:T(128)S(6)} %select_n.202) | dynamic-update-slice | bytes 247812 | tf_op jit(solution)/shard_map/dynamic_update_slice | solution.py:39
  118.4 4.1 %dynamic_update_slice.37 = f32[2,1,4,64,128]{4,3,2,1,0:T(8,128)} dynamic-update-slice(f32[2,1,4,64,128]{4,3,2,1,0:T(8,128)} %stack.71.clone.4, f32[2,1,4,44,88]{4,3,2,1,0:T(8,128)} %bitcast.100, s32[]{:T(128)} %constant.140.clone.1, s32[]{:T(128)} %constant.140.clone.1, s32[]{:T(128)} %constant.140.clone.1, s32[]{:T(128)S(6)} %select_n.203, s32[]{:T(128)S(6)} %select_n.204) | dynamic-update-slice | bytes 247812 | tf_op jit(solution)/shard_map/dynamic_update_slice | solution.py:39
  124.2 2.5 %fusion.26 = f32[2,2,8,64,128]{4,3,2,1,0:T(8,128)S(1)} fusion(f32[2,2,8,64,128]{4,3,2,1,0:T(8,128)S(1)} %pad_maximum_fusion.1, f32[2,2,12,64,128]{4,3,2,1,0:T(8,128)S(1)} %get-tuple-element.13, f32[2,2,12,64,128]{4,3,2,1,0:T(8,128)S(1)} %get-tuple-element.12), kind=kLoop, calls=%fused_computation.80 | loop fusion | flops 8650752 | bytes 10485760 | tf_op jit(solution)/shard_map/add | solution.py:84
  128.4 4.8 %collective-permute-start.4 = (f32[32768]{0:T(1024)S(1)}, f32[32768]{0:T(1024)S(1)}, u32[]{:S(2)}, u32[]{:S(2)}) collective-permute-start(f32[32768]{0:T(1024)S(1)} %bitcast.111), channel_id=1, source_target_pairs={{0,1},{1,0},{2,3},{3,2},{4,5},{5,4},{6,7},{7,6},{8,9},{9,8},{10,11... | collective-permute-start | bytes 393224 | tf_op jit(solution)/shard_map/ppermute | solution.py:147
  134.2 31.5 %collective-permute-start.5 = (f32[16384]{0:T(1024)S(1)}, f32[16384]{0:T(1024)S(1)}, u32[]{:S(2)}, u32[]{:S(2)}) collective-permute-start(f32[16384]{0:T(1024)S(1)} %slice_select_fusion.2), channel_id=1, source_target_pairs={{0,2},{1,3},{2,0},{3,1},{4,6},{5,7},{6,4},{7,5},{8,10},{9,11},{10,... | collective-permute-start | bytes 196616 | tf_op jit(solution)/shard_map/ppermute | solution.py:147
  165.8 2.1 %collective-permute-done.5 = f32[16384]{0:T(1024)S(1)} collective-permute-done((f32[16384]{0:T(1024)S(1)}, f32[16384]{0:T(1024)S(1)}, u32[]{:S(2)}, u32[]{:S(2)}) %collective-permute-start.5) | collective-permute-done | bytes 65568 | tf_op jit(solution)/shard_map/ppermute | solution.py:147
  168.0 1.9 collective-permute-start.6
  169.9 3.6 %collective-permute-done.6 = f32[8192]{0:T(1024)S(1)} collective-permute-done((f32[8192]{0:T(1024)S(1)}, f32[8192]{0:T(1024)S(1)}, u32[]{:S(2)}, u32[]{:S(2)}) %collective-permute-start.6) | collective-permute-done | bytes 32800 | tf_op jit(solution)/shard_map/ppermute | solution.py:147
  173.5 1.9 collective-permute-start.7
  175.5 6.5 %collective-permute-done.7 = f32[4096]{0:T(1024)S(1)} collective-permute-done((f32[4096]{0:T(1024)S(1)}, f32[4096]{0:T(1024)S(1)}, u32[]{:S(2)}, u32[]{:S(2)}) %collective-permute-start.7) | collective-permute-done | bytes 16416 | tf_op jit(solution)/shard_map/ppermute | solution.py:147
  181.9 1.9 collective-permute-start.8
  183.9 6.4 %collective-permute-done.8 = f32[4096]{0:T(1024)S(1)} collective-permute-done((f32[4096]{0:T(1024)S(1)}, f32[4096]{0:T(1024)S(1)}, u32[]{:S(2)}, u32[]{:S(2)}) %collective-permute-start.8) | collective-permute-done | bytes 16416 | tf_op jit(solution)/shard_map/ppermute | solution.py:151
  190.3 2.0 collective-permute-start.9
  192.3 3.5 %collective-permute-done.9 = f32[8192]{0:T(1024)S(1)} collective-permute-done((f32[8192]{0:T(1024)S(1)}, f32[8192]{0:T(1024)S(1)}, u32[]{:S(2)}, u32[]{:S(2)}) %collective-permute-start.9) | collective-permute-done | bytes 32800 | tf_op jit(solution)/shard_map/ppermute | solution.py:151
  195.9 2.8 %collective-permute-start.10 = (f32[16384]{0:T(1024)S(1)}, f32[16384]{0:T(1024)S(1)}, u32[]{:S(2)}, u32[]{:S(2)}) collective-permute-start(f32[16384]{0:T(1024)S(1)} %maximum_select_fusion.3), channel_id=1, source_target_pairs={{0,2},{1,3},{2,0},{3,1},{4,6},{5,7},{6,4},{7,5},{8,10},{9,11},{10,... | collective-permute-start | bytes 196616 | tf_op jit(solution)/shard_map/ppermute | solution.py:151
  198.7 2.5 %collective-permute-done.10 = f32[16384]{0:T(1024)S(1)} collective-permute-done((f32[16384]{0:T(1024)S(1)}, f32[16384]{0:T(1024)S(1)}, u32[]{:S(2)}, u32[]{:S(2)}) %collective-permute-start.10) | collective-permute-done | bytes 65568 | tf_op jit(solution)/shard_map/ppermute | solution.py:151
  201.3 8.3 %collective-permute-start.11 = (f32[32768]{0:T(1024)S(1)}, f32[32768]{0:T(1024)S(1)}, u32[]{:S(2)}, u32[]{:S(2)}) collective-permute-start(f32[32768]{0:T(1024)S(1)} %maximum_select_fusion.1), channel_id=1, source_target_pairs={{0,1},{1,0},{2,3},{3,2},{4,5},{5,4},{6,7},{7,6},{8,9},{9,8},{10,11... | collective-permute-start | bytes 393224 | tf_op jit(solution)/shard_map/ppermute | solution.py:151
  (113 shorter events, 38.0 us)
Async XLA Ops:
  12.1 18.4 %copy-start.10 = (s32[2]{0:T(128)S(1)}, s32[2]{0:T(128)}, u32[]{:S(2)}) copy-start(s32[2]{0:T(128)} %param.21) | copy-start | bytes 28
  12.1 18.4 %copy-start.11 = (s32[2]{0:T(128)S(1)}, s32[2]{0:T(128)}, u32[]{:S(2)}) copy-start(s32[2]{0:T(128)} %param.23) | copy-start | bytes 28
  12.1 18.4 %copy-start.12 = (s32[2]{0:T(128)S(1)}, s32[2]{0:T(128)}, u32[]{:S(2)}) copy-start(s32[2]{0:T(128)} %param.22) | copy-start | bytes 28
  12.1 18.4 %copy-start.13 = (s32[2]{0:T(128)S(1)}, s32[2]{0:T(128)}, u32[]{:S(2)}) copy-start(s32[2]{0:T(128)} %param.24) | copy-start | bytes 28
  12.1 18.5 %copy-start.9 = (s32[2,256]{1,0:T(2,128)S(1)}, s32[2,256]{1,0:T(2,128)}, u32[]{:S(2)}) copy-start(s32[2,256]{1,0:T(2,128)} %param.25) | copy-start | bytes 6148
  12.2 18.5 %copy-start.8 = (f32[2,2,256]{2,1,0:T(2,128)S(1)}, f32[2,2,256]{2,1,0:T(2,128)}, u32[]{:S(2)}) copy-start(f32[2,2,256]{2,1,0:T(2,128)} %param.19) | copy-start | bytes 12292
  12.2 18.5 %copy-start.15 = (s32[2]{0:T(128)S(1)}, s32[2]{0:T(128)}, u32[]{:S(2)}) copy-start(s32[2]{0:T(128)} %param.20) | copy-start | bytes 28
  12.3 21.9 %collective-permute-start.1 = (f32[2,2,121,128]{3,2,0,1:T(8,128)S(1)}, f32[2,2,121,128]{3,2,0,1:T(8,128)S(1)}, u32[]{:S(2)}, u32[]{:S(2)}) collective-permute-start(f32[2,2,121,128]{3,2,0,1:T(8,128)S(1)} %pad_maximum_fusion.3), channel_id=1, source_target_pairs={{0,16},{16,32},{32,48},{48,64},{64,80},{80,96},{96,112},{112,128},... | collective-permute-start | bytes 743432 | tf_op jit(solution)/shard_map/ppermute | solution.py:49
  28.2 5.9 %copy-start.14 = (f32[2,2]{1,0:T(2,128)S(1)}, f32[2,2]{1,0:T(2,128)}, u32[]{:S(2)}) copy-start(f32[2,2]{1,0:T(2,128)} %param.18) | copy-start | bytes 52
  28.2 5.9 %copy-start = (f32[2,8,64,128]{3,2,1,0:T(8,128)S(1)}, f32[2,8,64,128]{3,2,1,0:T(8,128)}, u32[]{:S(2)}) copy-start(f32[2,8,64,128]{3,2,1,0:T(8,128)} %param.14) | copy-start | bytes 1572868
  28.2 5.9 %copy-start.1 = (f32[2,8,64,128]{3,2,1,0:T(8,128)S(1)}, f32[2,8,64,128]{3,2,1,0:T(8,128)}, u32[]{:S(2)}) copy-start(f32[2,8,64,128]{3,2,1,0:T(8,128)} %param.16) | copy-start | bytes 1572868
  28.4 19.7 %collective-permute-start = (f32[2,2,121,128]{3,2,0,1:T(8,128)S(1)}, f32[2,2,121,128]{3,2,0,1:T(8,128)S(1)}, u32[]{:S(2)}, u32[]{:S(2)}) collective-permute-start(f32[2,2,121,128]{3,2,0,1:T(8,128)S(1)} %pad_maximum_fusion.2), channel_id=1, source_target_pairs={{16,0},{32,16},{48,32},{64,48},{80,64},{96,80},{112,96},{128,112},... | collective-permute-start | bytes 743432 | tf_op jit(solution)/shard_map/ppermute | solution.py:54
  62.3 2.5 %copy-start.2 = (f32[2,8,64,128]{3,2,1,0:T(8,128)S(1)}, f32[2,8,64,128]{3,2,1,0:T(8,128)}, u32[]{:S(2)}) copy-start(f32[2,8,64,128]{3,2,1,0:T(8,128)} %param.13) | copy-start | bytes 1572868
  62.3 2.5 %copy-start.4 = (f32[8,64,128]{2,1,0:T(8,128)S(1)}, f32[8,64,128]{2,1,0:T(8,128)}, u32[]{:S(2)}) copy-start(f32[8,64,128]{2,1,0:T(8,128)} %param.17) | copy-start | bytes 786436
  62.3 2.5 %copy-start.5 = (f32[2,8,64,128]{3,2,1,0:T(8,128)S(1)}, f32[2,8,64,128]{3,2,1,0:T(8,128)}, u32[]{:S(2)}) copy-start(f32[2,8,64,128]{3,2,1,0:T(8,128)} %param.15) | copy-start | bytes 1572868
  62.3 2.5 %copy-start.7 = (f32[2,512,128]{2,1,0:T(8,128)S(1)}, f32[2,512,128]{2,1,0:T(8,128)}, u32[]{:S(2)}) copy-start(f32[2,512,128]{2,1,0:T(8,128)} %fusion.58) | copy-start | bytes 1572868
  74.8 8.5 %collective-permute-start.3 = (f32[2,2,121,128]{3,2,0,1:T(8,128)}, f32[2,2,121,128]{3,2,0,1:T(8,128)}, u32[]{:S(2)}, u32[]{:S(2)}) collective-permute-start(f32[2,2,121,128]{3,2,0,1:T(8,128)} %pad_maximum_fusion.5), channel_id=1, source_target_pairs={{0,16},{16,32},{32,48},{48,64},{64,80},{80,96},{96,112},{112,128},... | collective-permute-start | bytes 743432 | tf_op jit(solution)/shard_map/ppermute | solution.py:49
  79.6 18.7 %collective-permute-start.2 = (f32[2,2,121,128]{3,2,0,1:T(8,128)}, f32[2,2,121,128]{3,2,0,1:T(8,128)}, u32[]{:S(2)}, u32[]{:S(2)}) collective-permute-start(f32[2,2,121,128]{3,2,0,1:T(8,128)} %pad_maximum_fusion.4), channel_id=1, source_target_pairs={{16,0},{32,16},{48,32},{64,48},{80,64},{96,80},{112,96},{128,112},... | collective-permute-start | bytes 743432 | tf_op jit(solution)/shard_map/ppermute | solution.py:54
  124.2 2.5 %copy-start.3 = (f32[2,8,64,128]{3,2,1,0:T(8,128)S(1)}, f32[2,8,64,128]{3,2,1,0:T(8,128)}, u32[]{:S(2)}) copy-start(f32[2,8,64,128]{3,2,1,0:T(8,128)} %param.13) | copy-start | bytes 1572868
  124.2 2.5 %copy-start.6 = (f32[2,512,128]{2,1,0:T(8,128)S(1)}, f32[2,512,128]{2,1,0:T(8,128)}, u32[]{:S(2)}) copy-start(f32[2,512,128]{2,1,0:T(8,128)} %fusion.56) | copy-start | bytes 1572868
  128.4 5.8 %collective-permute-start.4 = (f32[32768]{0:T(1024)S(1)}, f32[32768]{0:T(1024)S(1)}, u32[]{:S(2)}, u32[]{:S(2)}) collective-permute-start(f32[32768]{0:T(1024)S(1)} %bitcast.111), channel_id=1, source_target_pairs={{0,1},{1,0},{2,3},{3,2},{4,5},{5,4},{6,7},{7,6},{8,9},{9,8},{10,11... | collective-permute-start | bytes 393224 | tf_op jit(solution)/shard_map/ppermute | solution.py:147
  134.2 33.7 %collective-permute-start.5 = (f32[16384]{0:T(1024)S(1)}, f32[16384]{0:T(1024)S(1)}, u32[]{:S(2)}, u32[]{:S(2)}) collective-permute-start(f32[16384]{0:T(1024)S(1)} %slice_select_fusion.2), channel_id=1, source_target_pairs={{0,2},{1,3},{2,0},{3,1},{4,6},{5,7},{6,4},{7,5},{8,10},{9,11},{10,... | collective-permute-start | bytes 196616 | tf_op jit(solution)/shard_map/ppermute | solution.py:147
  168.0 5.6 %collective-permute-start.6 = (f32[8192]{0:T(1024)S(1)}, f32[8192]{0:T(1024)S(1)}, u32[]{:S(2)}, u32[]{:S(2)}) collective-permute-start(f32[8192]{0:T(1024)S(1)} %slice_select_fusion.3), channel_id=1, source_target_pairs={{0,4},{1,5},{2,6},{3,7},{4,0},{5,1},{6,2},{7,3},{8,12},{9,13},{10,... | collective-permute-start | bytes 98312 | tf_op jit(solution)/shard_map/ppermute | solution.py:147
  173.5 8.4 %collective-permute-start.7 = (f32[4096]{0:T(1024)S(1)}, f32[4096]{0:T(1024)S(1)}, u32[]{:S(2)}, u32[]{:S(2)}) collective-permute-start(f32[4096]{0:T(1024)S(1)} %slice_select_fusion.4), channel_id=1, source_target_pairs={{0,8},{1,9},{2,10},{3,11},{4,12},{5,13},{6,14},{7,15},{8,0},{9,1},... | collective-permute-start | bytes 49160 | tf_op jit(solution)/shard_map/ppermute | solution.py:147
  181.9 8.4 %collective-permute-start.8 = (f32[4096]{0:T(1024)S(1)}, f32[4096]{0:T(1024)S(1)}, u32[]{:S(2)}, u32[]{:S(2)}) collective-permute-start(f32[4096]{0:T(1024)S(1)} %select_add_fusion.2), channel_id=1, source_target_pairs={{0,8},{1,9},{2,10},{3,11},{4,12},{5,13},{6,14},{7,15},{8,0},{9,1},... | collective-permute-start | bytes 49160 | tf_op jit(solution)/shard_map/ppermute | solution.py:151
  190.3 5.5 %collective-permute-start.9 = (f32[8192]{0:T(1024)S(1)}, f32[8192]{0:T(1024)S(1)}, u32[]{:S(2)}, u32[]{:S(2)}) collective-permute-start(f32[8192]{0:T(1024)S(1)} %maximum_select_fusion.5), channel_id=1, source_target_pairs={{0,4},{1,5},{2,6},{3,7},{4,0},{5,1},{6,2},{7,3},{8,12},{9,13},{10,... | collective-permute-start | bytes 98312 | tf_op jit(solution)/shard_map/ppermute | solution.py:151
  195.9 5.4 %collective-permute-start.10 = (f32[16384]{0:T(1024)S(1)}, f32[16384]{0:T(1024)S(1)}, u32[]{:S(2)}, u32[]{:S(2)}) collective-permute-start(f32[16384]{0:T(1024)S(1)} %maximum_select_fusion.3), channel_id=1, source_target_pairs={{0,2},{1,3},{2,0},{3,1},{4,6},{5,7},{6,4},{7,5},{8,10},{9,11},{10,... | collective-permute-start | bytes 196616 | tf_op jit(solution)/shard_map/ppermute | solution.py:151
  201.3 9.2 %collective-permute-start.11 = (f32[32768]{0:T(1024)S(1)}, f32[32768]{0:T(1024)S(1)}, u32[]{:S(2)}, u32[]{:S(2)}) collective-permute-start(f32[32768]{0:T(1024)S(1)} %maximum_select_fusion.1), channel_id=1, source_target_pairs={{0,1},{1,0},{2,3},{3,2},{4,5},{5,4},{6,7},{7,6},{8,9},{9,8},{10,11... | collective-permute-start | bytes 393224 | tf_op jit(solution)/shard_map/ppermute | solution.py:151

commit v3 on v2

--- a/solution.py
+++ b/solution.py
@@ -2,6 +2,9 @@
 import jax.numpy as jnp
 from jax import lax
 from jax.sharding import PartitionSpec as P
+from jax.experimental import pallas as pl
+from jax.experimental.pallas import tpu as pltpu
+import functools
 
 STEPS = 2
 
@@ -151,6 +154,79 @@
         other = lax.ppermute(piece, axis, pairs)
         piece = jnp.where(upper, jnp.concatenate([other, piece]), jnp.concatenate([piece, other]))
     return piece.reshape(shape)
+
+
+def allreduce_kernel(count, local_ref, out_ref, gathered, reduced, spread, send1, recv1, send2, recv2):
+    me = lax.axis_index("shots")
+    slab = lax.axis_index("slab")
+    barrier = pltpu.get_barrier_semaphore()
+    for k in range(1, count):
+        peer = lax.rem(me + k, count)
+        pl.semaphore_signal(
+            barrier, inc=1, device_id=(slab, peer), device_id_type=pl.DeviceIdType.MESH
+        )
+    pl.semaphore_wait(barrier, count - 1)
+    copies = []
+    for k in range(1, count):
+        peer = lax.rem(me + k, count)
+        copy = pltpu.make_async_remote_copy(
+            src_ref=local_ref.at[peer],
+            dst_ref=gathered.at[k],
+            send_sem=send1.at[k],
+            recv_sem=recv1.at[k],
+            device_id=(slab, peer),
+            device_id_type=pl.DeviceIdType.MESH,
+        )
+        copy.start()
+        copies.append(copy)
+    for copy in copies:
+        copy.wait()
+    total = local_ref[me]
+    for k in range(1, count):
+        total = total + gathered[k]
+    reduced[...] = total
+    copies = []
+    for k in range(1, count):
+        peer = lax.rem(me + k, count)
+        copy = pltpu.make_async_remote_copy(
+            src_ref=reduced,
+            dst_ref=spread.at[k],
+            send_sem=send2.at[k],
+            recv_sem=recv2.at[k],
+            device_id=(slab, peer),
+            device_id_type=pl.DeviceIdType.MESH,
+        )
+        copy.start()
+        copies.append(copy)
+    out_ref[me] = total
+    for copy in copies:
+        copy.wait()
+    for k in range(1, count):
+        out_ref[lax.rem(me + count - k, count)] = spread[k]
+
+
+def shots_sum(value):
+    count = lax.axis_size("shots")
+    shape = value.shape
+    chunks = value.reshape(count, -1, 128)
+    rows = chunks.shape[1]
+    out = pl.pallas_call(
+        functools.partial(allreduce_kernel, count),
+        out_shape=jax.ShapeDtypeStruct(chunks.shape, jnp.float32),
+        in_specs=[pl.BlockSpec(memory_space=pltpu.VMEM)],
+        out_specs=pl.BlockSpec(memory_space=pltpu.VMEM),
+        scratch_shapes=[
+            pltpu.VMEM((count, rows, 128), jnp.float32),
+            pltpu.VMEM((rows, 128), jnp.float32),
+            pltpu.VMEM((count, rows, 128), jnp.float32),
+            pltpu.SemaphoreType.DMA((count,)),
+            pltpu.SemaphoreType.DMA((count,)),
+            pltpu.SemaphoreType.DMA((count,)),
+            pltpu.SemaphoreType.DMA((count,)),
+        ],
+        compiler_params=pltpu.CompilerParams(collective_id=0, has_side_effects=True),
+    )(chunks)
+    return out.reshape(shape)
 
 
 def per_device(
@@ -190,7 +266,7 @@
     local_sum = terms[0]
     for extra in terms[1:]:
         local_sum = local_sum + extra
-    image = tree_sum(local_sum, "shots")
+    image = shots_sum(local_sum)
     return (src_last, rcv_last, image)
 
 

time: 213 us -> 193 us (0.906)
  the two profiles are of different devices: /device:TPU:7 before, /device:TPU:39 now
where the time goes in v3:
time: 193 us; the launch traced here: 192 us
  waiting for transfers between devices  54.8 us (28%)
  local copies, waits for them, and re-layouts  54.5 us (28%)
  Pallas kernels  30.2 us (16%)
  starting transfers between devices  22 us (11%)
  other arithmetic  18 us (9%)
  between operations  8.95 us (5%)
  matrix products  3.11 us (2%)
    ppermute x2, waiting for transfers between devices, extended(): lax.ppermute(cut_windows(lax.slice_in_dim(block, 0, width, axis=dim), row...  43.5 us
    pallas_call x1, Pallas kernels, shots_sum(): pl.pallas_call(functools.partial(allreduce_kernel, count), out_shape=jax....  30.2 us
    dynamic_update_slice x8, local copies, waits for them, and re-layouts, paste_windows(): lax.dynamic_update_slice(empty, piece, (0, 0, row0[s], col0[s]))  29.4 us
    ppermute x2, starting transfers between devices, extended(): lax.ppermute(cut_windows(lax.slice_in_dim(block, block.shape[dim] - width...  16.4 us
    ppermute x2, waiting for transfers between devices, extended(): lax.ppermute(cut_windows(lax.slice_in_dim(block, block.shape[dim] - width...  11.2 us
    another operation x16, local copies, waits for them, and re-layouts, paste_windows(): return jnp.stack(pieces, axis=1)  10.5 us
    ppermute x2, starting transfers between devices, extended(): lax.ppermute(cut_windows(lax.slice_in_dim(block, 0, width, axis=dim), row...  5.58 us
    another operation x8, local copies, waits for them, and re-layouts, cut_windows(): return jnp.stack(pieces, axis=1)  5.04 us
  transfers between devices with their start and end apart: 4, of which 4 were waited for; matrix products, arithmetic and copies ran while one was open for 7% of the time, Pallas kernels for 0%

profile of v3, /device:TPU:39, one launch (start us, length us, event | category | flops | bytes accessed | tf_op | source)
XLA Modules:
  0.0 191.5 jit_solution(3766685353585783501)
XLA Ops:
  12.6 14.5 %collective-permute-start.1 = (f32[2,2,121,128]{3,2,0,1:T(8,128)S(1)}, f32[2,2,121,128]{3,2,0,1:T(8,128)S(1)}, u32[]{:S(2)}, u32[]{:S(2)}) collective-permute-start(f32[2,2,121,128]{3,2,0,1:T(8,128)S(1)} %pad_maximum_fusion.3), channel_id=1, source_target_pairs={{0,16},{16,32},{32,48},{48,64},{64,80},{80,96},{96,112},{112,128},... | collective-permute-start | bytes 743432 | tf_op jit(solution)/shard_map/ppermute | solution.py:52
  27.7 2.1 %collective-permute-start = (f32[2,2,121,128]{3,2,0,1:T(8,128)S(1)}, f32[2,2,121,128]{3,2,0,1:T(8,128)S(1)}, u32[]{:S(2)}, u32[]{:S(2)}) collective-permute-start(f32[2,2,121,128]{3,2,0,1:T(8,128)S(1)} %pad_maximum_fusion.2), channel_id=1, source_target_pairs={{16,0},{32,16},{48,32},{64,48},{80,64},{96,80},{112,96},{128,112},... | collective-permute-start | bytes 743432 | tf_op jit(solution)/shard_map/ppermute | solution.py:57
  33.5 9.3 %collective-permute-done.1 = f32[2,2,121,128]{3,2,0,1:T(8,128)S(1)} collective-permute-done((f32[2,2,121,128]{3,2,0,1:T(8,128)S(1)}, f32[2,2,121,128]{3,2,0,1:T(8,128)S(1)}, u32[]{:S(2)}, u32[]{:S(2)}) %collective-permute-start.1) | collective-permute-done | bytes 247840 | tf_op jit(solution)/shard_map/ppermute | solution.py:52
  43.2 21.5 %collective-permute-done = f32[2,2,121,128]{3,2,0,1:T(8,128)S(1)} collective-permute-done((f32[2,2,121,128]{3,2,0,1:T(8,128)S(1)}, f32[2,2,121,128]{3,2,0,1:T(8,128)S(1)}, u32[]{:S(2)}, u32[]{:S(2)}) %collective-permute-start) | collective-permute-done | bytes 247840 | tf_op jit(solution)/shard_map/ppermute | solution.py:57
  65.1 3.3 %dynamic_update_slice.34 = f32[2,1,4,64,128]{4,3,2,1,0:T(8,128)S(1)} dynamic-update-slice(f32[2,1,4,64,128]{4,3,2,1,0:T(8,128)S(1)} %stack.71.clone.3, f32[2,1,4,44,88]{4,3,2,1,0:T(8,128)S(1)} %bitcast.99, s32[]{:T(128)} %constant.64.clone.1, s32[]{:T(128)} %constant.64.clone.1, s32[]{:T(128)} %constant.64.clone.1, s32[]{:T(128)S(6)} %select_n.32, s32[]{:T(128)S(6)} %select_n.33) | dynamic-update-slice | bytes 247812 | tf_op jit(solution)/shard_map/dynamic_update_slice | solution.py:42
  68.4 3.4 %dynamic_update_slice.35 = f32[2,1,4,64,128]{4,3,2,1,0:T(8,128)S(1)} dynamic-update-slice(f32[2,1,4,64,128]{4,3,2,1,0:T(8,128)S(1)} %stack.71.clone.2, f32[2,1,4,44,88]{4,3,2,1,0:T(8,128)S(1)} %bitcast.97, s32[]{:T(128)} %constant.64.clone.1, s32[]{:T(128)} %constant.64.clone.1, s32[]{:T(128)} %constant.64.clone.1, s32[]{:T(128)S(6)} %select_n.34, s32[]{:T(128)S(6)} %select_n.35) | dynamic-update-slice | bytes 247812 | tf_op jit(solution)/shard_map/dynamic_update_slice | solution.py:42
  71.8 3.3 %dynamic_update_slice.32 = f32[2,1,4,64,128]{4,3,2,1,0:T(8,128)S(1)} dynamic-update-slice(f32[2,1,4,64,128]{4,3,2,1,0:T(8,128)S(1)} %stack.71.clone.1, f32[2,1,4,44,88]{4,3,2,1,0:T(8,128)S(1)} %bitcast.103, s32[]{:T(128)} %constant.64.clone.1, s32[]{:T(128)} %constant.64.clone.1, s32[]{:T(128)} %constant.64.clone.1, s32[]{:T(128)S(6)} %select_n.32, s32[]{:T(128)S(6)} %select_n.33) | dynamic-update-slice | bytes 247812 | tf_op jit(solution)/shard_map/dynamic_update_slice | solution.py:42
  75.1 3.4 %dynamic_update_slice.33 = f32[2,1,4,64,128]{4,3,2,1,0:T(8,128)S(1)} dynamic-update-slice(f32[2,1,4,64,128]{4,3,2,1,0:T(8,128)S(1)} %stack.71.clone, f32[2,1,4,44,88]{4,3,2,1,0:T(8,128)S(1)} %bitcast.102, s32[]{:T(128)} %constant.64.clone.1, s32[]{:T(128)} %constant.64.clone.1, s32[]{:T(128)} %constant.64.clone.1, s32[]{:T(128)S(6)} %select_n.34, s32[]{:T(128)S(6)} %select_n.35) | dynamic-update-slice | bytes 247812 | tf_op jit(solution)/shard_map/dynamic_update_slice | solution.py:42
  78.9 2.5 %fusion.6 = f32[2,2,8,64,128]{4,3,2,1,0:T(8,128)S(1)} fusion(f32[2,2,8,64,128]{4,3,2,1,0:T(8,128)S(1)} %pad_maximum_fusion, f32[2,2,12,64,128]{4,3,2,1,0:T(8,128)S(1)} %get-tuple-element.15, f32[2,2,12,64,128]{4,3,2,1,0:T(8,128)S(1)} %get-tuple-element.14), kind=kLoop, calls=%fused_computation.60 | loop fusion | flops 8650752 | bytes 10485760 | tf_op jit(solution)/shard_map/add | solution.py:87
  84.4 1.7 stack_reshape.30
  86.1 1.9 dynamic-slice_maximum_fusion
  87.9 1.7 stack_reshape.31
  89.7 1.7 pad_maximum_fusion.5
  91.3 1.9 collective-permute-start.3
  96.2 3.5 %collective-permute-start.2 = (f32[2,2,121,128]{3,2,0,1:T(8,128)}, f32[2,2,121,128]{3,2,0,1:T(8,128)}, u32[]{:S(2)}, u32[]{:S(2)}) collective-permute-start(f32[2,2,121,128]{3,2,0,1:T(8,128)} %pad_maximum_fusion.4), channel_id=1, source_target_pairs={{16,0},{32,16},{48,32},{64,48},{80,64},{96,80},{112,96},{128,112},... | collective-permute-start | bytes 743432 | tf_op jit(solution)/shard_map/ppermute | solution.py:57
  99.9 1.9 %collective-permute-done.3 = f32[2,2,121,128]{3,2,0,1:T(8,128)} collective-permute-done((f32[2,2,121,128]{3,2,0,1:T(8,128)}, f32[2,2,121,128]{3,2,0,1:T(8,128)}, u32[]{:S(2)}, u32[]{:S(2)}) %collective-permute-start.3) | collective-permute-done | bytes 247840 | tf_op jit(solution)/shard_map/ppermute | solution.py:52
  101.8 1.7 fusion.89
  103.5 1.7 stack.88
  105.2 1.7 stack.89
  106.9 22.0 %collective-permute-done.2 = f32[2,2,121,128]{3,2,0,1:T(8,128)} collective-permute-done((f32[2,2,121,128]{3,2,0,1:T(8,128)}, f32[2,2,121,128]{3,2,0,1:T(8,128)}, u32[]{:S(2)}, u32[]{:S(2)}) %collective-permute-start.2) | collective-permute-done | bytes 247840 | tf_op jit(solution)/shard_map/ppermute | solution.py:57
  128.9 1.7 fusion.88
  130.6 1.7 stack.84
  132.3 1.7 stack.85
  134.8 4.0 %dynamic_update_slice.38 = f32[2,1,4,64,128]{4,3,2,1,0:T(8,128)} dynamic-update-slice(f32[2,1,4,64,128]{4,3,2,1,0:T(8,128)} %stack.71.clone.7, f32[2,1,4,44,88]{4,3,2,1,0:T(8,128)} %bitcast.100, s32[]{:T(128)} %constant.64.clone.1, s32[]{:T(128)} %constant.64.clone.1, s32[]{:T(128)} %constant.64.clone.1, s32[]{:T(128)S(6)} %select_n.32, s32[]{:T(128)S(6)} %select_n.33) | dynamic-update-slice | bytes 247812 | tf_op jit(solution)/shard_map/dynamic_update_slice | solution.py:42
  139.5 4.1 %dynamic_update_slice.39 = f32[2,1,4,64,128]{4,3,2,1,0:T(8,128)} dynamic-update-slice(f32[2,1,4,64,128]{4,3,2,1,0:T(8,128)} %stack.71.clone.6, f32[2,1,4,44,88]{4,3,2,1,0:T(8,128)} %bitcast.98, s32[]{:T(128)} %constant.64.clone.1, s32[]{:T(128)} %constant.64.clone.1, s32[]{:T(128)} %constant.64.clone.1, s32[]{:T(128)S(6)} %select_n.34, s32[]{:T(128)S(6)} %select_n.35) | dynamic-update-slice | bytes 247812 | tf_op jit(solution)/shard_map/dynamic_update_slice | solution.py:42
  144.3 4.0 %dynamic_update_slice.36 = f32[2,1,4,64,128]{4,3,2,1,0:T(8,128)} dynamic-update-slice(f32[2,1,4,64,128]{4,3,2,1,0:T(8,128)} %stack.71.clone.5, f32[2,1,4,44,88]{4,3,2,1,0:T(8,128)} %bitcast.101, s32[]{:T(128)} %constant.64.clone.1, s32[]{:T(128)} %constant.64.clone.1, s32[]{:T(128)} %constant.64.clone.1, s32[]{:T(128)S(6)} %select_n.32, s32[]{:T(128)S(6)} %select_n.33) | dynamic-update-slice | bytes 247812 | tf_op jit(solution)/shard_map/dynamic_update_slice | solution.py:42
  149.0 4.1 %dynamic_update_slice.37 = f32[2,1,4,64,128]{4,3,2,1,0:T(8,128)} dynamic-update-slice(f32[2,1,4,64,128]{4,3,2,1,0:T(8,128)} %stack.71.clone.4, f32[2,1,4,44,88]{4,3,2,1,0:T(8,128)} %bitcast.96, s32[]{:T(128)} %constant.64.clone.1, s32[]{:T(128)} %constant.64.clone.1, s32[]{:T(128)} %constant.64.clone.1, s32[]{:T(128)S(6)} %select_n.34, s32[]{:T(128)S(6)} %select_n.35) | dynamic-update-slice | bytes 247812 | tf_op jit(solution)/shard_map/dynamic_update_slice | solution.py:42
  153.1 1.6 maximum_maximum_fusion.2
  154.8 2.5 %fusion.26 = f32[2,2,8,64,128]{4,3,2,1,0:T(8,128)S(1)} fusion(f32[2,2,8,64,128]{4,3,2,1,0:T(8,128)S(1)} %pad_maximum_fusion.1, f32[2,2,12,64,128]{4,3,2,1,0:T(8,128)S(1)} %get-tuple-element.13, f32[2,2,12,64,128]{4,3,2,1,0:T(8,128)S(1)} %get-tuple-element.12), kind=kLoop, calls=%fused_computation.80 | loop fusion | flops 8650752 | bytes 10485760 | tf_op jit(solution)/shard_map/add | solution.py:87
  157.3 1.7 multiply_reduce_fusion
  159.6 30.2 %shard_map.148 = f32[16,32,128]{2,1,0:T(8,128)} custom-call(f32[16,32,128]{2,1,0:T(8,128)} %bitcast.94), custom_call_target="tpu_custom_call" | custom-call | tf_op jit(solution)/shard_map/pallas_call | solution.py:213
  189.8 1.7 copy.33
  (85 shorter events, 19.1 us)
Async XLA Ops:
  12.3 17.5 %copy-start.10 = (s32[2]{0:T(128)S(1)}, s32[2]{0:T(128)}, u32[]{:S(2)}) copy-start(s32[2]{0:T(128)} %param.21) | copy-start | bytes 28
  12.4 17.5 %copy-start.11 = (s32[2]{0:T(128)S(1)}, s32[2]{0:T(128)}, u32[]{:S(2)}) copy-start(s32[2]{0:T(128)} %param.23) | copy-start | bytes 28
  12.4 17.5 %copy-start.12 = (s32[2]{0:T(128)S(1)}, s32[2]{0:T(128)}, u32[]{:S(2)}) copy-start(s32[2]{0:T(128)} %param.22) | copy-start | bytes 28
  12.4 17.5 %copy-start.13 = (s32[2]{0:T(128)S(1)}, s32[2]{0:T(128)}, u32[]{:S(2)}) copy-start(s32[2]{0:T(128)} %param.24) | copy-start | bytes 28
  12.4 17.6 %copy-start.9 = (s32[2,256]{1,0:T(2,128)S(1)}, s32[2,256]{1,0:T(2,128)}, u32[]{:S(2)}) copy-start(s32[2,256]{1,0:T(2,128)} %param.25) | copy-start | bytes 6148
  12.4 17.6 %copy-start.8 = (f32[2,2,256]{2,1,0:T(2,128)S(1)}, f32[2,2,256]{2,1,0:T(2,128)}, u32[]{:S(2)}) copy-start(f32[2,2,256]{2,1,0:T(2,128)} %param.19) | copy-start | bytes 12292
  12.4 17.6 %copy-start.15 = (s32[2]{0:T(128)S(1)}, s32[2]{0:T(128)}, u32[]{:S(2)}) copy-start(s32[2]{0:T(128)} %param.20) | copy-start | bytes 28
  12.6 30.2 %collective-permute-start.1 = (f32[2,2,121,128]{3,2,0,1:T(8,128)S(1)}, f32[2,2,121,128]{3,2,0,1:T(8,128)S(1)}, u32[]{:S(2)}, u32[]{:S(2)}) collective-permute-start(f32[2,2,121,128]{3,2,0,1:T(8,128)S(1)} %pad_maximum_fusion.3), channel_id=1, source_target_pairs={{0,16},{16,32},{32,48},{48,64},{64,80},{80,96},{96,112},{112,128},... | collective-permute-start | bytes 743432 | tf_op jit(solution)/shard_map/ppermute | solution.py:52
  27.5 5.9 %copy-start.14 = (f32[2,2]{1,0:T(2,128)S(1)}, f32[2,2]{1,0:T(2,128)}, u32[]{:S(2)}) copy-start(f32[2,2]{1,0:T(2,128)} %param.18) | copy-start | bytes 52
  27.5 5.9 %copy-start = (f32[2,8,64,128]{3,2,1,0:T(8,128)S(1)}, f32[2,8,64,128]{3,2,1,0:T(8,128)}, u32[]{:S(2)}) copy-start(f32[2,8,64,128]{3,2,1,0:T(8,128)} %param.14) | copy-start | bytes 1572868
  27.6 5.9 %copy-start.1 = (f32[2,8,64,128]{3,2,1,0:T(8,128)S(1)}, f32[2,8,64,128]{3,2,1,0:T(8,128)}, u32[]{:S(2)}) copy-start(f32[2,8,64,128]{3,2,1,0:T(8,128)} %param.16) | copy-start | bytes 1572868
  27.7 37.0 %collective-permute-start = (f32[2,2,121,128]{3,2,0,1:T(8,128)S(1)}, f32[2,2,121,128]{3,2,0,1:T(8,128)S(1)}, u32[]{:S(2)}, u32[]{:S(2)}) collective-permute-start(f32[2,2,121,128]{3,2,0,1:T(8,128)S(1)} %pad_maximum_fusion.2), channel_id=1, source_target_pairs={{16,0},{32,16},{48,32},{64,48},{80,64},{96,80},{112,96},{128,112},... | collective-permute-start | bytes 743432 | tf_op jit(solution)/shard_map/ppermute | solution.py:57
  78.9 2.5 %copy-start.2 = (f32[2,8,64,128]{3,2,1,0:T(8,128)S(1)}, f32[2,8,64,128]{3,2,1,0:T(8,128)}, u32[]{:S(2)}) copy-start(f32[2,8,64,128]{3,2,1,0:T(8,128)} %param.13) | copy-start | bytes 1572868
  78.9 2.5 %copy-start.4 = (f32[8,64,128]{2,1,0:T(8,128)S(1)}, f32[8,64,128]{2,1,0:T(8,128)}, u32[]{:S(2)}) copy-start(f32[8,64,128]{2,1,0:T(8,128)} %param.17) | copy-start | bytes 786436
  78.9 2.5 %copy-start.5 = (f32[2,8,64,128]{3,2,1,0:T(8,128)S(1)}, f32[2,8,64,128]{3,2,1,0:T(8,128)}, u32[]{:S(2)}) copy-start(f32[2,8,64,128]{3,2,1,0:T(8,128)} %param.15) | copy-start | bytes 1572868
  78.9 2.5 %copy-start.7 = (f32[2,512,128]{2,1,0:T(8,128)S(1)}, f32[2,512,128]{2,1,0:T(8,128)}, u32[]{:S(2)}) copy-start(f32[2,512,128]{2,1,0:T(8,128)} %fusion.58) | copy-start | bytes 1572868
  91.3 10.4 %collective-permute-start.3 = (f32[2,2,121,128]{3,2,0,1:T(8,128)}, f32[2,2,121,128]{3,2,0,1:T(8,128)}, u32[]{:S(2)}, u32[]{:S(2)}) collective-permute-start(f32[2,2,121,128]{3,2,0,1:T(8,128)} %pad_maximum_fusion.5), channel_id=1, source_target_pairs={{0,16},{16,32},{32,48},{48,64},{64,80},{80,96},{96,112},{112,128},... | collective-permute-start | bytes 743432 | tf_op jit(solution)/shard_map/ppermute | solution.py:52
  96.2 32.7 %collective-permute-start.2 = (f32[2,2,121,128]{3,2,0,1:T(8,128)}, f32[2,2,121,128]{3,2,0,1:T(8,128)}, u32[]{:S(2)}, u32[]{:S(2)}) collective-permute-start(f32[2,2,121,128]{3,2,0,1:T(8,128)} %pad_maximum_fusion.4), channel_id=1, source_target_pairs={{16,0},{32,16},{48,32},{64,48},{80,64},{96,80},{112,96},{128,112},... | collective-permute-start | bytes 743432 | tf_op jit(solution)/shard_map/ppermute | solution.py:57
  154.7 2.5 %copy-start.3 = (f32[2,8,64,128]{3,2,1,0:T(8,128)S(1)}, f32[2,8,64,128]{3,2,1,0:T(8,128)}, u32[]{:S(2)}) copy-start(f32[2,8,64,128]{3,2,1,0:T(8,128)} %param.13) | copy-start | bytes 1572868
  154.8 2.5 %copy-start.6 = (f32[2,512,128]{2,1,0:T(8,128)S(1)}, f32[2,512,128]{2,1,0:T(8,128)}, u32[]{:S(2)}) copy-start(f32[2,512,128]{2,1,0:T(8,128)} %fusion.56) | copy-start | bytes 1572868

commit v4 on v3

--- a/solution.py
+++ b/solution.py
@@ -22,43 +22,54 @@
     return row0, col0
 
 
-def cut_windows(layers, row0, col0):
+def selectors(row0, col0, rows_y, cols_x):
+    pick_y = (
+        jnp.arange(rows_y, dtype=jnp.int32)[None, :, None]
+        == row0[:, None, None] + jnp.arange(WIN_Y, dtype=jnp.int32)[None, None, :]
+    ).astype(jnp.float32)
+    pick_x = (
+        jnp.arange(cols_x, dtype=jnp.int32)[None, None, :]
+        == col0[:, None, None] + jnp.arange(WIN_X, dtype=jnp.int32)[None, :, None]
+    ).astype(jnp.float32)
+    return pick_y, pick_x
+
+
+def exact_einsum(spec, a, b):
+    return jnp.einsum(
+        spec, a, b, precision=lax.Precision.HIGHEST, preferred_element_type=jnp.float32
+    )
+
+
+def cut_windows(layers, pick_y, pick_x):
     fields, shots, width = layers.shape[:3]
-    pieces = []
-    for s in range(shots):
-        piece = lax.dynamic_slice(
-            layers[:, s], (0, 0, row0[s], col0[s]), (fields, width, WIN_Y, WIN_X)
-        )
-        pieces.append(piece.reshape(fields, -1, 128))
-    return jnp.stack(pieces, axis=1)
-
-
-def paste_windows(flat, row0, col0, width, rows_y, cols_x):
+    part = exact_einsum("fsjyx,sbx->fsjyb", layers, pick_x)
+    part = exact_einsum("sya,fsjyb->fsjab", pick_y, part)
+    return part.reshape(fields, shots, -1, 128)
+
+
+def paste_windows(flat, pick_y, pick_x, width):
     fields, shots = flat.shape[:2]
-    pieces = []
-    for s in range(shots):
-        piece = flat[:, s].reshape(fields, width, WIN_Y, WIN_X)
-        empty = jnp.zeros((fields, width, rows_y, cols_x), flat.dtype)
-        pieces.append(lax.dynamic_update_slice(empty, piece, (0, 0, row0[s], col0[s])))
-    return jnp.stack(pieces, axis=1)
-
-
-def extended(block, row0, col0, width):
+    part = flat.reshape(fields, shots, width, WIN_Y, WIN_X)
+    part = exact_einsum("fsjab,sbx->fsjax", part, pick_x)
+    return exact_einsum("sya,fsjax->fsjyx", pick_y, part)
+
+
+def extended(block, pick_y, pick_x, width):
     count = lax.axis_size("slab")
     forward = [(i, i + 1) for i in range(count - 1)]
     backward = [(target, source) for source, target in forward]
     dim = 2
     rows_y, cols_x = block.shape[-2:]
     low = lax.ppermute(
-        cut_windows(lax.slice_in_dim(block, block.shape[dim] - width, None, axis=dim), row0, col0),
+        cut_windows(lax.slice_in_dim(block, block.shape[dim] - width, None, axis=dim), pick_y, pick_x),
         "slab",
         forward,
     )
     high = lax.ppermute(
-        cut_windows(lax.slice_in_dim(block, 0, width, axis=dim), row0, col0), "slab", backward
-    )
-    low = paste_windows(low, row0, col0, width, rows_y, cols_x)
-    high = paste_windows(high, row0, col0, width, rows_y, cols_x)
+        cut_windows(lax.slice_in_dim(block, 0, width, axis=dim), pick_y, pick_x), "slab", backward
+    )
+    low = paste_windows(low, pick_y, pick_x, width)
+    high = paste_windows(high, pick_y, pick_x, width)
     return jnp.concatenate([low, block, high], axis=dim)
 
 
@@ -248,11 +259,12 @@
     start = lax.axis_index("slab") * depth
     mask = band_mask(source_y, source_x, half_y, half_x, rows_y, cols_x)[:, None]
     row0, col0 = band_corner(source_y, source_x, half_y, half_x, rows_y, cols_x)
+    pick_y, pick_x = selectors(row0, col0, rows_y, cols_x)
     terms = []
     up, u, vp, v = (src_prev, src_cur, rcv_prev, rcv_cur)
     for step in range(STEPS):
         stacked = jnp.stack([u, v])
-        padded = extended(stacked, row0, col0, 4)
+        padded = extended(stacked, pick_y, pick_x, 4)
         lap = laplace(padded)
         sdelta = point_field(
             source_depth - start, source_y, source_x, wavelet[step], depth, rows_y, cols_x

time: 193 us -> 150 us (0.78)
  the two profiles are of different devices: /device:TPU:39 before, /device:TPU:25 now
where the time goes in v4:
time: 150 us; the launch traced here: 148 us
  Pallas kernels  65.5 us (44%)
  starting transfers between devices  37.1 us (25%)
  waiting for transfers between devices  14.5 us (10%)
  other arithmetic  12 us (8%)
  matrix products  10.6 us (7%)
  local copies, waits for them, and re-layouts  7.29 us (5%)
    pallas_call x1, Pallas kernels, shots_sum(): pl.pallas_call(functools.partial(allreduce_kernel, count), out_shape=jax....  65.5 us
    ppermute x2, starting transfers between devices, extended(): lax.ppermute(cut_windows(lax.slice_in_dim(block, 0, width, axis=dim), pic...  31.9 us
    ppermute x2, waiting for transfers between devices, extended(): lax.ppermute(cut_windows(lax.slice_in_dim(block, block.shape[dim] - width...  11.4 us
    dot_general x16, matrix products, exact_einsum(): jnp.einsum(spec, a, b, precision=lax.Precision.HIGHEST, preferred_element...  7.45 us
    ppermute x2, starting transfers between devices, extended(): lax.ppermute(cut_windows(lax.slice_in_dim(block, block.shape[dim] - width...  5.22 us
    add x2, other arithmetic, laplace(): total = total + COEF[shift_k] * (side_y + side_x)  4.91 us
    reshape x4, local copies, waits for them, and re-layouts, paste_windows(): part = flat.reshape(fields, shots, width, WIN_Y, WIN_X)  3.13 us
    dot_general x2, matrix products, receiver_field(): jnp.einsum('szr,srx->szx', left, right, precision=lax.Precision.HIGHEST,...  3.11 us
  transfers between devices with their start and end apart: 4, of which 2 were waited for; matrix products, arithmetic and copies ran while one was open for 8% of the time, Pallas kernels for 0%

profile of v4, /device:TPU:25, one launch (start us, length us, event | category | flops | bytes accessed | tf_op | source)
XLA Modules:
  0.0 148.2 jit_solution(631710939837506352)
XLA Ops:
  0.6 0.7 subtract_clamp_fusion.1
  1.4 0.7 subtract_clamp_fusion
  2.1 1.3 fusion.66
  3.4 0.4 convolution_bitcast_fusion.5
  4.5 3.1 %collective-permute-start.1 = (f32[2,2,121,128]{3,2,1,0:T(8,128)S(1)}, f32[2,2,121,128]{3,2,1,0:T(8,128)S(1)}, u32[]{:S(2)}, u32[]{:S(2)}) collective-permute-start(f32[2,2,121,128]{3,2,1,0:T(8,128)S(1)} %copy.39), channel_id=1, source_target_pairs={{0,16},{16,32},{32,48},{48,64},{64,80},{80,96},{96,112},{112,128},... | collective-permute-start | bytes 743432 | tf_op jit(solution)/shard_map/ppermute | solution.py:63
  7.7 0.4 convolution_bitcast_fusion.7
  8.8 16.6 %collective-permute-start = (f32[2,2,121,128]{3,2,1,0:T(8,128)S(1)}, f32[2,2,121,128]{3,2,1,0:T(8,128)S(1)}, u32[]{:S(2)}, u32[]{:S(2)}) collective-permute-start(f32[2,2,121,128]{3,2,1,0:T(8,128)S(1)} %copy.38), channel_id=1, source_target_pairs={{16,0},{32,16},{48,32},{64,48},{80,64},{96,80},{112,96},{128,112},... | collective-permute-start | bytes 743432 | tf_op jit(solution)/shard_map/ppermute | solution.py:68
  25.7 0.6 slice_bitcast_fusion.6
  26.5 1.6 %fusion.58 = f32[2,512,128]{2,1,0:T(8,128)} fusion(f32[2,256]{1,0:T(2,128)S(1)} %get-tuple-element.21, s32[2,256]{1,0:T(2,128)S(1)} %multiply_add_fusion, s32[2,256]{1,0:T(2,128)S(1)} %get-tuple-element.7), kind=kOutput, calls=%fused_computation.128 | convolution fusion | flops 403243008 | bytes 530432 | tf_op jit(solution)/shard_map/szr,srx->szx/dot_general | solution.py:135
  28.2 1.6 %fusion.56 = f32[2,512,128]{2,1,0:T(8,128)} fusion(f32[2,256]{1,0:T(2,128)S(1)} %get-tuple-element.20, s32[2,256]{1,0:T(2,128)S(1)} %multiply_add_fusion, s32[2,256]{1,0:T(2,128)S(1)} %get-tuple-element.7), kind=kOutput, calls=%fused_computation.126 | convolution fusion | flops 403243008 | bytes 530432 | tf_op jit(solution)/shard_map/szr,srx->szx/dot_general | solution.py:135
  30.0 0.4 convolution_bitcast_fusion.12
  30.4 0.5 convolution_bitcast_fusion.4
  31.2 0.4 convolution_bitcast_fusion.14
  31.6 0.5 convolution_bitcast_fusion.6
  32.6 2.5 %fusion.6 = f32[2,2,8,64,128]{4,3,2,1,0:T(8,128)S(1)} fusion(f32[2,2,8,64,128]{4,3,2,1,0:T(8,128)S(1)} %pad_maximum_fusion.2, f32[2,2,12,64,128]{4,3,2,1,0:T(8,128)S(1)} %get-tuple-element.17, f32[2,2,12,64,128]{4,3,2,1,0:T(8,128)S(1)} %get-tuple-element.16), kind=kLoop, calls=%fused_computation.68 | loop fusion | flops 8650752 | bytes 10485760 | tf_op jit(solution)/shard_map/add | solution.py:98
  35.1 0.5 fusion.77
  35.6 0.4 convolution_bitcast_fusion.3
  36.7 15.3 %collective-permute-start.2 = (f32[2,2,121,128]{3,2,1,0:T(8,128)S(1)}, f32[2,2,121,128]{3,2,1,0:T(8,128)}, u32[]{:S(2)}, u32[]{:S(2)}) collective-permute-start(f32[2,2,121,128]{3,2,1,0:T(8,128)S(1)} %copy.40), channel_id=1, source_target_pairs={{16,0},{32,16},{48,32},{64,48},{80,64},{96,80},{112,96},{128,112},... | collective-permute-start | bytes 743432 | tf_op jit(solution)/shard_map/ppermute | solution.py:68
  52.0 0.4 convolution_bitcast_fusion.1
  53.0 0.7 copy.41
  53.7 2.1 %collective-permute-start.3 = (f32[2,2,121,128]{3,2,1,0:T(8,128)}, f32[2,2,121,128]{3,2,1,0:T(8,128)}, u32[]{:S(2)}, u32[]{:S(2)}) collective-permute-start(f32[2,2,121,128]{3,2,1,0:T(8,128)} %copy.41), channel_id=1, source_target_pairs={{0,16},{16,32},{32,48},{48,64},{64,80},{80,96},{96,112},{112,128},... | collective-permute-start | bytes 743432 | tf_op jit(solution)/shard_map/ppermute | solution.py:63
  55.9 3.1 %collective-permute-done.2 = f32[2,2,121,128]{3,2,1,0:T(8,128)} collective-permute-done((f32[2,2,121,128]{3,2,1,0:T(8,128)S(1)}, f32[2,2,121,128]{3,2,1,0:T(8,128)}, u32[]{:S(2)}, u32[]{:S(2)}) %collective-permute-start.2) | collective-permute-done | bytes 247840 | tf_op jit(solution)/shard_map/ppermute | solution.py:68
  59.0 1.3 reshape.264
  60.7 1.3 convolution_bitcast_fusion.2
  61.9 11.4 %collective-permute-done.3 = f32[2,2,121,128]{3,2,1,0:T(8,128)} collective-permute-done((f32[2,2,121,128]{3,2,1,0:T(8,128)}, f32[2,2,121,128]{3,2,1,0:T(8,128)}, u32[]{:S(2)}, u32[]{:S(2)}) %collective-permute-start.3) | collective-permute-done | bytes 247840 | tf_op jit(solution)/shard_map/ppermute | solution.py:63
  73.3 1.3 reshape.266
  75.0 0.5 convolution_bitcast_fusion
  76.1 2.5 %fusion.26 = f32[2,2,8,64,128]{4,3,2,1,0:T(8,128)S(1)} fusion(f32[2,2,8,64,128]{4,3,2,1,0:T(8,128)S(1)} %pad_maximum_fusion.3, f32[2,2,12,64,128]{4,3,2,1,0:T(8,128)S(1)} %get-tuple-element.13, f32[2,2,12,64,128]{4,3,2,1,0:T(8,128)S(1)} %get-tuple-element.12), kind=kLoop, calls=%fused_computation.88 | loop fusion | flops 8650752 | bytes 10485760 | tf_op jit(solution)/shard_map/add | solution.py:98
  78.6 1.6 %multiply_reduce_fusion = (f32[8,64,128]{2,1,0:T(8,128)S(1)}, f32[8,64,128]{2,1,0:T(8,128)S(1)}, f32[2,8,64,128]{3,2,1,0:T(8,128)}, f32[2,8,64,128]{3,2,1,0:T(8,128)}) fusion(f32[2,8,64,128]{3,2,1,0:T(8,128)S(1)} %copy-done, f32[2,8,64,128]{3,2,1,0:T(8,128)S(1)} %get-tuple-element.11, f32[2,8,64,128]{3,2,1,0:T(8,128)S(1)} %get-tuple-element.10, ...), kind=kLoop, calls=%fused_computation.161 | loop fusion | flops 2883584 | bytes 6096136 | tf_op jit(solution)/shard_map/reduce_sum | solution.py:275
  80.2 0.7 add.292
  81.0 65.5 %shard_map.148 = f32[16,32,128]{2,1,0:T(8,128)} custom-call(f32[16,32,128]{2,1,0:T(8,128)} %bitcast.138), custom_call_target="tpu_custom_call" | custom-call | tf_op jit(solution)/shard_map/pallas_call | solution.py:224
  146.5 1.7 %copy.67 = f32[8,64,128]{2,1,0:T(8,128)} copy(f32[8,64,128]{2,1,0:T(8,128)} %bitcast.139) | data formatting | bytes 524288
  (75 shorter events, 5.6 us)
Async XLA Ops:
  4.5 25.3 %collective-permute-start.1 = (f32[2,2,121,128]{3,2,1,0:T(8,128)S(1)}, f32[2,2,121,128]{3,2,1,0:T(8,128)S(1)}, u32[]{:S(2)}, u32[]{:S(2)}) collective-permute-start(f32[2,2,121,128]{3,2,1,0:T(8,128)S(1)} %copy.39), channel_id=1, source_target_pairs={{0,16},{16,32},{32,48},{48,64},{64,80},{80,96},{96,112},{112,128},... | collective-permute-start | bytes 743432 | tf_op jit(solution)/shard_map/ppermute | solution.py:63
  7.6 17.8 %copy-start.16 = (s32[2]{0:T(128)S(1)}, s32[2]{0:T(128)}, u32[]{:S(2)}) copy-start(s32[2]{0:T(128)} %param.21) | copy-start | bytes 28
  7.6 17.8 %copy-start.17 = (s32[2]{0:T(128)S(1)}, s32[2]{0:T(128)}, u32[]{:S(2)}) copy-start(s32[2]{0:T(128)} %param.23) | copy-start | bytes 28
  7.6 17.9 %copy-start.18 = (s32[2]{0:T(128)S(1)}, s32[2]{0:T(128)}, u32[]{:S(2)}) copy-start(s32[2]{0:T(128)} %param.22) | copy-start | bytes 28
  7.6 17.9 %copy-start.19 = (s32[2]{0:T(128)S(1)}, s32[2]{0:T(128)}, u32[]{:S(2)}) copy-start(s32[2]{0:T(128)} %param.24) | copy-start | bytes 28
  7.7 17.9 %copy-start.14 = (s32[2,256]{1,0:T(2,128)S(1)}, s32[2,256]{1,0:T(2,128)}, u32[]{:S(2)}) copy-start(s32[2,256]{1,0:T(2,128)} %param.25) | copy-start | bytes 6148
  7.7 18.0 %copy-start.12 = (f32[2,2,256]{2,1,0:T(2,128)S(1)}, f32[2,2,256]{2,1,0:T(2,128)}, u32[]{:S(2)}) copy-start(f32[2,2,256]{2,1,0:T(2,128)} %param.19) | copy-start | bytes 12292
  7.7 18.0 %copy-start.20 = (s32[2]{0:T(128)S(1)}, s32[2]{0:T(128)}, u32[]{:S(2)}) copy-start(s32[2]{0:T(128)} %param.20) | copy-start | bytes 28
  7.7 18.0 %copy-start.15 = (f32[2,2]{1,0:T(2,128)S(1)}, f32[2,2]{1,0:T(2,128)}, u32[]{:S(2)}) copy-start(f32[2,2]{1,0:T(2,128)} %param.18) | copy-start | bytes 52
  8.1 19.9 %copy-start = (f32[2,8,64,128]{3,2,1,0:T(8,128)S(1)}, f32[2,8,64,128]{3,2,1,0:T(8,128)}, u32[]{:S(2)}) copy-start(f32[2,8,64,128]{3,2,1,0:T(8,128)} %param.14) | copy-start | bytes 1572868
  8.2 19.9 %copy-start.1 = (f32[2,8,64,128]{3,2,1,0:T(8,128)S(1)}, f32[2,8,64,128]{3,2,1,0:T(8,128)}, u32[]{:S(2)}) copy-start(f32[2,8,64,128]{3,2,1,0:T(8,128)} %param.16) | copy-start | bytes 1572868
  8.8 22.1 %collective-permute-start = (f32[2,2,121,128]{3,2,1,0:T(8,128)S(1)}, f32[2,2,121,128]{3,2,1,0:T(8,128)S(1)}, u32[]{:S(2)}, u32[]{:S(2)}) collective-permute-start(f32[2,2,121,128]{3,2,1,0:T(8,128)S(1)} %copy.38), channel_id=1, source_target_pairs={{16,0},{32,16},{48,32},{64,48},{80,64},{96,80},{112,96},{128,112},... | collective-permute-start | bytes 743432 | tf_op jit(solution)/shard_map/ppermute | solution.py:68
  26.4 8.6 %copy-start.7 = (f32[2,64,128]{2,1,0:T(8,128)}, f32[2,64,128]{2,1,0:T(8,128)S(1)}, u32[]{:S(2)}) copy-start(f32[2,64,128]{2,1,0:T(8,128)S(1)} %and_convert_fusion) | copy-start | bytes 196612
  32.5 2.5 %copy-start.2 = (f32[2,8,64,128]{3,2,1,0:T(8,128)S(1)}, f32[2,8,64,128]{3,2,1,0:T(8,128)}, u32[]{:S(2)}) copy-start(f32[2,8,64,128]{3,2,1,0:T(8,128)} %param.13) | copy-start | bytes 1572868
  32.5 2.5 %copy-start.5 = (f32[8,64,128]{2,1,0:T(8,128)S(1)}, f32[8,64,128]{2,1,0:T(8,128)}, u32[]{:S(2)}) copy-start(f32[8,64,128]{2,1,0:T(8,128)} %param.17) | copy-start | bytes 786436
  32.5 2.5 %copy-start.9 = (f32[2,8,64,128]{3,2,1,0:T(8,128)S(1)}, f32[2,8,64,128]{3,2,1,0:T(8,128)}, u32[]{:S(2)}) copy-start(f32[2,8,64,128]{3,2,1,0:T(8,128)} %param.15) | copy-start | bytes 1572868
  32.5 2.5 %copy-start.11 = (f32[2,512,128]{2,1,0:T(8,128)S(1)}, f32[2,512,128]{2,1,0:T(8,128)}, u32[]{:S(2)}) copy-start(f32[2,512,128]{2,1,0:T(8,128)} %fusion.58) | copy-start | bytes 1572868
  36.7 22.3 %collective-permute-start.2 = (f32[2,2,121,128]{3,2,1,0:T(8,128)S(1)}, f32[2,2,121,128]{3,2,1,0:T(8,128)}, u32[]{:S(2)}, u32[]{:S(2)}) collective-permute-start(f32[2,2,121,128]{3,2,1,0:T(8,128)S(1)} %copy.40), channel_id=1, source_target_pairs={{16,0},{32,16},{48,32},{64,48},{80,64},{96,80},{112,96},{128,112},... | collective-permute-start | bytes 743432 | tf_op jit(solution)/shard_map/ppermute | solution.py:68
  53.7 19.6 %collective-permute-start.3 = (f32[2,2,121,128]{3,2,1,0:T(8,128)}, f32[2,2,121,128]{3,2,1,0:T(8,128)}, u32[]{:S(2)}, u32[]{:S(2)}) collective-permute-start(f32[2,2,121,128]{3,2,1,0:T(8,128)} %copy.41), channel_id=1, source_target_pairs={{0,16},{16,32},{32,48},{48,64},{64,80},{80,96},{96,112},{112,128},... | collective-permute-start | bytes 743432 | tf_op jit(solution)/shard_map/ppermute | solution.py:63
  74.6 1.0 copy-start.4
  76.0 2.5 %copy-start.3 = (f32[2,8,64,128]{3,2,1,0:T(8,128)S(1)}, f32[2,8,64,128]{3,2,1,0:T(8,128)}, u32[]{:S(2)}) copy-start(f32[2,8,64,128]{3,2,1,0:T(8,128)} %param.13) | copy-start | bytes 1572868
  76.0 2.5 %copy-start.6 = (f32[8,64,128]{2,1,0:T(8,128)S(1)}, f32[8,64,128]{2,1,0:T(8,128)}, u32[]{:S(2)}) copy-start(f32[8,64,128]{2,1,0:T(8,128)} %param.17) | copy-start | bytes 786436
  76.0 2.5 %copy-start.8 = (f32[2,64,128]{2,1,0:T(8,128)S(1)}, f32[2,64,128]{2,1,0:T(8,128)}, u32[]{:S(2)}) copy-start(f32[2,64,128]{2,1,0:T(8,128)} %copy-done.7) | copy-start | bytes 196612
  76.0 2.5 %copy-start.10 = (f32[2,512,128]{2,1,0:T(8,128)S(1)}, f32[2,512,128]{2,1,0:T(8,128)}, u32[]{:S(2)}) copy-start(f32[2,512,128]{2,1,0:T(8,128)} %fusion.56) | copy-start | bytes 1572868
  76.1 2.5 %copy-start.13 = (f32[2]{0:T(128)S(1)}, f32[2]{0:T(128)}, u32[]{:S(2)}) copy-start(f32[2]{0:T(128)} %get-tuple-element.22) | copy-start | bytes 28

commit v5 on v4

--- a/solution.py
+++ b/solution.py
@@ -167,74 +167,83 @@
     return piece.reshape(shape)
 
 
-def allreduce_kernel(count, local_ref, out_ref, gathered, reduced, spread, send1, recv1, send2, recv2):
+def allreduce_kernel(strides, local_ref, out_ref, *scratch):
+    rounds = len(strides)
+    halves = scratch[:rounds]
+    sums = scratch[rounds : 2 * rounds]
+    send_sems, recv_sems = scratch[2 * rounds], scratch[2 * rounds + 1]
     me = lax.axis_index("shots")
     slab = lax.axis_index("slab")
+    mesh_id = pl.DeviceIdType.MESH
     barrier = pltpu.get_barrier_semaphore()
-    for k in range(1, count):
-        peer = lax.rem(me + k, count)
-        pl.semaphore_signal(
-            barrier, inc=1, device_id=(slab, peer), device_id_type=pl.DeviceIdType.MESH
-        )
-    pl.semaphore_wait(barrier, count - 1)
-    copies = []
-    for k in range(1, count):
-        peer = lax.rem(me + k, count)
+    for stride in strides:
+        partner = me + stride - 2 * stride * ((me // stride) % 2)
+        pl.semaphore_signal(barrier, inc=1, device_id=(slab, partner), device_id_type=mesh_id)
+    pl.semaphore_wait(barrier, rounds)
+    source = local_ref
+    start = 0
+    rows = local_ref.shape[0]
+    for k, stride in enumerate(strides):
+        upper = (me // stride) % 2
+        partner = me + stride - 2 * stride * upper
+        rows //= 2
         copy = pltpu.make_async_remote_copy(
-            src_ref=local_ref.at[peer],
-            dst_ref=gathered.at[k],
-            send_sem=send1.at[k],
-            recv_sem=recv1.at[k],
-            device_id=(slab, peer),
-            device_id_type=pl.DeviceIdType.MESH,
+            src_ref=source.at[pl.ds(pl.multiple_of((1 - upper) * rows, 8), rows)],
+            dst_ref=halves[k],
+            send_sem=send_sems.at[k],
+            recv_sem=recv_sems.at[k],
+            device_id=(slab, partner),
+            device_id_type=mesh_id,
         )
         copy.start()
-        copies.append(copy)
-    for copy in copies:
         copy.wait()
-    total = local_ref[me]
-    for k in range(1, count):
-        total = total + gathered[k]
-    reduced[...] = total
-    copies = []
-    for k in range(1, count):
-        peer = lax.rem(me + k, count)
+        kept = source[pl.ds(pl.multiple_of(upper * rows, 8), rows)]
+        sums[k][...] = kept + halves[k][...]
+        source = sums[k]
+        start = start + upper * rows
+    out_ref[pl.ds(pl.multiple_of(start, 8), rows)] = sums[rounds - 1][...]
+    for k in reversed(range(rounds)):
+        stride = strides[k]
+        upper = (me // stride) % 2
+        partner = me + stride - 2 * stride * upper
+        mine = out_ref.at[pl.ds(pl.multiple_of(start, 8), rows)]
         copy = pltpu.make_async_remote_copy(
-            src_ref=reduced,
-            dst_ref=spread.at[k],
-            send_sem=send2.at[k],
-            recv_sem=recv2.at[k],
-            device_id=(slab, peer),
-            device_id_type=pl.DeviceIdType.MESH,
+            src_ref=mine,
+            dst_ref=mine,
+            send_sem=send_sems.at[rounds + k],
+            recv_sem=recv_sems.at[rounds + k],
+            device_id=(slab, partner),
+            device_id_type=mesh_id,
         )
         copy.start()
-        copies.append(copy)
-    out_ref[me] = total
-    for copy in copies:
         copy.wait()
-    for k in range(1, count):
-        out_ref[lax.rem(me + count - k, count)] = spread[k]
+        start = start - upper * rows
+        rows *= 2
 
 
 def shots_sum(value):
     count = lax.axis_size("shots")
+    strides = []
+    stride = 1
+    while stride < count:
+        strides.append(stride)
+        stride *= 2
     shape = value.shape
-    chunks = value.reshape(count, -1, 128)
-    rows = chunks.shape[1]
+    chunks = value.reshape(-1, 128)
+    rows = chunks.shape[0]
+    scratch = []
+    for k in range(len(strides)):
+        scratch.append(pltpu.VMEM((rows >> (k + 1), 128), jnp.float32))
+    for k in range(len(strides)):
+        scratch.append(pltpu.VMEM((rows >> (k + 1), 128), jnp.float32))
+    scratch.append(pltpu.SemaphoreType.DMA((2 * len(strides),)))
+    scratch.append(pltpu.SemaphoreType.DMA((2 * len(strides),)))
     out = pl.pallas_call(
-        functools.partial(allreduce_kernel, count),
+        functools.partial(allreduce_kernel, tuple(strides)),
         out_shape=jax.ShapeDtypeStruct(chunks.shape, jnp.float32),
         in_specs=[pl.BlockSpec(memory_space=pltpu.VMEM)],
         out_specs=pl.BlockSpec(memory_space=pltpu.VMEM),
-        scratch_shapes=[
-            pltpu.VMEM((count, rows, 128), jnp.float32),
-            pltpu.VMEM((rows, 128), jnp.float32),
-            pltpu.VMEM((count, rows, 128), jnp.float32),
-            pltpu.SemaphoreType.DMA((count,)),
-            pltpu.SemaphoreType.DMA((count,)),
-            pltpu.SemaphoreType.DMA((count,)),
-            pltpu.SemaphoreType.DMA((count,)),
-        ],
+        scratch_shapes=scratch,
         compiler_params=pltpu.CompilerParams(collective_id=0, has_side_effects=True),
     )(chunks)
     return out.reshape(shape)

time: 150 us -> 145 us (0.967)
  Pallas kernels: 65.5 us -> 59.3 us
    pallas_call x1, Pallas kernels: 65.5 us -> 59.3 us  [shots_sum(): pl.pallas_call(functools.partial(allreduce_kernel, tuple(strides)), out_s...]
where the time goes in v5:
time: 145 us; the launch traced here: 142 us
  Pallas kernels  59.3 us (41%)
  starting transfers between devices  37.1 us (26%)
  waiting for transfers between devices  14.5 us (10%)
  other arithmetic  12 us (8%)
  matrix products  10.6 us (7%)
  local copies, waits for them, and re-layouts  7.29 us (5%)
    pallas_call x1, Pallas kernels, shots_sum(): pl.pallas_call(functools.partial(allreduce_kernel, tuple(strides)), out_s...  59.3 us
    ppermute x2, starting transfers between devices, extended(): lax.ppermute(cut_windows(lax.slice_in_dim(block, 0, width, axis=dim), pic...  31.9 us
    ppermute x2, waiting for transfers between devices, extended(): lax.ppermute(cut_windows(lax.slice_in_dim(block, block.shape[dim] - width...  11.4 us
    dot_general x16, matrix products, exact_einsum(): jnp.einsum(spec, a, b, precision=lax.Precision.HIGHEST, preferred_element...  7.45 us
    ppermute x2, starting transfers between devices, extended(): lax.ppermute(cut_windows(lax.slice_in_dim(block, block.shape[dim] - width...  5.22 us
    add x2, other arithmetic, laplace(): total = total + COEF[shift_k] * (side_y + side_x)  4.91 us
    reshape x4, local copies, waits for them, and re-layouts, paste_windows(): part = flat.reshape(fields, shots, width, WIN_Y, WIN_X)  3.13 us
    dot_general x2, matrix products, receiver_field(): jnp.einsum('szr,srx->szx', left, right, precision=lax.Precision.HIGHEST,...  3.11 us
  transfers between devices with their start and end apart: 4, of which 2 were waited for; matrix products, arithmetic and copies ran while one was open for 8% of the time, Pallas kernels for 0%

profile of v5, /device:TPU:25, one launch (start us, length us, event | category | flops | bytes accessed | tf_op | source)
XLA Modules:
  0.0 142.0 jit_solution(17711515109653665355)
XLA Ops:
  0.6 0.7 subtract_clamp_fusion.1
  1.4 0.7 subtract_clamp_fusion
  2.1 1.3 fusion.66
  3.4 0.4 convolution_bitcast_fusion.5
  4.5 3.1 %collective-permute-start.1 = (f32[2,2,121,128]{3,2,1,0:T(8,128)S(1)}, f32[2,2,121,128]{3,2,1,0:T(8,128)S(1)}, u32[]{:S(2)}, u32[]{:S(2)}) collective-permute-start(f32[2,2,121,128]{3,2,1,0:T(8,128)S(1)} %copy.39), channel_id=1, source_target_pairs={{0,16},{16,32},{32,48},{48,64},{64,80},{80,96},{96,112},{112,128},... | collective-permute-start | bytes 743432 | tf_op jit(solution)/shard_map/ppermute | solution.py:63
  7.7 0.4 convolution_bitcast_fusion.7
  8.8 16.6 %collective-permute-start = (f32[2,2,121,128]{3,2,1,0:T(8,128)S(1)}, f32[2,2,121,128]{3,2,1,0:T(8,128)S(1)}, u32[]{:S(2)}, u32[]{:S(2)}) collective-permute-start(f32[2,2,121,128]{3,2,1,0:T(8,128)S(1)} %copy.38), channel_id=1, source_target_pairs={{16,0},{32,16},{48,32},{64,48},{80,64},{96,80},{112,96},{128,112},... | collective-permute-start | bytes 743432 | tf_op jit(solution)/shard_map/ppermute | solution.py:68
  25.7 0.6 slice_bitcast_fusion.6
  26.5 1.6 %fusion.58 = f32[2,512,128]{2,1,0:T(8,128)} fusion(f32[2,256]{1,0:T(2,128)S(1)} %get-tuple-element.21, s32[2,256]{1,0:T(2,128)S(1)} %multiply_add_fusion, s32[2,256]{1,0:T(2,128)S(1)} %get-tuple-element.7), kind=kOutput, calls=%fused_computation.128 | convolution fusion | flops 403243008 | bytes 530432 | tf_op jit(solution)/shard_map/szr,srx->szx/dot_general | solution.py:135
  28.2 1.6 %fusion.56 = f32[2,512,128]{2,1,0:T(8,128)} fusion(f32[2,256]{1,0:T(2,128)S(1)} %get-tuple-element.20, s32[2,256]{1,0:T(2,128)S(1)} %multiply_add_fusion, s32[2,256]{1,0:T(2,128)S(1)} %get-tuple-element.7), kind=kOutput, calls=%fused_computation.126 | convolution fusion | flops 403243008 | bytes 530432 | tf_op jit(solution)/shard_map/szr,srx->szx/dot_general | solution.py:135
  30.0 0.4 convolution_bitcast_fusion.12
  30.4 0.5 convolution_bitcast_fusion.4
  31.2 0.4 convolution_bitcast_fusion.14
  31.6 0.5 convolution_bitcast_fusion.6
  32.6 2.5 %fusion.6 = f32[2,2,8,64,128]{4,3,2,1,0:T(8,128)S(1)} fusion(f32[2,2,8,64,128]{4,3,2,1,0:T(8,128)S(1)} %pad_maximum_fusion.2, f32[2,2,12,64,128]{4,3,2,1,0:T(8,128)S(1)} %get-tuple-element.17, f32[2,2,12,64,128]{4,3,2,1,0:T(8,128)S(1)} %get-tuple-element.16), kind=kLoop, calls=%fused_computation.68 | loop fusion | flops 8650752 | bytes 10485760 | tf_op jit(solution)/shard_map/add | solution.py:98
  35.1 0.5 fusion.77
  35.6 0.4 convolution_bitcast_fusion.3
  36.7 15.3 %collective-permute-start.2 = (f32[2,2,121,128]{3,2,1,0:T(8,128)S(1)}, f32[2,2,121,128]{3,2,1,0:T(8,128)}, u32[]{:S(2)}, u32[]{:S(2)}) collective-permute-start(f32[2,2,121,128]{3,2,1,0:T(8,128)S(1)} %copy.40), channel_id=1, source_target_pairs={{16,0},{32,16},{48,32},{64,48},{80,64},{96,80},{112,96},{128,112},... | collective-permute-start | bytes 743432 | tf_op jit(solution)/shard_map/ppermute | solution.py:68
  52.0 0.4 convolution_bitcast_fusion.1
  53.0 0.7 copy.41
  53.7 2.1 %collective-permute-start.3 = (f32[2,2,121,128]{3,2,1,0:T(8,128)}, f32[2,2,121,128]{3,2,1,0:T(8,128)}, u32[]{:S(2)}, u32[]{:S(2)}) collective-permute-start(f32[2,2,121,128]{3,2,1,0:T(8,128)} %copy.41), channel_id=1, source_target_pairs={{0,16},{16,32},{32,48},{48,64},{64,80},{80,96},{96,112},{112,128},... | collective-permute-start | bytes 743432 | tf_op jit(solution)/shard_map/ppermute | solution.py:63
  55.9 3.1 %collective-permute-done.2 = f32[2,2,121,128]{3,2,1,0:T(8,128)} collective-permute-done((f32[2,2,121,128]{3,2,1,0:T(8,128)S(1)}, f32[2,2,121,128]{3,2,1,0:T(8,128)}, u32[]{:S(2)}, u32[]{:S(2)}) %collective-permute-start.2) | collective-permute-done | bytes 247840 | tf_op jit(solution)/shard_map/ppermute | solution.py:68
  59.0 1.3 reshape.264
  60.7 1.3 convolution_bitcast_fusion.2
  61.9 11.4 %collective-permute-done.3 = f32[2,2,121,128]{3,2,1,0:T(8,128)} collective-permute-done((f32[2,2,121,128]{3,2,1,0:T(8,128)}, f32[2,2,121,128]{3,2,1,0:T(8,128)}, u32[]{:S(2)}, u32[]{:S(2)}) %collective-permute-start.3) | collective-permute-done | bytes 247840 | tf_op jit(solution)/shard_map/ppermute | solution.py:63
  73.3 1.3 reshape.266
  75.0 0.5 convolution_bitcast_fusion
  76.1 2.5 %fusion.26 = f32[2,2,8,64,128]{4,3,2,1,0:T(8,128)S(1)} fusion(f32[2,2,8,64,128]{4,3,2,1,0:T(8,128)S(1)} %pad_maximum_fusion.3, f32[2,2,12,64,128]{4,3,2,1,0:T(8,128)S(1)} %get-tuple-element.13, f32[2,2,12,64,128]{4,3,2,1,0:T(8,128)S(1)} %get-tuple-element.12), kind=kLoop, calls=%fused_computation.88 | loop fusion | flops 8650752 | bytes 10485760 | tf_op jit(solution)/shard_map/add | solution.py:98
  78.6 1.6 %multiply_reduce_fusion = (f32[8,64,128]{2,1,0:T(8,128)S(1)}, f32[8,64,128]{2,1,0:T(8,128)S(1)}, f32[2,8,64,128]{3,2,1,0:T(8,128)}, f32[2,8,64,128]{3,2,1,0:T(8,128)}) fusion(f32[2,8,64,128]{3,2,1,0:T(8,128)S(1)} %copy-done, f32[2,8,64,128]{3,2,1,0:T(8,128)S(1)} %get-tuple-element.11, f32[2,8,64,128]{3,2,1,0:T(8,128)S(1)} %get-tuple-element.10, ...), kind=kLoop, calls=%fused_computation.161 | loop fusion | flops 2883584 | bytes 6096136 | tf_op jit(solution)/shard_map/reduce_sum | solution.py:284
  80.2 0.7 add.292
  81.0 59.3 %shard_map.148 = f32[512,128]{1,0:T(8,128)} custom-call(f32[512,128]{1,0:T(8,128)} %bitcast.138), custom_call_target="tpu_custom_call" | custom-call | tf_op jit(solution)/shard_map/pallas_call | solution.py:241
  140.3 1.7 %copy.67 = f32[8,64,128]{2,1,0:T(8,128)} copy(f32[8,64,128]{2,1,0:T(8,128)} %bitcast.139) | data formatting | bytes 524288
  (75 shorter events, 5.6 us)
Async XLA Ops:
  4.5 25.3 %collective-permute-start.1 = (f32[2,2,121,128]{3,2,1,0:T(8,128)S(1)}, f32[2,2,121,128]{3,2,1,0:T(8,128)S(1)}, u32[]{:S(2)}, u32[]{:S(2)}) collective-permute-start(f32[2,2,121,128]{3,2,1,0:T(8,128)S(1)} %copy.39), channel_id=1, source_target_pairs={{0,16},{16,32},{32,48},{48,64},{64,80},{80,96},{96,112},{112,128},... | collective-permute-start | bytes 743432 | tf_op jit(solution)/shard_map/ppermute | solution.py:63
  7.6 17.8 %copy-start.16 = (s32[2]{0:T(128)S(1)}, s32[2]{0:T(128)}, u32[]{:S(2)}) copy-start(s32[2]{0:T(128)} %param.21) | copy-start | bytes 28
  7.6 17.8 %copy-start.17 = (s32[2]{0:T(128)S(1)}, s32[2]{0:T(128)}, u32[]{:S(2)}) copy-start(s32[2]{0:T(128)} %param.23) | copy-start | bytes 28
  7.6 17.9 %copy-start.18 = (s32[2]{0:T(128)S(1)}, s32[2]{0:T(128)}, u32[]{:S(2)}) copy-start(s32[2]{0:T(128)} %param.22) | copy-start | bytes 28
  7.6 17.9 %copy-start.19 = (s32[2]{0:T(128)S(1)}, s32[2]{0:T(128)}, u32[]{:S(2)}) copy-start(s32[2]{0:T(128)} %param.24) | copy-start | bytes 28
  7.7 17.9 %copy-start.14 = (s32[2,256]{1,0:T(2,128)S(1)}, s32[2,256]{1,0:T(2,128)}, u32[]{:S(2)}) copy-start(s32[2,256]{1,0:T(2,128)} %param.25) | copy-start | bytes 6148
  7.7 18.0 %copy-start.12 = (f32[2,2,256]{2,1,0:T(2,128)S(1)}, f32[2,2,256]{2,1,0:T(2,128)}, u32[]{:S(2)}) copy-start(f32[2,2,256]{2,1,0:T(2,128)} %param.19) | copy-start | bytes 12292
  7.7 18.0 %copy-start.20 = (s32[2]{0:T(128)S(1)}, s32[2]{0:T(128)}, u32[]{:S(2)}) copy-start(s32[2]{0:T(128)} %param.20) | copy-start | bytes 28
  7.7 18.0 %copy-start.15 = (f32[2,2]{1,0:T(2,128)S(1)}, f32[2,2]{1,0:T(2,128)}, u32[]{:S(2)}) copy-start(f32[2,2]{1,0:T(2,128)} %param.18) | copy-start | bytes 52
  8.1 19.9 %copy-start = (f32[2,8,64,128]{3,2,1,0:T(8,128)S(1)}, f32[2,8,64,128]{3,2,1,0:T(8,128)}, u32[]{:S(2)}) copy-start(f32[2,8,64,128]{3,2,1,0:T(8,128)} %param.14) | copy-start | bytes 1572868
  8.2 19.9 %copy-start.1 = (f32[2,8,64,128]{3,2,1,0:T(8,128)S(1)}, f32[2,8,64,128]{3,2,1,0:T(8,128)}, u32[]{:S(2)}) copy-start(f32[2,8,64,128]{3,2,1,0:T(8,128)} %param.16) | copy-start | bytes 1572868
  8.8 22.1 %collective-permute-start = (f32[2,2,121,128]{3,2,1,0:T(8,128)S(1)}, f32[2,2,121,128]{3,2,1,0:T(8,128)S(1)}, u32[]{:S(2)}, u32[]{:S(2)}) collective-permute-start(f32[2,2,121,128]{3,2,1,0:T(8,128)S(1)} %copy.38), channel_id=1, source_target_pairs={{16,0},{32,16},{48,32},{64,48},{80,64},{96,80},{112,96},{128,112},... | collective-permute-start | bytes 743432 | tf_op jit(solution)/shard_map/ppermute | solution.py:68
  26.4 8.6 %copy-start.7 = (f32[2,64,128]{2,1,0:T(8,128)}, f32[2,64,128]{2,1,0:T(8,128)S(1)}, u32[]{:S(2)}) copy-start(f32[2,64,128]{2,1,0:T(8,128)S(1)} %and_convert_fusion) | copy-start | bytes 196612
  32.5 2.5 %copy-start.2 = (f32[2,8,64,128]{3,2,1,0:T(8,128)S(1)}, f32[2,8,64,128]{3,2,1,0:T(8,128)}, u32[]{:S(2)}) copy-start(f32[2,8,64,128]{3,2,1,0:T(8,128)} %param.13) | copy-start | bytes 1572868
  32.5 2.5 %copy-start.5 = (f32[8,64,128]{2,1,0:T(8,128)S(1)}, f32[8,64,128]{2,1,0:T(8,128)}, u32[]{:S(2)}) copy-start(f32[8,64,128]{2,1,0:T(8,128)} %param.17) | copy-start | bytes 786436
  32.5 2.5 %copy-start.9 = (f32[2,8,64,128]{3,2,1,0:T(8,128)S(1)}, f32[2,8,64,128]{3,2,1,0:T(8,128)}, u32[]{:S(2)}) copy-start(f32[2,8,64,128]{3,2,1,0:T(8,128)} %param.15) | copy-start | bytes 1572868
  32.5 2.5 %copy-start.11 = (f32[2,512,128]{2,1,0:T(8,128)S(1)}, f32[2,512,128]{2,1,0:T(8,128)}, u32[]{:S(2)}) copy-start(f32[2,512,128]{2,1,0:T(8,128)} %fusion.58) | copy-start | bytes 1572868
  36.7 22.3 %collective-permute-start.2 = (f32[2,2,121,128]{3,2,1,0:T(8,128)S(1)}, f32[2,2,121,128]{3,2,1,0:T(8,128)}, u32[]{:S(2)}, u32[]{:S(2)}) collective-permute-start(f32[2,2,121,128]{3,2,1,0:T(8,128)S(1)} %copy.40), channel_id=1, source_target_pairs={{16,0},{32,16},{48,32},{64,48},{80,64},{96,80},{112,96},{128,112},... | collective-permute-start | bytes 743432 | tf_op jit(solution)/shard_map/ppermute | solution.py:68
  53.7 19.6 %collective-permute-start.3 = (f32[2,2,121,128]{3,2,1,0:T(8,128)}, f32[2,2,121,128]{3,2,1,0:T(8,128)}, u32[]{:S(2)}, u32[]{:S(2)}) collective-permute-start(f32[2,2,121,128]{3,2,1,0:T(8,128)} %copy.41), channel_id=1, source_target_pairs={{0,16},{16,32},{32,48},{48,64},{64,80},{80,96},{96,112},{112,128},... | collective-permute-start | bytes 743432 | tf_op jit(solution)/shard_map/ppermute | solution.py:63
  74.6 1.0 copy-start.4
  76.0 2.5 %copy-start.3 = (f32[2,8,64,128]{3,2,1,0:T(8,128)S(1)}, f32[2,8,64,128]{3,2,1,0:T(8,128)}, u32[]{:S(2)}) copy-start(f32[2,8,64,128]{3,2,1,0:T(8,128)} %param.13) | copy-start | bytes 1572868
  76.0 2.5 %copy-start.6 = (f32[8,64,128]{2,1,0:T(8,128)S(1)}, f32[8,64,128]{2,1,0:T(8,128)}, u32[]{:S(2)}) copy-start(f32[8,64,128]{2,1,0:T(8,128)} %param.17) | copy-start | bytes 786436
  76.0 2.5 %copy-start.8 = (f32[2,64,128]{2,1,0:T(8,128)S(1)}, f32[2,64,128]{2,1,0:T(8,128)}, u32[]{:S(2)}) copy-start(f32[2,64,128]{2,1,0:T(8,128)} %copy-done.7) | copy-start | bytes 196612
  76.0 2.5 %copy-start.10 = (f32[2,512,128]{2,1,0:T(8,128)S(1)}, f32[2,512,128]{2,1,0:T(8,128)}, u32[]{:S(2)}) copy-start(f32[2,512,128]{2,1,0:T(8,128)} %fusion.56) | copy-start | bytes 1572868
  76.1 2.5 %copy-start.13 = (f32[2]{0:T(128)S(1)}, f32[2]{0:T(128)}, u32[]{:S(2)}) copy-start(f32[2]{0:T(128)} %get-tuple-element.22) | copy-start | bytes 28

commit v6 on v5

--- a/solution.py
+++ b/solution.py
@@ -54,20 +54,141 @@
     return exact_einsum("sya,fsjax->fsjyx", pick_y, part)
 
 
-def extended(block, pick_y, pick_x, width):
-    count = lax.axis_size("slab")
-    forward = [(i, i + 1) for i in range(count - 1)]
-    backward = [(target, source) for source, target in forward]
+def halo_kernel(n, lo_send, hi_send, lo_recv, hi_recv, relay_f, relay_b, sems):
+    i = lax.axis_index("slab")
+    shot = lax.axis_index("shots")
+    x = i % 4
+    part = lo_send.shape[0] // 3
+    mesh_id = pl.DeviceIdType.MESH
+    barrier = pltpu.get_barrier_semaphore()
+    greeted = 0
+    for d in (-3, -2, -1, 1, 2, 3):
+        ok = (i + d >= 0) & (i + d < n)
+
+        @pl.when(ok)
+        def _():
+            pl.semaphore_signal(barrier, inc=1, device_id=(i + d, shot), device_id_type=mesh_id)
+
+        greeted = greeted + ok.astype(jnp.int32)
+    pl.semaphore_wait(barrier, greeted)
+
+    def rows(p):
+        return pl.ds(p * part, part)
+
+    def remote(src, dst, send, recv, target):
+        return pltpu.make_async_remote_copy(
+            src_ref=src,
+            dst_ref=dst,
+            send_sem=sems.at[send],
+            recv_sem=sems.at[recv],
+            device_id=(target, shot),
+            device_id_type=mesh_id,
+        )
+
+    has_up = i + 1 < n
+    has_down = i >= 1
+    up_far = x == 3
+    down_far = x == 0
+    for p in range(3):
+        direct_up = has_up if p == 0 else has_up & jnp.logical_not(up_far)
+
+        @pl.when(direct_up)
+        def _():
+            remote(lo_send.at[rows(p)], lo_recv.at[rows(p)], p, 8 + p, i + 1).start()
+
+        direct_down = has_down if p == 0 else has_down & jnp.logical_not(down_far)
+
+        @pl.when(direct_down)
+        def _():
+            remote(hi_send.at[rows(p)], hi_recv.at[rows(p)], 3 + p, 11 + p, i - 1).start()
+
+        if p > 0:
+
+            @pl.when(has_up & up_far)
+            def _():
+                remote(lo_send.at[rows(p)], relay_f, p, 14, i + 1 + p).start()
+
+            @pl.when(has_down & down_far)
+            def _():
+                remote(hi_send.at[rows(p)], relay_b, 3 + p, 15, i - 4 + p).start()
+
+    for p in (1, 2):
+        fwd = (x == p) & (i - 1 - p >= 0)
+
+        @pl.when(fwd)
+        def _():
+            remote(lo_send.at[rows(p)], relay_f, p, 14, i).wait_recv()
+            copy = remote(relay_f, lo_recv.at[rows(p)], 6, 8 + p, i - p)
+            copy.start()
+            copy.wait_send()
+
+        bwd = (x == p) & (i + 4 - p < n)
+
+        @pl.when(bwd)
+        def _():
+            remote(hi_send.at[rows(p)], relay_b, 3 + p, 15, i).wait_recv()
+            copy = remote(relay_b, hi_recv.at[rows(p)], 7, 11 + p, i + 3 - p)
+            copy.start()
+            copy.wait_send()
+
+    for p in range(3):
+
+        @pl.when(has_up)
+        def _():
+            remote(lo_send.at[rows(p)], lo_recv.at[rows(p)], p, 8 + p, i + 1).wait_send()
+
+        @pl.when(has_down)
+        def _():
+            remote(hi_send.at[rows(p)], hi_recv.at[rows(p)], 3 + p, 11 + p, i - 1).wait_send()
+
+        @pl.when(has_down)
+        def _():
+            remote(lo_send.at[rows(p)], lo_recv.at[rows(p)], p, 8 + p, i).wait_recv()
+
+        @pl.when(has_up)
+        def _():
+            remote(hi_send.at[rows(p)], hi_recv.at[rows(p)], 3 + p, 11 + p, i).wait_recv()
+
+
+def exchange(lo_flat, hi_flat, call_id):
+    n = lax.axis_size("slab")
+    shape = lo_flat.shape
+    total = lo_flat.size // 128
+    part = -(-total // 24) * 8
+    padded = 3 * part
+
+    def prep(a):
+        return jnp.pad(a.reshape(total, 128), ((0, padded - total), (0, 0)))
+
+    vmem = pl.BlockSpec(memory_space=pltpu.VMEM)
+    lo_recv, hi_recv = pl.pallas_call(
+        functools.partial(halo_kernel, n),
+        out_shape=(
+            jax.ShapeDtypeStruct((padded, 128), jnp.float32),
+            jax.ShapeDtypeStruct((padded, 128), jnp.float32),
+        ),
+        in_specs=[vmem, vmem],
+        out_specs=(vmem, vmem),
+        scratch_shapes=[
+            pltpu.VMEM((part, 128), jnp.float32),
+            pltpu.VMEM((part, 128), jnp.float32),
+            pltpu.SemaphoreType.DMA((16,)),
+        ],
+        compiler_params=pltpu.CompilerParams(collective_id=call_id, has_side_effects=True),
+    )(prep(lo_flat), prep(hi_flat))
+    return lo_recv[:total].reshape(shape), hi_recv[:total].reshape(shape)
+
+
+def extended(block, pick_y, pick_x, width, call_id):
     dim = 2
-    rows_y, cols_x = block.shape[-2:]
-    low = lax.ppermute(
-        cut_windows(lax.slice_in_dim(block, block.shape[dim] - width, None, axis=dim), pick_y, pick_x),
-        "slab",
-        forward,
-    )
-    high = lax.ppermute(
-        cut_windows(lax.slice_in_dim(block, 0, width, axis=dim), pick_y, pick_x), "slab", backward
-    )
+    lo_flat = cut_windows(
+        lax.slice_in_dim(block, block.shape[dim] - width, None, axis=dim), pick_y, pick_x
+    )
+    hi_flat = cut_windows(lax.slice_in_dim(block, 0, width, axis=dim), pick_y, pick_x)
+    low, high = exchange(lo_flat, hi_flat, call_id)
+    i = lax.axis_index("slab")
+    low = jnp.where(i >= 1, low, 0.0)
+    high = jnp.where(i + 1 < lax.axis_size("slab"), high, 0.0)
     low = paste_windows(low, pick_y, pick_x, width)
     high = paste_windows(high, pick_y, pick_x, width)
     return jnp.concatenate([low, block, high], axis=dim)
@@ -273,7 +394,7 @@
     up, u, vp, v = (src_prev, src_cur, rcv_prev, rcv_cur)
     for step in range(STEPS):
         stacked = jnp.stack([u, v])
-        padded = extended(stacked, pick_y, pick_x, 4)
+        padded = extended(stacked, pick_y, pick_x, 4, 1 + step)
         lap = laplace(padded)
         sdelta = point_field(
             source_depth - start, source_y, source_x, wavelet[step], depth, rows_y, cols_x

time: 145 us -> 146 us (level); the launches traced: 142 us -> 145 us
  Pallas kernels: 59.3 us -> 113 us
  starting transfers between devices: 37.1 us -> 0 us
  waiting for transfers between devices: 14.5 us -> 0 us
  other arithmetic: 12 us -> 14.7 us
  matrix products: 10.6 us -> 8.19 us
    pallas_call x0 -> x2, Pallas kernels: none -> 53.1 us  [exchange(): pl.pallas_call(functools.partial(halo_kernel, n), out_shape=(jax.ShapeDty...]
    ppermute x4 -> x0, starting transfers between devices: 37.1 us -> none  [the longest x2 31.9 us: extended(): lax.ppermute(cut_windows(lax.slice_in_dim(block, 0, width, axis=dim), pic...]
    ppermute x4 -> x0, waiting for transfers between devices: 14.5 us -> none  [the longest x2 11.4 us: extended(): lax.ppermute(cut_windows(lax.slice_in_dim(block, block.shape[dim] - width...]
    reshape x12 -> x0, local copies, waits for them, and re-layouts: 4.76 us -> none  [the longest x4 3.13 us: paste_windows(): part = flat.reshape(fields, shots, width, WIN_Y, WIN_X)]
    pad x0 -> x4, local copies, waits for them, and re-layouts: none -> 2.87 us  [prep(): return jnp.pad(a.reshape(total, 128), ((0, padded - total), (0, 0)))]
    select_n x0 -> x3, other arithmetic: none -> 2.13 us  [the longest x2 1.12 us: extended(): low = jnp.where(i >= 1, low, 0.0)]
    dot_general x2, matrix products: 3.11 us -> 1.52 us  [receiver_field(): jnp.einsum('szr,srx->szx', left, right, precision=lax.Precision.HIGHEST,...]
  transfers between devices with their start and end apart: 4 -> 0, of which waited for: 2 -> 0; matrix products, arithmetic and copies ran while one was open for 8% -> 0% of each run, Pallas kernels for 0% -> 0%
where the time goes in v6:
time: 146 us; the launch traced here: 145 us
  Pallas kernels  113 us (77%)
  other arithmetic  14.7 us (10%)
  matrix products  8.19 us (6%)
  local copies, waits for them, and re-layouts  7.38 us (5%)
    pallas_call x1, Pallas kernels, shots_sum(): pl.pallas_call(functools.partial(allreduce_kernel, tuple(strides)), out_s...  60.3 us
    pallas_call x2, Pallas kernels, exchange(): pl.pallas_call(functools.partial(halo_kernel, n), out_shape=(jax.ShapeDty...  53.1 us
    dot_general x16, matrix products, exact_einsum(): jnp.einsum(spec, a, b, precision=lax.Precision.HIGHEST, preferred_element...  6.67 us
    add x2, other arithmetic, laplace(): total = total + COEF[shift_k] * (side_y + side_x)  4.91 us

profile of v6, /device:TPU:25, one launch (start us, length us, event | category | flops | bytes accessed | tf_op | source)
XLA Modules:
  0.0 144.8 jit_solution(13787630538062994845)
XLA Ops:
  0.6 0.7 subtract_clamp_fusion.1
  1.4 1.3 fusion.67
  2.7 0.4 convolution_bitcast_fusion.7
  3.9 0.7 pad.20.lo_send
  4.6 0.4 convolution_bitcast_fusion.6
  5.7 0.7 pad.21.hi_send
  6.4 28.5 %shard_map.148 = (f32[504,128]{1,0:T(8,128)}, f32[504,128]{1,0:T(8,128)}) custom-call(f32[504,128]{1,0:T(8,128)} %pad.20.lo_send, f32[504,128]{1,0:T(8,128)} %pad.21.hi_send), custom_call_target="tpu_custom_call" | custom-call | tf_op jit(solution)/shard_map/pallas_call | solution.py:164
  34.9 1.1 slice_select_fusion.2
  36.3 0.4 convolution_bitcast_fusion.13
  36.7 0.5 convolution_bitcast_fusion.5
  37.9 0.5 convolution_bitcast_fusion.4
  38.4 0.4 pad_maximum_fusion
  39.0 2.5 %fusion.6 = f32[2,2,8,64,128]{4,3,2,1,0:T(8,128)S(1)} fusion(f32[2,2,8,64,128]{4,3,2,1,0:T(8,128)S(1)} %pad_maximum_fusion.2, f32[2,2,12,64,128]{4,3,2,1,0:T(8,128)S(1)} %get-tuple-element.25, f32[2,2,12,64,128]{4,3,2,1,0:T(8,128)S(1)} %get-tuple-element.24), kind=kLoop, calls=%fused_computation.68 | loop fusion | flops 8650752 | bytes 10485760 | tf_op jit(solution)/shard_map/add | solution.py:219
  41.5 0.6 slice_bitcast_fusion.4
  42.1 0.8 fusion.58
  43.3 1.7 %fusion.77 = (f32[2,8,64,128]{3,2,1,0:T(8,128)S(1)}, f32[2,8,64,128]{3,2,1,0:T(8,128)S(1)}) fusion(f32[2,8,64,128]{3,2,1,0:T(8,128)S(1)} %bitcast.132, f32[2,2,8,64,128]{4,3,2,1,0:T(8,128)S(1)} %fusion.6, f32[2,8,64,128]{3,2,1,0:T(8,128)} %param.15, f32[2,8,64,128]{3,2,1,0:T(8,128)S(1)} %copy-done.1, f32[8,64,128]{2,1,0:T(8,128)S(1)} %copy-done.3, ...), kind=kLoop, calls=%fused_computation.153 | loop fusion | flops 1835008 | bytes 5047560 | tf_op jit(solution)/shard_map/mul | solution.py:404
  45.1 0.4 convolution_bitcast_fusion.2
  46.2 0.7 pad.24.hi_send
  46.9 0.4 convolution_bitcast_fusion.3
  47.9 0.7 pad.23.lo_send
  48.7 24.6 %shard_map.149 = (f32[504,128]{1,0:T(8,128)}, f32[504,128]{1,0:T(8,128)}) custom-call(f32[504,128]{1,0:T(8,128)} %pad.23.lo_send, f32[504,128]{1,0:T(8,128)} %pad.24.hi_send), custom_call_target="tpu_custom_call" | custom-call | tf_op jit(solution)/shard_map/pallas_call | solution.py:164
  73.3 1.0 slice_select_fusion.1
  74.6 0.4 convolution_bitcast_fusion.9
  75.0 0.5 convolution_bitcast_fusion.1
  75.8 0.4 convolution_bitcast_fusion.8
  76.2 0.5 convolution_bitcast_fusion
  77.2 2.5 %fusion.26 = f32[2,2,8,64,128]{4,3,2,1,0:T(8,128)S(1)} fusion(f32[2,2,8,64,128]{4,3,2,1,0:T(8,128)S(1)} %pad_maximum_fusion.3, f32[2,2,12,64,128]{4,3,2,1,0:T(8,128)S(1)} %get-tuple-element.21, f32[2,2,12,64,128]{4,3,2,1,0:T(8,128)S(1)} %get-tuple-element.20), kind=kLoop, calls=%fused_computation.88 | loop fusion | flops 8650752 | bytes 10485760 | tf_op jit(solution)/shard_map/add | solution.py:219
  79.7 0.8 fusion.56
  80.5 1.7 %multiply_reduce_fusion = (f32[8,64,128]{2,1,0:T(8,128)S(1)}, f32[8,64,128]{2,1,0:T(8,128)S(1)}, f32[2,8,64,128]{3,2,1,0:T(8,128)}, f32[2,8,64,128]{3,2,1,0:T(8,128)}) fusion(f32[2,8,64,128]{3,2,1,0:T(8,128)S(1)} %copy-done, f32[2,8,64,128]{3,2,1,0:T(8,128)S(1)} %get-tuple-element.19, f32[2,8,64,128]{3,2,1,0:T(8,128)S(1)} %get-tuple-element.18, ...), kind=kLoop, calls=%fused_computation.161 | loop fusion | flops 2883584 | bytes 6096136 | tf_op jit(solution)/shard_map/reduce_sum | solution.py:405
  82.1 0.7 add.305
  82.9 60.3 %shard_map.150 = f32[512,128]{1,0:T(8,128)} custom-call(f32[512,128]{1,0:T(8,128)} %bitcast.130), custom_call_target="tpu_custom_call" | custom-call | tf_op jit(solution)/shard_map/pallas_call | solution.py:362
  143.1 1.7 %copy.67 = f32[8,64,128]{2,1,0:T(8,128)} copy(f32[8,64,128]{2,1,0:T(8,128)} %bitcast.131) | data formatting | bytes 524288
  (66 shorter events, 5.3 us)
Async XLA Ops:
  1.4 1.8 %copy-start.11 = (s32[2]{0:T(128)S(1)}, s32[2]{0:T(128)}, u32[]{:S(2)}) copy-start(s32[2]{0:T(128)} %param.21) | copy-start | bytes 28
  1.4 1.8 %copy-start.12 = (s32[2]{0:T(128)S(1)}, s32[2]{0:T(128)}, u32[]{:S(2)}) copy-start(s32[2]{0:T(128)} %param.23) | copy-start | bytes 28
  36.7 1.7 %copy-start = (f32[2,8,64,128]{3,2,1,0:T(8,128)S(1)}, f32[2,8,64,128]{3,2,1,0:T(8,128)}, u32[]{:S(2)}) copy-start(f32[2,8,64,128]{3,2,1,0:T(8,128)} %param.14) | copy-start | bytes 1572868
  36.7 1.7 %copy-start.1 = (f32[2,8,64,128]{3,2,1,0:T(8,128)S(1)}, f32[2,8,64,128]{3,2,1,0:T(8,128)}, u32[]{:S(2)}) copy-start(f32[2,8,64,128]{3,2,1,0:T(8,128)} %param.16) | copy-start | bytes 1572868
  38.9 2.5 %copy-start.8 = (s32[2,256]{1,0:T(2,128)S(1)}, s32[2,256]{1,0:T(2,128)}, u32[]{:S(2)}) copy-start(s32[2,256]{1,0:T(2,128)} %param.25) | copy-start | bytes 6148
  38.9 2.6 %copy-start.7 = (f32[2,2,256]{2,1,0:T(2,128)S(1)}, f32[2,2,256]{2,1,0:T(2,128)}, u32[]{:S(2)}) copy-start(f32[2,2,256]{2,1,0:T(2,128)} %param.19) | copy-start | bytes 12292
  38.9 3.9 %copy-start.15 = (s32[2]{0:T(128)S(1)}, s32[2]{0:T(128)}, u32[]{:S(2)}) copy-start(s32[2]{0:T(128)} %param.20) | copy-start | bytes 28
  38.9 4.2 %copy-start.13 = (s32[2]{0:T(128)S(1)}, s32[2]{0:T(128)}, u32[]{:S(2)}) copy-start(s32[2]{0:T(128)} %param.22) | copy-start | bytes 28
  38.9 4.2 %copy-start.14 = (s32[2]{0:T(128)S(1)}, s32[2]{0:T(128)}, u32[]{:S(2)}) copy-start(s32[2]{0:T(128)} %param.24) | copy-start | bytes 28
  39.0 4.3 %copy-start.10 = (f32[2,2]{1,0:T(2,128)S(1)}, f32[2,2]{1,0:T(2,128)}, u32[]{:S(2)}) copy-start(f32[2,2]{1,0:T(2,128)} %param.18) | copy-start | bytes 52
  39.0 4.3 %copy-start.3 = (f32[8,64,128]{2,1,0:T(8,128)S(1)}, f32[8,64,128]{2,1,0:T(8,128)}, u32[]{:S(2)}) copy-start(f32[8,64,128]{2,1,0:T(8,128)} %param.17) | copy-start | bytes 786436
  43.3 1.7 %copy-start.4 = (f32[2,64,128]{2,1,0:T(8,128)}, f32[2,64,128]{2,1,0:T(8,128)S(1)}, u32[]{:S(2)}) copy-start(f32[2,64,128]{2,1,0:T(8,128)S(1)} %and_convert_fusion) | copy-start | bytes 196612
  73.3 2.2 %copy-start.6 = (f32[504,128]{1,0:T(8,128)S(1)}, f32[504,128]{1,0:T(8,128)}, u32[]{:S(2)}) copy-start(f32[504,128]{1,0:T(8,128)} %get-tuple-element.10) | copy-start | bytes 774148
  77.2 2.5 %copy-start.9 = (f32[2,256]{1,0:T(2,128)S(1)}, f32[2,256]{1,0:T(2,128)}, u32[]{:S(2)}) copy-start(f32[2,256]{1,0:T(2,128)} %get-tuple-element.28) | copy-start | bytes 6148
  77.2 3.3 %copy-start.2 = (f32[2,8,64,128]{3,2,1,0:T(8,128)S(1)}, f32[2,8,64,128]{3,2,1,0:T(8,128)}, u32[]{:S(2)}) copy-start(f32[2,8,64,128]{3,2,1,0:T(8,128)} %param.13) | copy-start | bytes 1572868
  77.2 3.3 %copy-start.5 = (f32[2,64,128]{2,1,0:T(8,128)S(1)}, f32[2,64,128]{2,1,0:T(8,128)}, u32[]{:S(2)}) copy-start(f32[2,64,128]{2,1,0:T(8,128)} %copy-done.4) | copy-start | bytes 196612

commit v7 on v6

--- a/solution.py
+++ b/solution.py
@@ -106,28 +106,28 @@
 
             @pl.when(has_up & up_far)
             def _():
-                remote(lo_send.at[rows(p)], relay_f, p, 14, i + 1 + p).start()
+                remote(lo_send.at[rows(p)], relay_f, p, 14, i - 3 + p).start()
 
             @pl.when(has_down & down_far)
             def _():
-                remote(hi_send.at[rows(p)], relay_b, 3 + p, 15, i - 4 + p).start()
+                remote(hi_send.at[rows(p)], relay_b, 3 + p, 15, i + p).start()
 
     for p in (1, 2):
-        fwd = (x == p) & (i - 1 - p >= 0)
+        fwd = (x == p) & (i + 4 - p < n)
 
         @pl.when(fwd)
         def _():
             remote(lo_send.at[rows(p)], relay_f, p, 14, i).wait_recv()
-            copy = remote(relay_f, lo_recv.at[rows(p)], 6, 8 + p, i - p)
+            copy = remote(relay_f, lo_recv.at[rows(p)], 6, 8 + p, i + 4 - p)
             copy.start()
             copy.wait_send()
 
-        bwd = (x == p) & (i + 4 - p < n)
+        bwd = (x == p) & (i - p >= 1)
 
         @pl.when(bwd)
         def _():
             remote(hi_send.at[rows(p)], relay_b, 3 + p, 15, i).wait_recv()
-            copy = remote(relay_b, hi_recv.at[rows(p)], 7, 11 + p, i + 3 - p)
+            copy = remote(relay_b, hi_recv.at[rows(p)], 7, 11 + p, i - p - 1)
             copy.start()
             copy.wait_send()
 

time: 146 us -> 142 us (0.973)
  Pallas kernels: 113 us -> 110 us
    pallas_call x1, Pallas kernels: 60.3 us -> 47.2 us  [shots_sum(): pl.pallas_call(functools.partial(allreduce_kernel, tuple(strides)), out_s...]
    pallas_call x2, Pallas kernels: 53.1 us -> 62.6 us  [exchange(): pl.pallas_call(functools.partial(halo_kernel, n), out_shape=(jax.ShapeDty...]
where the time goes in v7:
time: 142 us; the launch traced here: 141 us
  Pallas kernels  110 us (77%)
  other arithmetic  14.7 us (10%)
  matrix products  8.19 us (6%)
  local copies, waits for them, and re-layouts  7.38 us (5%)
    pallas_call x2, Pallas kernels, exchange(): pl.pallas_call(functools.partial(halo_kernel, n), out_shape=(jax.ShapeDty...  62.6 us
    pallas_call x1, Pallas kernels, shots_sum(): pl.pallas_call(functools.partial(allreduce_kernel, tuple(strides)), out_s...  47.2 us
    dot_general x16, matrix products, exact_einsum(): jnp.einsum(spec, a, b, precision=lax.Precision.HIGHEST, preferred_element...  6.67 us
    add x2, other arithmetic, laplace(): total = total + COEF[shift_k] * (side_y + side_x)  4.91 us
    pad x4, local copies, waits for them, and re-layouts, prep(): return jnp.pad(a.reshape(total, 128), ((0, padded - total), (0, 0)))  2.87 us

profile of v7, /device:TPU:25, one launch (start us, length us, event | category | flops | bytes accessed | tf_op | source)
XLA Modules:
  0.0 141.3 jit_solution(15637611865106826511)
XLA Ops:
  0.6 0.7 subtract_clamp_fusion.1
  1.4 1.3 fusion.67
  2.7 0.4 convolution_bitcast_fusion.7
  3.9 0.7 pad.20.lo_send
  4.6 0.4 convolution_bitcast_fusion.6
  5.7 0.7 pad.21.hi_send
  6.4 32.4 %shard_map.148 = (f32[504,128]{1,0:T(8,128)}, f32[504,128]{1,0:T(8,128)}) custom-call(f32[504,128]{1,0:T(8,128)} %pad.20.lo_send, f32[504,128]{1,0:T(8,128)} %pad.21.hi_send), custom_call_target="tpu_custom_call" | custom-call | tf_op jit(solution)/shard_map/pallas_call | solution.py:164
  38.8 1.1 slice_select_fusion.2
  40.2 0.4 convolution_bitcast_fusion.13
  40.6 0.5 convolution_bitcast_fusion.5
  41.4 0.4 convolution_bitcast_fusion.12
  41.8 0.5 convolution_bitcast_fusion.4
  42.3 0.4 pad_maximum_fusion
  42.9 2.5 %fusion.6 = f32[2,2,8,64,128]{4,3,2,1,0:T(8,128)S(1)} fusion(f32[2,2,8,64,128]{4,3,2,1,0:T(8,128)S(1)} %pad_maximum_fusion.2, f32[2,2,12,64,128]{4,3,2,1,0:T(8,128)S(1)} %get-tuple-element.25, f32[2,2,12,64,128]{4,3,2,1,0:T(8,128)S(1)} %get-tuple-element.24), kind=kLoop, calls=%fused_computation.68 | loop fusion | flops 8650752 | bytes 10485760 | tf_op jit(solution)/shard_map/add | solution.py:219
  45.4 0.6 slice_bitcast_fusion.4
  46.0 0.8 fusion.58
  47.2 1.7 %fusion.77 = (f32[2,8,64,128]{3,2,1,0:T(8,128)S(1)}, f32[2,8,64,128]{3,2,1,0:T(8,128)S(1)}) fusion(f32[2,8,64,128]{3,2,1,0:T(8,128)S(1)} %bitcast.132, f32[2,2,8,64,128]{4,3,2,1,0:T(8,128)S(1)} %fusion.6, f32[2,8,64,128]{3,2,1,0:T(8,128)} %param.15, f32[2,8,64,128]{3,2,1,0:T(8,128)S(1)} %copy-done.1, f32[8,64,128]{2,1,0:T(8,128)S(1)} %copy-done.3, ...), kind=kLoop, calls=%fused_computation.153 | loop fusion | flops 1835008 | bytes 5047560 | tf_op jit(solution)/shard_map/mul | solution.py:404
  49.0 0.4 convolution_bitcast_fusion.2
  50.1 0.7 pad.24.hi_send
  50.8 0.4 convolution_bitcast_fusion.3
  51.8 0.7 pad.23.lo_send
  52.6 30.2 %shard_map.149 = (f32[504,128]{1,0:T(8,128)}, f32[504,128]{1,0:T(8,128)}) custom-call(f32[504,128]{1,0:T(8,128)} %pad.23.lo_send, f32[504,128]{1,0:T(8,128)} %pad.24.hi_send), custom_call_target="tpu_custom_call" | custom-call | tf_op jit(solution)/shard_map/pallas_call | solution.py:164
  82.8 1.0 slice_select_fusion.1
  84.5 0.5 convolution_bitcast_fusion.1
  85.4 0.4 convolution_bitcast_fusion.8
  85.7 0.5 convolution_bitcast_fusion
  86.7 2.5 %fusion.26 = f32[2,2,8,64,128]{4,3,2,1,0:T(8,128)S(1)} fusion(f32[2,2,8,64,128]{4,3,2,1,0:T(8,128)S(1)} %pad_maximum_fusion.3, f32[2,2,12,64,128]{4,3,2,1,0:T(8,128)S(1)} %get-tuple-element.21, f32[2,2,12,64,128]{4,3,2,1,0:T(8,128)S(1)} %get-tuple-element.20), kind=kLoop, calls=%fused_computation.88 | loop fusion | flops 8650752 | bytes 10485760 | tf_op jit(solution)/shard_map/add | solution.py:219
  89.2 0.8 fusion.56
  90.0 1.7 %multiply_reduce_fusion = (f32[8,64,128]{2,1,0:T(8,128)S(1)}, f32[8,64,128]{2,1,0:T(8,128)S(1)}, f32[2,8,64,128]{3,2,1,0:T(8,128)}, f32[2,8,64,128]{3,2,1,0:T(8,128)}) fusion(f32[2,8,64,128]{3,2,1,0:T(8,128)S(1)} %copy-done, f32[2,8,64,128]{3,2,1,0:T(8,128)S(1)} %get-tuple-element.19, f32[2,8,64,128]{3,2,1,0:T(8,128)S(1)} %get-tuple-element.18, ...), kind=kLoop, calls=%fused_computation.161 | loop fusion | flops 2883584 | bytes 6096136 | tf_op jit(solution)/shard_map/reduce_sum | solution.py:405
  91.7 0.7 add.305
  92.4 47.2 %shard_map.150 = f32[512,128]{1,0:T(8,128)} custom-call(f32[512,128]{1,0:T(8,128)} %bitcast.130), custom_call_target="tpu_custom_call" | custom-call | tf_op jit(solution)/shard_map/pallas_call | solution.py:362
  139.6 1.7 %copy.67 = f32[8,64,128]{2,1,0:T(8,128)} copy(f32[8,64,128]{2,1,0:T(8,128)} %bitcast.131) | data formatting | bytes 524288
  (66 shorter events, 5.3 us)
Async XLA Ops:
  1.4 1.8 %copy-start.11 = (s32[2]{0:T(128)S(1)}, s32[2]{0:T(128)}, u32[]{:S(2)}) copy-start(s32[2]{0:T(128)} %param.21) | copy-start | bytes 28
  1.4 1.8 %copy-start.12 = (s32[2]{0:T(128)S(1)}, s32[2]{0:T(128)}, u32[]{:S(2)}) copy-start(s32[2]{0:T(128)} %param.23) | copy-start | bytes 28
  40.6 1.7 %copy-start = (f32[2,8,64,128]{3,2,1,0:T(8,128)S(1)}, f32[2,8,64,128]{3,2,1,0:T(8,128)}, u32[]{:S(2)}) copy-start(f32[2,8,64,128]{3,2,1,0:T(8,128)} %param.14) | copy-start | bytes 1572868
  40.6 1.7 %copy-start.1 = (f32[2,8,64,128]{3,2,1,0:T(8,128)S(1)}, f32[2,8,64,128]{3,2,1,0:T(8,128)}, u32[]{:S(2)}) copy-start(f32[2,8,64,128]{3,2,1,0:T(8,128)} %param.16) | copy-start | bytes 1572868
  42.8 2.5 %copy-start.8 = (s32[2,256]{1,0:T(2,128)S(1)}, s32[2,256]{1,0:T(2,128)}, u32[]{:S(2)}) copy-start(s32[2,256]{1,0:T(2,128)} %param.25) | copy-start | bytes 6148
  42.8 2.6 %copy-start.7 = (f32[2,2,256]{2,1,0:T(2,128)S(1)}, f32[2,2,256]{2,1,0:T(2,128)}, u32[]{:S(2)}) copy-start(f32[2,2,256]{2,1,0:T(2,128)} %param.19) | copy-start | bytes 12292
  42.8 3.9 %copy-start.15 = (s32[2]{0:T(128)S(1)}, s32[2]{0:T(128)}, u32[]{:S(2)}) copy-start(s32[2]{0:T(128)} %param.20) | copy-start | bytes 28
  42.8 4.2 %copy-start.13 = (s32[2]{0:T(128)S(1)}, s32[2]{0:T(128)}, u32[]{:S(2)}) copy-start(s32[2]{0:T(128)} %param.22) | copy-start | bytes 28
  42.8 4.2 %copy-start.14 = (s32[2]{0:T(128)S(1)}, s32[2]{0:T(128)}, u32[]{:S(2)}) copy-start(s32[2]{0:T(128)} %param.24) | copy-start | bytes 28
  42.9 4.3 %copy-start.10 = (f32[2,2]{1,0:T(2,128)S(1)}, f32[2,2]{1,0:T(2,128)}, u32[]{:S(2)}) copy-start(f32[2,2]{1,0:T(2,128)} %param.18) | copy-start | bytes 52
  42.9 4.3 %copy-start.3 = (f32[8,64,128]{2,1,0:T(8,128)S(1)}, f32[8,64,128]{2,1,0:T(8,128)}, u32[]{:S(2)}) copy-start(f32[8,64,128]{2,1,0:T(8,128)} %param.17) | copy-start | bytes 786436
  47.2 1.7 %copy-start.4 = (f32[2,64,128]{2,1,0:T(8,128)}, f32[2,64,128]{2,1,0:T(8,128)S(1)}, u32[]{:S(2)}) copy-start(f32[2,64,128]{2,1,0:T(8,128)S(1)} %and_convert_fusion) | copy-start | bytes 196612
  82.8 2.2 %copy-start.6 = (f32[504,128]{1,0:T(8,128)S(1)}, f32[504,128]{1,0:T(8,128)}, u32[]{:S(2)}) copy-start(f32[504,128]{1,0:T(8,128)} %get-tuple-element.10) | copy-start | bytes 774148
  86.7 2.5 %copy-start.9 = (f32[2,256]{1,0:T(2,128)S(1)}, f32[2,256]{1,0:T(2,128)}, u32[]{:S(2)}) copy-start(f32[2,256]{1,0:T(2,128)} %get-tuple-element.28) | copy-start | bytes 6148
  86.7 3.3 %copy-start.2 = (f32[2,8,64,128]{3,2,1,0:T(8,128)S(1)}, f32[2,8,64,128]{3,2,1,0:T(8,128)}, u32[]{:S(2)}) copy-start(f32[2,8,64,128]{3,2,1,0:T(8,128)} %param.13) | copy-start | bytes 1572868
  86.7 3.3 %copy-start.5 = (f32[2,64,128]{2,1,0:T(8,128)S(1)}, f32[2,64,128]{2,1,0:T(8,128)}, u32[]{:S(2)}) copy-start(f32[2,64,128]{2,1,0:T(8,128)} %copy-done.4) | copy-start | bytes 196612

commit v8 on v7

--- a/solution.py
+++ b/solution.py
@@ -54,7 +54,7 @@
     return exact_einsum("sya,fsjax->fsjyx", pick_y, part)
 
 
-def halo_kernel(n, lo_send, hi_send, lo_recv, hi_recv, relay_f, relay_b, sems):
+def halo_kernel(n, lo_send, hi_send, lo_recv, hi_recv, f_near, f_far, b_near, b_far, sems):
     i = lax.axis_index("slab")
     shot = lax.axis_index("shots")
     x = i % 4
@@ -62,7 +62,7 @@
     mesh_id = pl.DeviceIdType.MESH
     barrier = pltpu.get_barrier_semaphore()
     greeted = 0
-    for d in (-3, -2, -1, 1, 2, 3):
+    for d in (-4, -3, -2, -1, 1, 2, 3, 4):
         ok = (i + d >= 0) & (i + d < n)
 
         @pl.when(ok)
@@ -94,60 +94,58 @@
 
         @pl.when(direct_up)
         def _():
-            remote(lo_send.at[rows(p)], lo_recv.at[rows(p)], p, 8 + p, i + 1).start()
+            remote(lo_send.at[rows(p)], lo_recv.at[rows(p)], p, 10 + p, i + 1).start()
 
         direct_down = has_down if p == 0 else has_down & jnp.logical_not(down_far)
 
         @pl.when(direct_down)
         def _():
-            remote(hi_send.at[rows(p)], hi_recv.at[rows(p)], 3 + p, 11 + p, i - 1).start()
+            remote(hi_send.at[rows(p)], hi_recv.at[rows(p)], 3 + p, 13 + p, i - 1).start()
 
         if p > 0:
 
             @pl.when(has_up & up_far)
             def _():
-                remote(lo_send.at[rows(p)], relay_f, p, 14, i - 3 + p).start()
+                remote(lo_send.at[rows(p)], f_near, p, 16, i - 3 + p).start()
 
             @pl.when(has_down & down_far)
             def _():
-                remote(hi_send.at[rows(p)], relay_b, 3 + p, 15, i + p).start()
-
-    for p in (1, 2):
-        fwd = (x == p) & (i + 4 - p < n)
-
-        @pl.when(fwd)
-        def _():
-            remote(lo_send.at[rows(p)], relay_f, p, 14, i).wait_recv()
-            copy = remote(relay_f, lo_recv.at[rows(p)], 6, 8 + p, i + 4 - p)
+                remote(hi_send.at[rows(p)], b_near, 3 + p, 18, i + p).start()
+
+    def relay(cond, landing, recv, out, send, out_recv, target, src_part):
+        @pl.when(cond)
+        def _():
+            remote(src_part, landing, 0, recv, i).wait_recv()
+            copy = remote(landing, out, send, out_recv, target)
             copy.start()
             copy.wait_send()
 
-        bwd = (x == p) & (i - p >= 1)
-
-        @pl.when(bwd)
-        def _():
-            remote(hi_send.at[rows(p)], relay_b, 3 + p, 15, i).wait_recv()
-            copy = remote(relay_b, hi_recv.at[rows(p)], 7, 11 + p, i - p - 1)
-            copy.start()
-            copy.wait_send()
+    for p in (1, 2):
+        mine = x == p
+        relay(mine & (i + 4 - p < n), f_near, 16, f_far, 6, 17, i + 4, lo_send.at[rows(p)])
+        relay(mine & (i - p >= 1), b_near, 18, b_far, 8, 19, i - 4, hi_send.at[rows(p)])
+    for p in (1, 2):
+        mine = x == p
+        relay(mine & (i - p >= 1), f_far, 17, lo_recv.at[rows(p)], 7, 10 + p, i - p, f_near)
+        relay(mine & (i + 4 - p < n), b_far, 19, hi_recv.at[rows(p)], 9, 13 + p, i + 3 - p, b_near)
 
     for p in range(3):
 
         @pl.when(has_up)
         def _():
-            remote(lo_send.at[rows(p)], lo_recv.at[rows(p)], p, 8 + p, i + 1).wait_send()
+            remote(lo_send.at[rows(p)], lo_recv.at[rows(p)], p, 10 + p, i + 1).wait_send()
 
         @pl.when(has_down)
         def _():
-            remote(hi_send.at[rows(p)], hi_recv.at[rows(p)], 3 + p, 11 + p, i - 1).wait_send()
+            remote(hi_send.at[rows(p)], hi_recv.at[rows(p)], 3 + p, 13 + p, i - 1).wait_send()
 
         @pl.when(has_down)
         def _():
-            remote(lo_send.at[rows(p)], lo_recv.at[rows(p)], p, 8 + p, i).wait_recv()
+            remote(lo_send.at[rows(p)], lo_recv.at[rows(p)], p, 10 + p, i).wait_recv()
 
         @pl.when(has_up)
         def _():
-            remote(hi_send.at[rows(p)], hi_recv.at[rows(p)], 3 + p, 11 + p, i).wait_recv()
+            remote(hi_send.at[rows(p)], hi_recv.at[rows(p)], 3 + p, 13 + p, i).wait_recv()
 
 
 def exchange(lo_flat, hi_flat, call_id):
@@ -172,7 +170,9 @@
         scratch_shapes=[
             pltpu.VMEM((part, 128), jnp.float32),
             pltpu.VMEM((part, 128), jnp.float32),
-            pltpu.SemaphoreType.DMA((16,)),
+            pltpu.VMEM((part, 128), jnp.float32),
+            pltpu.VMEM((part, 128), jnp.float32),
+            pltpu.SemaphoreType.DMA((20,)),
         ],
         compiler_params=pltpu.CompilerParams(collective_id=call_id, has_side_effects=True),
     )(prep(lo_flat), prep(hi_flat))

time: 142 us -> 148 us (1.042)
  Pallas kernels: 110 us -> 115 us
    pallas_call x2, Pallas kernels: 62.6 us -> 68.2 us  [exchange(): pl.pallas_call(functools.partial(halo_kernel, n), out_shape=(jax.ShapeDty...]
where the time goes in v8:
time: 148 us; the launch traced here: 146 us
  Pallas kernels  115 us (78%)
  other arithmetic  14.7 us (10%)
  matrix products  8.18 us (6%)
  local copies, waits for them, and re-layouts  7.38 us (5%)
    pallas_call x2, Pallas kernels, exchange(): pl.pallas_call(functools.partial(halo_kernel, n), out_shape=(jax.ShapeDty...  68.2 us
    pallas_call x1, Pallas kernels, shots_sum(): pl.pallas_call(functools.partial(allreduce_kernel, tuple(strides)), out_s...  46.7 us
    dot_general x16, matrix products, exact_einsum(): jnp.einsum(spec, a, b, precision=lax.Precision.HIGHEST, preferred_element...  6.66 us
    add x2, other arithmetic, laplace(): total = total + COEF[shift_k] * (side_y + side_x)  4.91 us

profile of v8, /device:TPU:25, one launch (start us, length us, event | category | flops | bytes accessed | tf_op | source)
XLA Modules:
  0.0 146.3 jit_solution(18272103963127578168)
XLA Ops:
  0.6 0.7 subtract_clamp_fusion.1
  1.4 1.3 fusion.67
  2.7 0.4 convolution_bitcast_fusion.7
  3.9 0.7 pad.20.lo_send
  4.6 0.4 convolution_bitcast_fusion.6
  5.7 0.7 pad.21.hi_send
  6.4 39.6 %shard_map.148 = (f32[504,128]{1,0:T(8,128)}, f32[504,128]{1,0:T(8,128)}) custom-call(f32[504,128]{1,0:T(8,128)} %pad.20.lo_send, f32[504,128]{1,0:T(8,128)} %pad.21.hi_send), custom_call_target="tpu_custom_call" | custom-call | tf_op jit(solution)/shard_map/pallas_call | solution.py:162
  46.0 1.1 slice_select_fusion.2
  47.8 0.5 convolution_bitcast_fusion.5
  48.6 0.4 convolution_bitcast_fusion.12
  49.0 0.5 convolution_bitcast_fusion.4
  49.5 0.4 pad_maximum_fusion
  50.1 2.5 %fusion.6 = f32[2,2,8,64,128]{4,3,2,1,0:T(8,128)S(1)} fusion(f32[2,2,8,64,128]{4,3,2,1,0:T(8,128)S(1)} %pad_maximum_fusion.2, f32[2,2,12,64,128]{4,3,2,1,0:T(8,128)S(1)} %get-tuple-element.25, f32[2,2,12,64,128]{4,3,2,1,0:T(8,128)S(1)} %get-tuple-element.24), kind=kLoop, calls=%fused_computation.68 | loop fusion | flops 8650752 | bytes 10485760 | tf_op jit(solution)/shard_map/add | solution.py:219
  52.6 0.6 slice_bitcast_fusion.4
  53.2 0.8 fusion.58
  54.4 1.7 %fusion.77 = (f32[2,8,64,128]{3,2,1,0:T(8,128)S(1)}, f32[2,8,64,128]{3,2,1,0:T(8,128)S(1)}) fusion(f32[2,8,64,128]{3,2,1,0:T(8,128)S(1)} %bitcast.132, f32[2,2,8,64,128]{4,3,2,1,0:T(8,128)S(1)} %fusion.6, f32[2,8,64,128]{3,2,1,0:T(8,128)} %param.15, f32[2,8,64,128]{3,2,1,0:T(8,128)S(1)} %copy-done.1, f32[8,64,128]{2,1,0:T(8,128)S(1)} %copy-done.3, ...), kind=kLoop, calls=%fused_computation.153 | loop fusion | flops 1835008 | bytes 5047560 | tf_op jit(solution)/shard_map/mul | solution.py:404
  56.2 0.4 convolution_bitcast_fusion.2
  57.3 0.7 pad.24.hi_send
  58.0 0.4 convolution_bitcast_fusion.3
  59.0 0.7 pad.23.lo_send
  59.7 28.6 %shard_map.149 = (f32[504,128]{1,0:T(8,128)}, f32[504,128]{1,0:T(8,128)}) custom-call(f32[504,128]{1,0:T(8,128)} %pad.23.lo_send, f32[504,128]{1,0:T(8,128)} %pad.24.hi_send), custom_call_target="tpu_custom_call" | custom-call | tf_op jit(solution)/shard_map/pallas_call | solution.py:162
  88.3 1.0 slice_select_fusion.1
  89.7 0.4 convolution_bitcast_fusion.9
  90.1 0.5 convolution_bitcast_fusion.1
  90.9 0.4 convolution_bitcast_fusion.8
  91.3 0.5 convolution_bitcast_fusion
  92.3 2.5 %fusion.26 = f32[2,2,8,64,128]{4,3,2,1,0:T(8,128)S(1)} fusion(f32[2,2,8,64,128]{4,3,2,1,0:T(8,128)S(1)} %pad_maximum_fusion.3, f32[2,2,12,64,128]{4,3,2,1,0:T(8,128)S(1)} %get-tuple-element.21, f32[2,2,12,64,128]{4,3,2,1,0:T(8,128)S(1)} %get-tuple-element.20), kind=kLoop, calls=%fused_computation.88 | loop fusion | flops 8650752 | bytes 10485760 | tf_op jit(solution)/shard_map/add | solution.py:219
  94.8 0.8 fusion.56
  95.5 1.7 %multiply_reduce_fusion = (f32[8,64,128]{2,1,0:T(8,128)S(1)}, f32[8,64,128]{2,1,0:T(8,128)S(1)}, f32[2,8,64,128]{3,2,1,0:T(8,128)}, f32[2,8,64,128]{3,2,1,0:T(8,128)}) fusion(f32[2,8,64,128]{3,2,1,0:T(8,128)S(1)} %copy-done, f32[2,8,64,128]{3,2,1,0:T(8,128)S(1)} %get-tuple-element.19, f32[2,8,64,128]{3,2,1,0:T(8,128)S(1)} %get-tuple-element.18, ...), kind=kLoop, calls=%fused_computation.161 | loop fusion | flops 2883584 | bytes 6096136 | tf_op jit(solution)/shard_map/reduce_sum | solution.py:405
  97.2 0.7 add.305
  97.9 46.7 %shard_map.150 = f32[512,128]{1,0:T(8,128)} custom-call(f32[512,128]{1,0:T(8,128)} %bitcast.130), custom_call_target="tpu_custom_call" | custom-call | tf_op jit(solution)/shard_map/pallas_call | solution.py:362
  144.7 1.7 %copy.67 = f32[8,64,128]{2,1,0:T(8,128)} copy(f32[8,64,128]{2,1,0:T(8,128)} %bitcast.131) | data formatting | bytes 524288
  (66 shorter events, 5.3 us)
Async XLA Ops:
  1.4 1.8 %copy-start.11 = (s32[2]{0:T(128)S(1)}, s32[2]{0:T(128)}, u32[]{:S(2)}) copy-start(s32[2]{0:T(128)} %param.21) | copy-start | bytes 28
  1.4 1.8 %copy-start.12 = (s32[2]{0:T(128)S(1)}, s32[2]{0:T(128)}, u32[]{:S(2)}) copy-start(s32[2]{0:T(128)} %param.23) | copy-start | bytes 28
  47.8 1.7 %copy-start = (f32[2,8,64,128]{3,2,1,0:T(8,128)S(1)}, f32[2,8,64,128]{3,2,1,0:T(8,128)}, u32[]{:S(2)}) copy-start(f32[2,8,64,128]{3,2,1,0:T(8,128)} %param.14) | copy-start | bytes 1572868
  47.8 1.7 %copy-start.1 = (f32[2,8,64,128]{3,2,1,0:T(8,128)S(1)}, f32[2,8,64,128]{3,2,1,0:T(8,128)}, u32[]{:S(2)}) copy-start(f32[2,8,64,128]{3,2,1,0:T(8,128)} %param.16) | copy-start | bytes 1572868
  50.0 2.5 %copy-start.8 = (s32[2,256]{1,0:T(2,128)S(1)}, s32[2,256]{1,0:T(2,128)}, u32[]{:S(2)}) copy-start(s32[2,256]{1,0:T(2,128)} %param.25) | copy-start | bytes 6148
  50.0 2.6 %copy-start.7 = (f32[2,2,256]{2,1,0:T(2,128)S(1)}, f32[2,2,256]{2,1,0:T(2,128)}, u32[]{:S(2)}) copy-start(f32[2,2,256]{2,1,0:T(2,128)} %param.19) | copy-start | bytes 12292
  50.0 3.9 %copy-start.15 = (s32[2]{0:T(128)S(1)}, s32[2]{0:T(128)}, u32[]{:S(2)}) copy-start(s32[2]{0:T(128)} %param.20) | copy-start | bytes 28
  50.0 4.2 %copy-start.13 = (s32[2]{0:T(128)S(1)}, s32[2]{0:T(128)}, u32[]{:S(2)}) copy-start(s32[2]{0:T(128)} %param.22) | copy-start | bytes 28
  50.0 4.2 %copy-start.14 = (s32[2]{0:T(128)S(1)}, s32[2]{0:T(128)}, u32[]{:S(2)}) copy-start(s32[2]{0:T(128)} %param.24) | copy-start | bytes 28
  50.1 4.3 %copy-start.10 = (f32[2,2]{1,0:T(2,128)S(1)}, f32[2,2]{1,0:T(2,128)}, u32[]{:S(2)}) copy-start(f32[2,2]{1,0:T(2,128)} %param.18) | copy-start | bytes 52
  50.1 4.3 %copy-start.3 = (f32[8,64,128]{2,1,0:T(8,128)S(1)}, f32[8,64,128]{2,1,0:T(8,128)}, u32[]{:S(2)}) copy-start(f32[8,64,128]{2,1,0:T(8,128)} %param.17) | copy-start | bytes 786436
  54.4 1.7 %copy-start.4 = (f32[2,64,128]{2,1,0:T(8,128)}, f32[2,64,128]{2,1,0:T(8,128)S(1)}, u32[]{:S(2)}) copy-start(f32[2,64,128]{2,1,0:T(8,128)S(1)} %and_convert_fusion) | copy-start | bytes 196612
  88.3 2.2 %copy-start.6 = (f32[504,128]{1,0:T(8,128)S(1)}, f32[504,128]{1,0:T(8,128)}, u32[]{:S(2)}) copy-start(f32[504,128]{1,0:T(8,128)} %get-tuple-element.10) | copy-start | bytes 774148
  92.3 2.5 %copy-start.9 = (f32[2,256]{1,0:T(2,128)S(1)}, f32[2,256]{1,0:T(2,128)}, u32[]{:S(2)}) copy-start(f32[2,256]{1,0:T(2,128)} %get-tuple-element.28) | copy-start | bytes 6148
  92.3 3.3 %copy-start.2 = (f32[2,8,64,128]{3,2,1,0:T(8,128)S(1)}, f32[2,8,64,128]{3,2,1,0:T(8,128)}, u32[]{:S(2)}) copy-start(f32[2,8,64,128]{3,2,1,0:T(8,128)} %param.13) | copy-start | bytes 1572868
  92.3 3.3 %copy-start.5 = (f32[2,64,128]{2,1,0:T(8,128)S(1)}, f32[2,64,128]{2,1,0:T(8,128)}, u32[]{:S(2)}) copy-start(f32[2,64,128]{2,1,0:T(8,128)} %copy-done.4) | copy-start | bytes 196612

commit v9 on v7

--- a/solution.py
+++ b/solution.py
@@ -288,83 +288,84 @@
     return piece.reshape(shape)
 
 
-def allreduce_kernel(strides, local_ref, out_ref, *scratch):
-    rounds = len(strides)
-    halves = scratch[:rounds]
-    sums = scratch[rounds : 2 * rounds]
-    send_sems, recv_sems = scratch[2 * rounds], scratch[2 * rounds + 1]
+def allreduce_kernel(chips, local_ref, out_ref, half_in, gathered, spread, send_sems, recv_sems):
     me = lax.axis_index("shots")
     slab = lax.axis_index("slab")
+    core = me % 2
+    chip = me // 2
     mesh_id = pl.DeviceIdType.MESH
+    rows = local_ref.shape[0] // 2
+    chunk = rows // chips
     barrier = pltpu.get_barrier_semaphore()
-    for stride in strides:
-        partner = me + stride - 2 * stride * ((me // stride) % 2)
-        pl.semaphore_signal(barrier, inc=1, device_id=(slab, partner), device_id_type=mesh_id)
-    pl.semaphore_wait(barrier, rounds)
-    source = local_ref
-    start = 0
-    rows = local_ref.shape[0]
-    for k, stride in enumerate(strides):
-        upper = (me // stride) % 2
-        partner = me + stride - 2 * stride * upper
-        rows //= 2
-        copy = pltpu.make_async_remote_copy(
-            src_ref=source.at[pl.ds(pl.multiple_of((1 - upper) * rows, 8), rows)],
-            dst_ref=halves[k],
-            send_sem=send_sems.at[k],
-            recv_sem=recv_sems.at[k],
-            device_id=(slab, partner),
+    pl.semaphore_signal(barrier, inc=1, device_id=(slab, me + 1 - 2 * core), device_id_type=mesh_id)
+    for k in range(1, chips):
+        peer = lax.rem(chip + k, chips) * 2 + core
+        pl.semaphore_signal(barrier, inc=1, device_id=(slab, peer), device_id_type=mesh_id)
+    pl.semaphore_wait(barrier, chips)
+
+    def remote(src, dst, slot, target):
+        return pltpu.make_async_remote_copy(
+            src_ref=src,
+            dst_ref=dst,
+            send_sem=send_sems.at[slot],
+            recv_sem=recv_sems.at[slot],
+            device_id=(slab, target),
             device_id_type=mesh_id,
         )
+
+    mine = pl.ds(pl.multiple_of(core * rows, 8), rows)
+    theirs = pl.ds(pl.multiple_of((1 - core) * rows, 8), rows)
+    copy = remote(local_ref.at[theirs], half_in, 0, me + 1 - 2 * core)
+    copy.start()
+    copy.wait()
+    out_ref[mine] = local_ref[mine] + half_in[...]
+    copies = []
+    for k in range(1, chips):
+        target = lax.rem(chip + k, chips)
+        src = out_ref.at[pl.ds(pl.multiple_of(core * rows + target * chunk, 8), chunk)]
+        copy = remote(src, gathered.at[k], k, target * 2 + core)
         copy.start()
+        copies.append(copy)
+    for copy in copies:
         copy.wait()
-        kept = source[pl.ds(pl.multiple_of(upper * rows, 8), rows)]
-        sums[k][...] = kept + halves[k][...]
-        source = sums[k]
-        start = start + upper * rows
-    out_ref[pl.ds(pl.multiple_of(start, 8), rows)] = sums[rounds - 1][...]
-    for k in reversed(range(rounds)):
-        stride = strides[k]
-        upper = (me // stride) % 2
-        partner = me + stride - 2 * stride * upper
-        mine = out_ref.at[pl.ds(pl.multiple_of(start, 8), rows)]
-        copy = pltpu.make_async_remote_copy(
-            src_ref=mine,
-            dst_ref=mine,
-            send_sem=send_sems.at[rounds + k],
-            recv_sem=recv_sems.at[rounds + k],
-            device_id=(slab, partner),
-            device_id_type=mesh_id,
-        )
+    own = pl.ds(pl.multiple_of(core * rows + chip * chunk, 8), chunk)
+    total = out_ref[own]
+    for k in range(1, chips):
+        total = total + gathered[k]
+    out_ref[own] = total
+    copies = []
+    for k in range(1, chips):
+        target = lax.rem(chip + k, chips)
+        copy = remote(out_ref.at[own], spread.at[k], chips + k, target * 2 + core)
         copy.start()
+        copies.append(copy)
+    for copy in copies:
         copy.wait()
-        start = start - upper * rows
-        rows *= 2
+    for k in range(1, chips):
+        source = lax.rem(chip + chips - k, chips)
+        out_ref[pl.ds(pl.multiple_of(core * rows + source * chunk, 8), chunk)] = spread[k]
+    copy = remote(out_ref.at[mine], out_ref.at[mine], 2 * chips, me + 1 - 2 * core)
+    copy.start()
+    copy.wait()
 
 
 def shots_sum(value):
-    count = lax.axis_size("shots")
-    strides = []
-    stride = 1
-    while stride < count:
-        strides.append(stride)
-        stride *= 2
+    chips = lax.axis_size("shots") // 2
     shape = value.shape
     chunks = value.reshape(-1, 128)
     rows = chunks.shape[0]
-    scratch = []
-    for k in range(len(strides)):
-        scratch.append(pltpu.VMEM((rows >> (k + 1), 128), jnp.float32))
-    for k in range(len(strides)):
-        scratch.append(pltpu.VMEM((rows >> (k + 1), 128), jnp.float32))
-    scratch.append(pltpu.SemaphoreType.DMA((2 * len(strides),)))
-    scratch.append(pltpu.SemaphoreType.DMA((2 * len(strides),)))
     out = pl.pallas_call(
-        functools.partial(allreduce_kernel, tuple(strides)),
+        functools.partial(allreduce_kernel, chips),
         out_shape=jax.ShapeDtypeStruct(chunks.shape, jnp.float32),
         in_specs=[pl.BlockSpec(memory_space=pltpu.VMEM)],
         out_specs=pl.BlockSpec(memory_space=pltpu.VMEM),
-        scratch_shapes=scratch,
+        scratch_shapes=[
+            pltpu.VMEM((rows // 2, 128), jnp.float32),
+            pltpu.VMEM((chips, rows // 2 // chips, 128), jnp.float32),
+            pltpu.VMEM((chips, rows // 2 // chips, 128), jnp.float32),
+            pltpu.SemaphoreType.DMA((2 * chips + 1,)),
+            pltpu.SemaphoreType.DMA((2 * chips + 1,)),
+        ],
         compiler_params=pltpu.CompilerParams(collective_id=0, has_side_effects=True),
     )(chunks)
     return out.reshape(shape)

time: 142 us -> 136 us (0.958)
  Pallas kernels: 110 us -> 104 us
    pallas_call x1, Pallas kernels: 47.2 us -> 41.6 us  [shots_sum(): pl.pallas_call(functools.partial(allreduce_kernel, chips), out_shape=jax....]
where the time goes in v9:
time: 136 us
  Pallas kernels  104 us (76%)
  other arithmetic  14.7 us (11%)
  matrix products  8.19 us (6%)
  local copies, waits for them, and re-layouts  7.38 us (5%)
    pallas_call x2, Pallas kernels, exchange(): pl.pallas_call(functools.partial(halo_kernel, n), out_shape=(jax.ShapeDty...  62.6 us
    pallas_call x1, Pallas kernels, shots_sum(): pl.pallas_call(functools.partial(allreduce_kernel, chips), out_shape=jax....  41.6 us
    dot_general x16, matrix products, exact_einsum(): jnp.einsum(spec, a, b, precision=lax.Precision.HIGHEST, preferred_element...  6.67 us
    add x2, other arithmetic, laplace(): total = total + COEF[shift_k] * (side_y + side_x)  4.91 us
    pad x4, local copies, waits for them, and re-layouts, prep(): return jnp.pad(a.reshape(total, 128), ((0, padded - total), (0, 0)))  2.87 us

profile of v9, /device:TPU:25, one launch (start us, length us, event | category | flops | bytes accessed | tf_op | source)
XLA Modules:
  0.0 135.6 jit_solution(15506981044901646317)
XLA Ops:
  0.6 0.7 subtract_clamp_fusion.1
  1.4 1.3 fusion.67
  2.7 0.4 convolution_bitcast_fusion.7
  3.9 0.7 pad.20.lo_send
  4.6 0.4 convolution_bitcast_fusion.6
  5.7 0.7 pad.21.hi_send
  6.4 32.4 %shard_map.148 = (f32[504,128]{1,0:T(8,128)}, f32[504,128]{1,0:T(8,128)}) custom-call(f32[504,128]{1,0:T(8,128)} %pad.20.lo_send, f32[504,128]{1,0:T(8,128)} %pad.21.hi_send), custom_call_target="tpu_custom_call" | custom-call | tf_op jit(solution)/shard_map/pallas_call | solution.py:164
  38.8 1.1 slice_select_fusion.2
  40.2 0.4 convolution_bitcast_fusion.13
  40.6 0.5 convolution_bitcast_fusion.5
  41.4 0.4 convolution_bitcast_fusion.12
  41.8 0.5 convolution_bitcast_fusion.4
  42.3 0.4 pad_maximum_fusion
  42.9 2.5 %fusion.6 = f32[2,2,8,64,128]{4,3,2,1,0:T(8,128)S(1)} fusion(f32[2,2,8,64,128]{4,3,2,1,0:T(8,128)S(1)} %pad_maximum_fusion.2, f32[2,2,12,64,128]{4,3,2,1,0:T(8,128)S(1)} %get-tuple-element.25, f32[2,2,12,64,128]{4,3,2,1,0:T(8,128)S(1)} %get-tuple-element.24), kind=kLoop, calls=%fused_computation.68 | loop fusion | flops 8650752 | bytes 10485760 | tf_op jit(solution)/shard_map/add | solution.py:219
  45.4 0.6 slice_bitcast_fusion.4
  46.0 0.8 fusion.58
  47.2 1.7 %fusion.77 = (f32[2,8,64,128]{3,2,1,0:T(8,128)S(1)}, f32[2,8,64,128]{3,2,1,0:T(8,128)S(1)}) fusion(f32[2,8,64,128]{3,2,1,0:T(8,128)S(1)} %bitcast.132, f32[2,2,8,64,128]{4,3,2,1,0:T(8,128)S(1)} %fusion.6, f32[2,8,64,128]{3,2,1,0:T(8,128)} %param.15, f32[2,8,64,128]{3,2,1,0:T(8,128)S(1)} %copy-done.1, f32[8,64,128]{2,1,0:T(8,128)S(1)} %copy-done.3, ...), kind=kLoop, calls=%fused_computation.153 | loop fusion | flops 1835008 | bytes 5047560 | tf_op jit(solution)/shard_map/mul | solution.py:405
  49.0 0.4 convolution_bitcast_fusion.2
  50.1 0.7 pad.24.hi_send
  50.8 0.4 convolution_bitcast_fusion.3
  51.8 0.7 pad.23.lo_send
  52.6 30.2 %shard_map.149 = (f32[504,128]{1,0:T(8,128)}, f32[504,128]{1,0:T(8,128)}) custom-call(f32[504,128]{1,0:T(8,128)} %pad.23.lo_send, f32[504,128]{1,0:T(8,128)} %pad.24.hi_send), custom_call_target="tpu_custom_call" | custom-call | tf_op jit(solution)/shard_map/pallas_call | solution.py:164
  82.8 1.0 slice_select_fusion.1
  84.5 0.5 convolution_bitcast_fusion.1
  85.4 0.4 convolution_bitcast_fusion.8
  85.7 0.5 convolution_bitcast_fusion
  86.7 2.5 %fusion.26 = f32[2,2,8,64,128]{4,3,2,1,0:T(8,128)S(1)} fusion(f32[2,2,8,64,128]{4,3,2,1,0:T(8,128)S(1)} %pad_maximum_fusion.3, f32[2,2,12,64,128]{4,3,2,1,0:T(8,128)S(1)} %get-tuple-element.21, f32[2,2,12,64,128]{4,3,2,1,0:T(8,128)S(1)} %get-tuple-element.20), kind=kLoop, calls=%fused_computation.88 | loop fusion | flops 8650752 | bytes 10485760 | tf_op jit(solution)/shard_map/add | solution.py:219
  89.2 0.8 fusion.56
  90.0 1.7 %multiply_reduce_fusion = (f32[8,64,128]{2,1,0:T(8,128)S(1)}, f32[8,64,128]{2,1,0:T(8,128)S(1)}, f32[2,8,64,128]{3,2,1,0:T(8,128)}, f32[2,8,64,128]{3,2,1,0:T(8,128)}) fusion(f32[2,8,64,128]{3,2,1,0:T(8,128)S(1)} %copy-done, f32[2,8,64,128]{3,2,1,0:T(8,128)S(1)} %get-tuple-element.19, f32[2,8,64,128]{3,2,1,0:T(8,128)S(1)} %get-tuple-element.18, ...), kind=kLoop, calls=%fused_computation.161 | loop fusion | flops 2883584 | bytes 6096136 | tf_op jit(solution)/shard_map/reduce_sum | solution.py:406
  91.7 0.7 add.305
  92.4 41.6 %shard_map.150 = f32[512,128]{1,0:T(8,128)} custom-call(f32[512,128]{1,0:T(8,128)} %bitcast.130), custom_call_target="tpu_custom_call" | custom-call | tf_op jit(solution)/shard_map/pallas_call | solution.py:357
  133.9 1.7 %copy.67 = f32[8,64,128]{2,1,0:T(8,128)} copy(f32[8,64,128]{2,1,0:T(8,128)} %bitcast.131) | data formatting | bytes 524288
  (66 shorter events, 5.3 us)
Async XLA Ops:
  1.4 1.8 %copy-start.11 = (s32[2]{0:T(128)S(1)}, s32[2]{0:T(128)}, u32[]{:S(2)}) copy-start(s32[2]{0:T(128)} %param.21) | copy-start | bytes 28
  1.4 1.8 %copy-start.12 = (s32[2]{0:T(128)S(1)}, s32[2]{0:T(128)}, u32[]{:S(2)}) copy-start(s32[2]{0:T(128)} %param.23) | copy-start | bytes 28
  40.6 1.7 %copy-start = (f32[2,8,64,128]{3,2,1,0:T(8,128)S(1)}, f32[2,8,64,128]{3,2,1,0:T(8,128)}, u32[]{:S(2)}) copy-start(f32[2,8,64,128]{3,2,1,0:T(8,128)} %param.14) | copy-start | bytes 1572868
  40.6 1.7 %copy-start.1 = (f32[2,8,64,128]{3,2,1,0:T(8,128)S(1)}, f32[2,8,64,128]{3,2,1,0:T(8,128)}, u32[]{:S(2)}) copy-start(f32[2,8,64,128]{3,2,1,0:T(8,128)} %param.16) | copy-start | bytes 1572868
  42.8 2.5 %copy-start.8 = (s32[2,256]{1,0:T(2,128)S(1)}, s32[2,256]{1,0:T(2,128)}, u32[]{:S(2)}) copy-start(s32[2,256]{1,0:T(2,128)} %param.25) | copy-start | bytes 6148
  42.8 2.6 %copy-start.7 = (f32[2,2,256]{2,1,0:T(2,128)S(1)}, f32[2,2,256]{2,1,0:T(2,128)}, u32[]{:S(2)}) copy-start(f32[2,2,256]{2,1,0:T(2,128)} %param.19) | copy-start | bytes 12292
  42.8 3.9 %copy-start.15 = (s32[2]{0:T(128)S(1)}, s32[2]{0:T(128)}, u32[]{:S(2)}) copy-start(s32[2]{0:T(128)} %param.20) | copy-start | bytes 28
  42.8 4.2 %copy-start.13 = (s32[2]{0:T(128)S(1)}, s32[2]{0:T(128)}, u32[]{:S(2)}) copy-start(s32[2]{0:T(128)} %param.22) | copy-start | bytes 28
  42.8 4.2 %copy-start.14 = (s32[2]{0:T(128)S(1)}, s32[2]{0:T(128)}, u32[]{:S(2)}) copy-start(s32[2]{0:T(128)} %param.24) | copy-start | bytes 28
  42.9 4.3 %copy-start.10 = (f32[2,2]{1,0:T(2,128)S(1)}, f32[2,2]{1,0:T(2,128)}, u32[]{:S(2)}) copy-start(f32[2,2]{1,0:T(2,128)} %param.18) | copy-start | bytes 52
  42.9 4.3 %copy-start.3 = (f32[8,64,128]{2,1,0:T(8,128)S(1)}, f32[8,64,128]{2,1,0:T(8,128)}, u32[]{:S(2)}) copy-start(f32[8,64,128]{2,1,0:T(8,128)} %param.17) | copy-start | bytes 786436
  47.2 1.7 %copy-start.4 = (f32[2,64,128]{2,1,0:T(8,128)}, f32[2,64,128]{2,1,0:T(8,128)S(1)}, u32[]{:S(2)}) copy-start(f32[2,64,128]{2,1,0:T(8,128)S(1)} %and_convert_fusion) | copy-start | bytes 196612
  82.8 2.2 %copy-start.6 = (f32[504,128]{1,0:T(8,128)S(1)}, f32[504,128]{1,0:T(8,128)}, u32[]{:S(2)}) copy-start(f32[504,128]{1,0:T(8,128)} %get-tuple-element.10) | copy-start | bytes 774148
  86.7 2.5 %copy-start.9 = (f32[2,256]{1,0:T(2,128)S(1)}, f32[2,256]{1,0:T(2,128)}, u32[]{:S(2)}) copy-start(f32[2,256]{1,0:T(2,128)} %get-tuple-element.28) | copy-start | bytes 6148
  86.7 3.3 %copy-start.2 = (f32[2,8,64,128]{3,2,1,0:T(8,128)S(1)}, f32[2,8,64,128]{3,2,1,0:T(8,128)}, u32[]{:S(2)}) copy-start(f32[2,8,64,128]{3,2,1,0:T(8,128)} %param.13) | copy-start | bytes 1572868
  86.7 3.3 %copy-start.5 = (f32[2,64,128]{2,1,0:T(8,128)S(1)}, f32[2,64,128]{2,1,0:T(8,128)}, u32[]{:S(2)}) copy-start(f32[2,64,128]{2,1,0:T(8,128)} %copy-done.4) | copy-start | bytes 196612

commit v10 on v9

--- a/solution.py
+++ b/solution.py
@@ -54,11 +54,13 @@
     return exact_einsum("sya,fsjax->fsjyx", pick_y, part)
 
 
-def halo_kernel(n, lo_send, hi_send, lo_recv, hi_recv, relay_f, relay_b, sems):
+def halo_kernel(n, send_ref, recv_ref, relay_f, relay_b, sems):
+    lo_send, hi_send = send_ref.at[0], send_ref.at[1]
+    lo_recv, hi_recv = recv_ref.at[0], recv_ref.at[1]
     i = lax.axis_index("slab")
     shot = lax.axis_index("shots")
     x = i % 4
-    part = lo_send.shape[0] // 3
+    part = send_ref.shape[1] // 3
     mesh_id = pl.DeviceIdType.MESH
     barrier = pltpu.get_barrier_semaphore()
     greeted = 0
@@ -150,48 +152,46 @@
             remote(hi_send.at[rows(p)], hi_recv.at[rows(p)], 3 + p, 11 + p, i).wait_recv()
 
 
-def exchange(lo_flat, hi_flat, call_id):
+def exchange(both, call_id):
     n = lax.axis_size("slab")
-    shape = lo_flat.shape
-    total = lo_flat.size // 128
+    shape = both.shape
+    total = both[0].size // 128
     part = -(-total // 24) * 8
     padded = 3 * part
-
-    def prep(a):
-        return jnp.pad(a.reshape(total, 128), ((0, padded - total), (0, 0)))
-
+    send = jnp.pad(both.reshape(2, total, 128), ((0, 0), (0, padded - total), (0, 0)))
     vmem = pl.BlockSpec(memory_space=pltpu.VMEM)
-    lo_recv, hi_recv = pl.pallas_call(
+    recv = pl.pallas_call(
         functools.partial(halo_kernel, n),
-        out_shape=(
-            jax.ShapeDtypeStruct((padded, 128), jnp.float32),
-            jax.ShapeDtypeStruct((padded, 128), jnp.float32),
-        ),
-        in_specs=[vmem, vmem],
-        out_specs=(vmem, vmem),
+        out_shape=jax.ShapeDtypeStruct((2, padded, 128), jnp.float32),
+        in_specs=[vmem],
+        out_specs=vmem,
         scratch_shapes=[
             pltpu.VMEM((part, 128), jnp.float32),
             pltpu.VMEM((part, 128), jnp.float32),
             pltpu.SemaphoreType.DMA((16,)),
         ],
         compiler_params=pltpu.CompilerParams(collective_id=call_id, has_side_effects=True),
-    )(prep(lo_flat), prep(hi_flat))
-    return lo_recv[:total].reshape(shape), hi_recv[:total].reshape(shape)
+    )(send)
+    return recv[:, :total].reshape(shape)
 
 
 def extended(block, pick_y, pick_x, width, call_id):
     dim = 2
-    lo_flat = cut_windows(
-        lax.slice_in_dim(block, block.shape[dim] - width, None, axis=dim), pick_y, pick_x
-    )
-    hi_flat = cut_windows(lax.slice_in_dim(block, 0, width, axis=dim), pick_y, pick_x)
-    low, high = exchange(lo_flat, hi_flat, call_id)
+    sides = jnp.stack(
+        [
+            lax.slice_in_dim(block, block.shape[dim] - width, None, axis=dim),
+            lax.slice_in_dim(block, 0, width, axis=dim),
+        ]
+    )
+    part = exact_einsum("zfsjyx,sbx->zfsjyb", sides, pick_x)
+    part = exact_einsum("sya,zfsjyb->zfsjab", pick_y, part)
+    got = exchange(part, call_id)
     i = lax.axis_index("slab")
-    low = jnp.where(i >= 1, low, 0.0)
-    high = jnp.where(i + 1 < lax.axis_size("slab"), high, 0.0)
-    low = paste_windows(low, pick_y, pick_x, width)
-    high = paste_windows(high, pick_y, pick_x, width)
-    return jnp.concatenate([low, block, high], axis=dim)
+    present = jnp.stack([i >= 1, i + 1 < lax.axis_size("slab")])
+    got = jnp.where(present[:, None, None, None, None, None], got, 0.0)
+    got = exact_einsum("zfsjab,sbx->zfsjax", got, pick_x)
+    got = exact_einsum("sya,zfsjax->zfsjyx", pick_y, got)
+    return jnp.concatenate([got[0], block, got[1]], axis=dim)
 
 
 def laplace(padded):

time: 136 us -> 133 us (0.978)
  other arithmetic: 14.7 us -> 11.9 us
  matrix products: 8.19 us -> 6.63 us
    reshape x0 -> x4, local copies, waits for them, and re-layouts: none -> 2.27 us  [the longest x2 1.23 us: exchange(): return recv[:, :total].reshape(shape)]
    slice x0 -> x2, local copies, waits for them, and re-layouts: none -> 2.14 us  [exchange(): return recv[:, :total].reshape(shape)]
    select_n x3 -> x0, other arithmetic: 2.13 us -> none  [the longest x2 1.12 us: extended(): low = jnp.where(i >= 1, low, 0.0)]
    dot_general x16 -> x8, matrix products: 6.67 us -> 5.11 us  [exact_einsum(): jnp.einsum(spec, a, b, precision=lax.Precision.HIGHEST, preferred_element...]
    another operation x0 -> x3, other arithmetic: none -> 1.45 us  [the longest x2 1.37 us: extended(): jnp.stack([lax.slice_in_dim(block, block.shape[dim] - width, None, axis=d...]
    another operation x4 -> x2, other arithmetic: 1.54 us -> 0.18 us  [per_device(): stacked = jnp.stack([u, v])]
    pad x4 -> x2, local copies, waits for them, and re-layouts: 2.87 us -> 1.64 us  [exchange(): jnp.pad(both.reshape(2, total, 128), ((0, 0), (0, padded - total), (0, 0)))]
where the time goes in v10:
time: 133 us; the launch traced here: 132 us
  Pallas kernels  104 us (78%)
  other arithmetic  11.9 us (9%)
  local copies, waits for them, and re-layouts  8.52 us (6%)
  matrix products  6.63 us (5%)
    pallas_call x2, Pallas kernels, exchange(): pl.pallas_call(functools.partial(halo_kernel, n), out_shape=jax.ShapeDtyp...  62.5 us
    pallas_call x1, Pallas kernels, shots_sum(): pl.pallas_call(functools.partial(allreduce_kernel, chips), out_shape=jax....  41.6 us
    dot_general x8, matrix products, exact_einsum(): jnp.einsum(spec, a, b, precision=lax.Precision.HIGHEST, preferred_element...  5.11 us
    add x2, other arithmetic, laplace(): total = total + COEF[shift_k] * (side_y + side_x)  4.91 us

profile of v10, /device:TPU:25, one launch (start us, length us, event | category | flops | bytes accessed | tf_op | source)
XLA Modules:
  0.0 132.3 jit_solution(6571781117392355357)
XLA Ops:
  0.7 1.3 fusion.73
  2.1 0.7 convolution_bitcast_fusion.3
  2.9 0.6 convolution_bitcast_fusion.5
  3.5 0.5 reshape.247
  4.1 0.8 pad.14.send_ref
  4.9 32.3 %shard_map.148 = f32[2,504,128]{2,1,0:T(8,128)} custom-call(f32[2,504,128]{2,1,0:T(8,128)} %pad.14.send_ref), custom_call_target="tpu_custom_call" | custom-call | tf_op jit(solution)/shard_map/pallas_call | solution.py:163
  37.2 1.1 slice.216
  38.3 0.6 reshape.248
  39.0 0.6 convolution_bitcast_fusion.7
  39.6 0.7 convolution_bitcast_fusion.2
  40.5 0.2 copy-done
  40.7 0.2 copy-done.1
  40.8 0.4 pad_maximum_fusion
  41.4 2.5 %fusion.6 = f32[2,2,8,64,128]{4,3,2,1,0:T(8,128)S(1)} fusion(f32[2,2,8,64,128]{4,3,2,1,0:T(8,128)S(1)} %pad_maximum_fusion.2, f32[2,2,12,64,128]{4,3,2,1,0:T(8,128)S(1)} %get-tuple-element.19, f32[2,2,12,64,128]{4,3,2,1,0:T(8,128)S(1)} %get-tuple-element.18), kind=kLoop, calls=%fused_computation.60 | loop fusion | flops 8650752 | bytes 10485760 | tf_op jit(solution)/shard_map/add | solution.py:219
  43.9 0.8 fusion.60
  45.1 1.7 %fusion.85 = (f32[2,8,64,128]{3,2,1,0:T(8,128)S(1)}, f32[2,8,64,128]{3,2,1,0:T(8,128)S(1)}) fusion(f32[2,8,64,128]{3,2,1,0:T(8,128)S(1)} %bitcast.122, f32[2,2,8,64,128]{4,3,2,1,0:T(8,128)S(1)} %fusion.6, f32[2,8,64,128]{3,2,1,0:T(8,128)} %param.15, f32[2,8,64,128]{3,2,1,0:T(8,128)S(1)} %copy-done.1, f32[8,64,128]{2,1,0:T(8,128)S(1)} %copy-done.3, ...), kind=kLoop, calls=%fused_computation.157 | loop fusion | flops 1835008 | bytes 5047560 | tf_op jit(solution)/shard_map/mul | solution.py:405
  46.9 0.7 convolution_bitcast_fusion.1
  47.5 0.6 convolution_bitcast_fusion.4
  48.2 0.5 reshape.250
  48.7 0.8 pad.16.send_ref
  49.6 30.1 %shard_map.149 = f32[2,504,128]{2,1,0:T(8,128)} custom-call(f32[2,504,128]{2,1,0:T(8,128)} %pad.16.send_ref), custom_call_target="tpu_custom_call" | custom-call | tf_op jit(solution)/shard_map/pallas_call | solution.py:163
  79.7 1.1 slice.249
  80.8 0.6 reshape.251
  81.4 0.6 convolution_bitcast_fusion.6
  82.0 0.7 convolution_bitcast_fusion
  82.8 0.4 pad_maximum_fusion.1
  83.3 2.5 %fusion.26 = f32[2,2,8,64,128]{4,3,2,1,0:T(8,128)S(1)} fusion(f32[2,2,8,64,128]{4,3,2,1,0:T(8,128)S(1)} %pad_maximum_fusion.3, f32[2,2,12,64,128]{4,3,2,1,0:T(8,128)S(1)} %get-tuple-element.13, f32[2,2,12,64,128]{4,3,2,1,0:T(8,128)S(1)} %get-tuple-element.12), kind=kLoop, calls=%fused_computation.80 | loop fusion | flops 8650752 | bytes 10485760 | tf_op jit(solution)/shard_map/add | solution.py:219
  85.8 0.8 fusion.58
  86.6 1.7 %multiply_reduce_fusion = (f32[8,64,128]{2,1,0:T(8,128)S(1)}, f32[8,64,128]{2,1,0:T(8,128)S(1)}, f32[2,8,64,128]{3,2,1,0:T(8,128)}, f32[2,8,64,128]{3,2,1,0:T(8,128)}) fusion(f32[2,8,64,128]{3,2,1,0:T(8,128)S(1)} %copy-done, f32[2,8,64,128]{3,2,1,0:T(8,128)S(1)} %get-tuple-element.11, f32[2,8,64,128]{3,2,1,0:T(8,128)S(1)} %get-tuple-element.10, ...), kind=kLoop, calls=%fused_computation.163 | loop fusion | flops 2883584 | bytes 6096136 | tf_op jit(solution)/shard_map/reduce_sum | solution.py:406
  88.2 0.7 add.301
  89.0 41.6 %shard_map.150 = f32[512,128]{1,0:T(8,128)} custom-call(f32[512,128]{1,0:T(8,128)} %bitcast.120), custom_call_target="tpu_custom_call" | custom-call | tf_op jit(solution)/shard_map/pallas_call | solution.py:357
  130.6 1.7 %copy.51 = f32[8,64,128]{2,1,0:T(8,128)} copy(f32[8,64,128]{2,1,0:T(8,128)} %bitcast.121) | data formatting | bytes 524288
  (46 shorter events, 1.3 us)
Async XLA Ops:
  0.6 1.4 %copy-start.10 = (s32[2]{0:T(128)S(1)}, s32[2]{0:T(128)}, u32[]{:S(2)}) copy-start(s32[2]{0:T(128)} %param.22) | copy-start | bytes 28
  0.6 1.4 %copy-start.11 = (s32[2]{0:T(128)S(1)}, s32[2]{0:T(128)}, u32[]{:S(2)}) copy-start(s32[2]{0:T(128)} %param.24) | copy-start | bytes 28
  2.0 0.8 copy-start.8
  2.0 0.8 copy-start.9
  39.6 1.0 copy-start
  39.6 1.2 copy-start.1
  41.3 2.5 %copy-start.6 = (s32[2,256]{1,0:T(2,128)S(1)}, s32[2,256]{1,0:T(2,128)}, u32[]{:S(2)}) copy-start(s32[2,256]{1,0:T(2,128)} %param.25) | copy-start | bytes 6148
  41.3 2.6 %copy-start.5 = (f32[2,2,256]{2,1,0:T(2,128)S(1)}, f32[2,2,256]{2,1,0:T(2,128)}, u32[]{:S(2)}) copy-start(f32[2,2,256]{2,1,0:T(2,128)} %param.19) | copy-start | bytes 12292
  41.3 3.3 %copy-start.12 = (s32[2]{0:T(128)S(1)}, s32[2]{0:T(128)}, u32[]{:S(2)}) copy-start(s32[2]{0:T(128)} %param.20) | copy-start | bytes 28
  41.3 3.7 %copy-start.7 = (f32[2,2]{1,0:T(2,128)S(1)}, f32[2,2]{1,0:T(2,128)}, u32[]{:S(2)}) copy-start(f32[2,2]{1,0:T(2,128)} %param.18) | copy-start | bytes 52
  41.4 3.7 %copy-start.3 = (f32[8,64,128]{2,1,0:T(8,128)S(1)}, f32[8,64,128]{2,1,0:T(8,128)}, u32[]{:S(2)}) copy-start(f32[8,64,128]{2,1,0:T(8,128)} %param.17) | copy-start | bytes 786436
  83.3 3.3 %copy-start.2 = (f32[2,8,64,128]{3,2,1,0:T(8,128)S(1)}, f32[2,8,64,128]{3,2,1,0:T(8,128)}, u32[]{:S(2)}) copy-start(f32[2,8,64,128]{3,2,1,0:T(8,128)} %param.13) | copy-start | bytes 1572868
  83.3 3.2 %copy-start.4 = (f32[8,64,128]{2,1,0:T(8,128)S(1)}, f32[8,64,128]{2,1,0:T(8,128)}, u32[]{:S(2)}) copy-start(f32[8,64,128]{2,1,0:T(8,128)} %param.17) | copy-start | bytes 786436

commit v11 on v10

--- a/solution.py
+++ b/solution.py
@@ -54,13 +54,14 @@
     return exact_einsum("sya,fsjax->fsjyx", pick_y, part)
 
 
-def halo_kernel(n, send_ref, recv_ref, relay_f, relay_b, sems):
+def halo_kernel(n, bounds, send_ref, recv_ref, relay_f1, relay_f2, relay_b1, relay_b2, sems):
     lo_send, hi_send = send_ref.at[0], send_ref.at[1]
     lo_recv, hi_recv = recv_ref.at[0], recv_ref.at[1]
     i = lax.axis_index("slab")
     shot = lax.axis_index("shots")
     x = i % 4
-    part = send_ref.shape[1] // 3
+    relay_f = {1: relay_f1, 2: relay_f2}
+    relay_b = {1: relay_b1, 2: relay_b2}
     mesh_id = pl.DeviceIdType.MESH
     barrier = pltpu.get_barrier_semaphore()
     greeted = 0
@@ -75,7 +76,7 @@
     pl.semaphore_wait(barrier, greeted)
 
     def rows(p):
-        return pl.ds(p * part, part)
+        return pl.ds(bounds[p], bounds[p + 1] - bounds[p])
 
     def remote(src, dst, send, recv, target):
         return pltpu.make_async_remote_copy(
@@ -108,19 +109,19 @@
 
             @pl.when(has_up & up_far)
             def _():
-                remote(lo_send.at[rows(p)], relay_f, p, 14, i - 3 + p).start()
+                remote(lo_send.at[rows(p)], relay_f[p], p, 14, i - 3 + p).start()
 
             @pl.when(has_down & down_far)
             def _():
-                remote(hi_send.at[rows(p)], relay_b, 3 + p, 15, i + p).start()
+                remote(hi_send.at[rows(p)], relay_b[p], 3 + p, 15, i + p).start()
 
     for p in (1, 2):
         fwd = (x == p) & (i + 4 - p < n)
 
         @pl.when(fwd)
         def _():
-            remote(lo_send.at[rows(p)], relay_f, p, 14, i).wait_recv()
-            copy = remote(relay_f, lo_recv.at[rows(p)], 6, 8 + p, i + 4 - p)
+            remote(lo_send.at[rows(p)], relay_f[p], p, 14, i).wait_recv()
+            copy = remote(relay_f[p], lo_recv.at[rows(p)], 6, 8 + p, i + 4 - p)
             copy.start()
             copy.wait_send()
 
@@ -128,8 +129,8 @@
 
         @pl.when(bwd)
         def _():
-            remote(hi_send.at[rows(p)], relay_b, 3 + p, 15, i).wait_recv()
-            copy = remote(relay_b, hi_recv.at[rows(p)], 7, 11 + p, i - p - 1)
+            remote(hi_send.at[rows(p)], relay_b[p], 3 + p, 15, i).wait_recv()
+            copy = remote(relay_b[p], hi_recv.at[rows(p)], 7, 11 + p, i - p - 1)
             copy.start()
             copy.wait_send()
 
@@ -156,23 +157,24 @@
     n = lax.axis_size("slab")
     shape = both.shape
     total = both[0].size // 128
-    part = -(-total // 24) * 8
-    padded = 3 * part
-    send = jnp.pad(both.reshape(2, total, 128), ((0, 0), (0, padded - total), (0, 0)))
+    part = total // 3 // 8 * 8
+    bounds = (0, part, 2 * part, total)
     vmem = pl.BlockSpec(memory_space=pltpu.VMEM)
     recv = pl.pallas_call(
-        functools.partial(halo_kernel, n),
-        out_shape=jax.ShapeDtypeStruct((2, padded, 128), jnp.float32),
+        functools.partial(halo_kernel, n, bounds),
+        out_shape=jax.ShapeDtypeStruct((2, total, 128), jnp.float32),
         in_specs=[vmem],
         out_specs=vmem,
         scratch_shapes=[
             pltpu.VMEM((part, 128), jnp.float32),
+            pltpu.VMEM((total - 2 * part, 128), jnp.float32),
             pltpu.VMEM((part, 128), jnp.float32),
+            pltpu.VMEM((total - 2 * part, 128), jnp.float32),
             pltpu.SemaphoreType.DMA((16,)),
         ],
         compiler_params=pltpu.CompilerParams(collective_id=call_id, has_side_effects=True),
-    )(send)
-    return recv[:, :total].reshape(shape)
+    )(both.reshape(2, total, 128))
+    return recv.reshape(shape)
 
 
 def extended(block, pick_y, pick_x, width, call_id):

time: 133 us -> 131 us (0.985)
  Pallas kernels: 104 us -> 102 us
    slice x2 -> x0, local copies, waits for them, and re-layouts: 2.14 us -> none  [exchange(): return recv[:, :total].reshape(shape)]
    reshape x2, local copies, waits for them, and re-layouts: 1.23 us -> 3.3 us  [exchange(): return recv.reshape(shape)]
    pad x2 -> x0, local copies, waits for them, and re-layouts: 1.64 us -> none  [exchange(): jnp.pad(both.reshape(2, total, 128), ((0, 0), (0, padded - total), (0, 0)))]
    reshape x2, local copies, waits for them, and re-layouts: 1.05 us -> 2.67 us  [exchange(): both.reshape(2, total, 128)]
where the time goes in v11:
time: 131 us; the launch traced here: 130 us
  Pallas kernels  102 us (78%)
  other arithmetic  11.9 us (9%)
  local copies, waits for them, and re-layouts  8.42 us (6%)
  matrix products  6.63 us (5%)
    pallas_call x2, Pallas kernels, exchange(): pl.pallas_call(functools.partial(halo_kernel, n, bounds), out_shape=jax.S...  61.6 us
    pallas_call x1, Pallas kernels, shots_sum(): pl.pallas_call(functools.partial(allreduce_kernel, chips), out_shape=jax....  40.4 us
    dot_general x8, matrix products, exact_einsum(): jnp.einsum(spec, a, b, precision=lax.Precision.HIGHEST, preferred_element...  5.11 us
    add x2, other arithmetic, laplace(): total = total + COEF[shift_k] * (side_y + side_x)  4.91 us
    reshape x2, local copies, waits for them, and re-layouts, exchange(): return recv.reshape(shape)  3.3 us
    reshape x2, local copies, waits for them, and re-layouts, exchange(): both.reshape(2, total, 128)  2.67 us

profile of v11, /device:TPU:25, one launch (start us, length us, event | category | flops | bytes accessed | tf_op | source)
XLA Modules:
  0.0 130.1 jit_solution(1279406369930580748)
XLA Ops:
  0.7 1.3 %fusion.73 = (f32[1,2,2,4,64,128]{5,4,3,2,1,0:T(8,128)S(1)}, f32[1,2,2,4,64,128]{5,4,3,2,1,0:T(8,128)S(1)}) fusion(f32[1,2,8,64,128]{4,3,2,1,0:T(8,128)} %bitcast.108, f32[1,2,8,64,128]{4,3,2,1,0:T(8,128)} %bitcast.111), kind=kLoop, calls=%fused_computation.140 | loop fusion | flops 262144 | bytes 2097152 | tf_op jit(solution)/shard_map/stack | solution.py:182
  2.1 0.7 convolution_bitcast_fusion.3
  2.9 0.6 convolution_bitcast_fusion.5
  3.5 1.3 %reshape.247.send_ref = f32[2,484,128]{2,1,0:T(8,128)} reshape(f32[2,2,2,4,44,88]{5,4,3,2,1,0:T(8,128)S(1)} %copy.22) | data formatting | bytes 991232 | tf_op jit(solution)/shard_map/reshape | solution.py:176
  4.9 31.9 %shard_map.148 = f32[2,484,128]{2,1,0:T(8,128)} custom-call(f32[2,484,128]{2,1,0:T(8,128)} %reshape.247.send_ref), custom_call_target="tpu_custom_call" | custom-call | tf_op jit(solution)/shard_map/pallas_call | solution.py:163
  36.8 1.7 %reshape.248 = f32[2,2,2,4,44,88]{5,4,3,2,1,0:T(8,128)S(1)} reshape(f32[2,484,128]{2,1,0:T(8,128)} %shard_map.148) | data formatting | bytes 991232 | tf_op jit(solution)/shard_map/reshape | solution.py:177
  38.5 0.1 pad_add_fusion
  38.6 0.6 convolution_bitcast_fusion.7
  39.2 0.7 convolution_bitcast_fusion.2
  39.9 0.1 slice_bitcast_fusion.7
  40.0 0.2 copy-done
  40.2 0.2 copy-done.1
  40.4 0.4 pad_maximum_fusion
  40.9 2.5 %fusion.6 = f32[2,2,8,64,128]{4,3,2,1,0:T(8,128)S(1)} fusion(f32[2,2,8,64,128]{4,3,2,1,0:T(8,128)S(1)} %pad_maximum_fusion.2, f32[2,2,12,64,128]{4,3,2,1,0:T(8,128)S(1)} %get-tuple-element.19, f32[2,2,12,64,128]{4,3,2,1,0:T(8,128)S(1)} %get-tuple-element.18), kind=kLoop, calls=%fused_computation.60 | loop fusion | flops 8650752 | bytes 10485760 | tf_op jit(solution)/shard_map/add | solution.py:221
  43.4 0.8 fusion.60
  44.5 0.1 and_convert_fusion
  44.7 1.7 %fusion.85 = (f32[2,8,64,128]{3,2,1,0:T(8,128)S(1)}, f32[2,8,64,128]{3,2,1,0:T(8,128)S(1)}) fusion(f32[2,8,64,128]{3,2,1,0:T(8,128)S(1)} %bitcast.122, f32[2,2,8,64,128]{4,3,2,1,0:T(8,128)S(1)} %fusion.6, f32[2,8,64,128]{3,2,1,0:T(8,128)} %param.15, f32[2,8,64,128]{3,2,1,0:T(8,128)S(1)} %copy-done.1, f32[8,64,128]{2,1,0:T(8,128)S(1)} %copy-done.3, ...), kind=kLoop, calls=%fused_computation.157 | loop fusion | flops 1835008 | bytes 5047560 | tf_op jit(solution)/shard_map/mul | solution.py:407
  46.4 0.6 convolution_bitcast_fusion.1
  47.1 0.6 convolution_bitcast_fusion.4
  47.7 1.3 %reshape.250.send_ref = f32[2,484,128]{2,1,0:T(8,128)} reshape(f32[2,2,2,4,44,88]{5,4,3,2,1,0:T(8,128)S(1)} %copy.25) | data formatting | bytes 991232 | tf_op jit(solution)/shard_map/reshape | solution.py:176
  49.1 29.7 %shard_map.149 = f32[2,484,128]{2,1,0:T(8,128)} custom-call(f32[2,484,128]{2,1,0:T(8,128)} %reshape.250.send_ref), custom_call_target="tpu_custom_call" | custom-call | tf_op jit(solution)/shard_map/pallas_call | solution.py:163
  78.8 1.7 %reshape.251 = f32[2,2,2,4,44,88]{5,4,3,2,1,0:T(8,128)S(1)} reshape(f32[2,484,128]{2,1,0:T(8,128)} %shard_map.149) | data formatting | bytes 991232 | tf_op jit(solution)/shard_map/reshape | solution.py:177
  80.5 0.6 convolution_bitcast_fusion.6
  81.1 0.7 convolution_bitcast_fusion
  81.8 0.1 slice_bitcast_fusion.3
  81.9 0.4 pad_maximum_fusion.1
  82.4 2.5 %fusion.26 = f32[2,2,8,64,128]{4,3,2,1,0:T(8,128)S(1)} fusion(f32[2,2,8,64,128]{4,3,2,1,0:T(8,128)S(1)} %pad_maximum_fusion.3, f32[2,2,12,64,128]{4,3,2,1,0:T(8,128)S(1)} %get-tuple-element.13, f32[2,2,12,64,128]{4,3,2,1,0:T(8,128)S(1)} %get-tuple-element.12), kind=kLoop, calls=%fused_computation.80 | loop fusion | flops 8650752 | bytes 10485760 | tf_op jit(solution)/shard_map/add | solution.py:221
  84.8 0.8 fusion.58
  85.6 1.7 %multiply_reduce_fusion = (f32[8,64,128]{2,1,0:T(8,128)S(1)}, f32[8,64,128]{2,1,0:T(8,128)S(1)}, f32[2,8,64,128]{3,2,1,0:T(8,128)}, f32[2,8,64,128]{3,2,1,0:T(8,128)}) fusion(f32[2,8,64,128]{3,2,1,0:T(8,128)S(1)} %copy-done, f32[2,8,64,128]{3,2,1,0:T(8,128)S(1)} %get-tuple-element.11, f32[2,8,64,128]{3,2,1,0:T(8,128)S(1)} %get-tuple-element.10, ...), kind=kLoop, calls=%fused_computation.163 | loop fusion | flops 2883584 | bytes 6096136 | tf_op jit(solution)/shard_map/reduce_sum | solution.py:408
  87.3 0.7 add.297
  88.0 40.4 %shard_map.150 = f32[512,128]{1,0:T(8,128)} custom-call(f32[512,128]{1,0:T(8,128)} %bitcast.120), custom_call_target="tpu_custom_call" | custom-call | tf_op jit(solution)/shard_map/pallas_call | solution.py:359
  128.4 1.7 %copy.51 = f32[8,64,128]{2,1,0:T(8,128)} copy(f32[8,64,128]{2,1,0:T(8,128)} %bitcast.121) | data formatting | bytes 524288
  (40 shorter events, 0.9 us)
Async XLA Ops:
  0.6 1.4 %copy-start.9 = (s32[2]{0:T(128)S(1)}, s32[2]{0:T(128)}, u32[]{:S(2)}) copy-start(s32[2]{0:T(128)} %param.22) | copy-start | bytes 28
  0.6 1.4 %copy-start.10 = (s32[2]{0:T(128)S(1)}, s32[2]{0:T(128)}, u32[]{:S(2)}) copy-start(s32[2]{0:T(128)} %param.24) | copy-start | bytes 28
  2.0 0.8 copy-start.7
  2.0 0.8 copy-start.8
  39.2 1.0 copy-start
  39.2 1.2 copy-start.1
  40.8 2.5 %copy-start.5 = (s32[2,256]{1,0:T(2,128)S(1)}, s32[2,256]{1,0:T(2,128)}, u32[]{:S(2)}) copy-start(s32[2,256]{1,0:T(2,128)} %param.25) | copy-start | bytes 6148
  40.9 2.6 %copy-start.4 = (f32[2,2,256]{2,1,0:T(2,128)S(1)}, f32[2,2,256]{2,1,0:T(2,128)}, u32[]{:S(2)}) copy-start(f32[2,2,256]{2,1,0:T(2,128)} %param.19) | copy-start | bytes 12292
  40.9 3.3 %copy-start.11 = (s32[2]{0:T(128)S(1)}, s32[2]{0:T(128)}, u32[]{:S(2)}) copy-start(s32[2]{0:T(128)} %param.20) | copy-start | bytes 28
  40.9 3.7 %copy-start.6 = (f32[2,2]{1,0:T(2,128)S(1)}, f32[2,2]{1,0:T(2,128)}, u32[]{:S(2)}) copy-start(f32[2,2]{1,0:T(2,128)} %param.18) | copy-start | bytes 52
  40.9 3.7 %copy-start.3 = (f32[8,64,128]{2,1,0:T(8,128)S(1)}, f32[8,64,128]{2,1,0:T(8,128)}, u32[]{:S(2)}) copy-start(f32[8,64,128]{2,1,0:T(8,128)} %param.17) | copy-start | bytes 786436
  82.4 3.2 %copy-start.2 = (f32[2,8,64,128]{3,2,1,0:T(8,128)S(1)}, f32[2,8,64,128]{3,2,1,0:T(8,128)}, u32[]{:S(2)}) copy-start(f32[2,8,64,128]{3,2,1,0:T(8,128)} %param.13) | copy-start | bytes 1572868

commit v12 on v11

--- a/solution.py
+++ b/solution.py
@@ -54,124 +54,64 @@
     return exact_einsum("sya,fsjax->fsjyx", pick_y, part)
 
 
-def halo_kernel(n, bounds, send_ref, recv_ref, relay_f1, relay_f2, relay_b1, relay_b2, sems):
-    lo_send, hi_send = send_ref.at[0], send_ref.at[1]
-    lo_recv, hi_recv = recv_ref.at[0], recv_ref.at[1]
+def halo_kernel(n, send_ref, recv_ref, sems):
     i = lax.axis_index("slab")
     shot = lax.axis_index("shots")
-    x = i % 4
-    relay_f = {1: relay_f1, 2: relay_f2}
-    relay_b = {1: relay_b1, 2: relay_b2}
     mesh_id = pl.DeviceIdType.MESH
+    has_up = i + 1 < n
+    has_down = i >= 1
     barrier = pltpu.get_barrier_semaphore()
-    greeted = 0
-    for d in (-3, -2, -1, 1, 2, 3):
-        ok = (i + d >= 0) & (i + d < n)
-
-        @pl.when(ok)
-        def _():
-            pl.semaphore_signal(barrier, inc=1, device_id=(i + d, shot), device_id_type=mesh_id)
-
-        greeted = greeted + ok.astype(jnp.int32)
-    pl.semaphore_wait(barrier, greeted)
-
-    def rows(p):
-        return pl.ds(bounds[p], bounds[p + 1] - bounds[p])
-
-    def remote(src, dst, send, recv, target):
+
+    @pl.when(has_up)
+    def _():
+        pl.semaphore_signal(barrier, inc=1, device_id=(i + 1, shot), device_id_type=mesh_id)
+
+    @pl.when(has_down)
+    def _():
+        pl.semaphore_signal(barrier, inc=1, device_id=(i - 1, shot), device_id_type=mesh_id)
+
+    pl.semaphore_wait(barrier, has_up.astype(jnp.int32) + has_down.astype(jnp.int32))
+
+    def remote(side, target):
         return pltpu.make_async_remote_copy(
-            src_ref=src,
-            dst_ref=dst,
-            send_sem=sems.at[send],
-            recv_sem=sems.at[recv],
+            src_ref=send_ref.at[side],
+            dst_ref=recv_ref.at[side],
+            send_sem=sems.at[side],
+            recv_sem=sems.at[2 + side],
             device_id=(target, shot),
             device_id_type=mesh_id,
         )
 
-    has_up = i + 1 < n
-    has_down = i >= 1
-    up_far = x == 3
-    down_far = x == 0
-    for p in range(3):
-        direct_up = has_up if p == 0 else has_up & jnp.logical_not(up_far)
-
-        @pl.when(direct_up)
-        def _():
-            remote(lo_send.at[rows(p)], lo_recv.at[rows(p)], p, 8 + p, i + 1).start()
-
-        direct_down = has_down if p == 0 else has_down & jnp.logical_not(down_far)
-
-        @pl.when(direct_down)
-        def _():
-            remote(hi_send.at[rows(p)], hi_recv.at[rows(p)], 3 + p, 11 + p, i - 1).start()
-
-        if p > 0:
-
-            @pl.when(has_up & up_far)
-            def _():
-                remote(lo_send.at[rows(p)], relay_f[p], p, 14, i - 3 + p).start()
-
-            @pl.when(has_down & down_far)
-            def _():
-                remote(hi_send.at[rows(p)], relay_b[p], 3 + p, 15, i + p).start()
-
-    for p in (1, 2):
-        fwd = (x == p) & (i + 4 - p < n)
-
-        @pl.when(fwd)
-        def _():
-            remote(lo_send.at[rows(p)], relay_f[p], p, 14, i).wait_recv()
-            copy = remote(relay_f[p], lo_recv.at[rows(p)], 6, 8 + p, i + 4 - p)
-            copy.start()
-            copy.wait_send()
-
-        bwd = (x == p) & (i - p >= 1)
-
-        @pl.when(bwd)
-        def _():
-            remote(hi_send.at[rows(p)], relay_b[p], 3 + p, 15, i).wait_recv()
-            copy = remote(relay_b[p], hi_recv.at[rows(p)], 7, 11 + p, i - p - 1)
-            copy.start()
-            copy.wait_send()
-
-    for p in range(3):
-
-        @pl.when(has_up)
-        def _():
-            remote(lo_send.at[rows(p)], lo_recv.at[rows(p)], p, 8 + p, i + 1).wait_send()
-
-        @pl.when(has_down)
-        def _():
-            remote(hi_send.at[rows(p)], hi_recv.at[rows(p)], 3 + p, 11 + p, i - 1).wait_send()
-
-        @pl.when(has_down)
-        def _():
-            remote(lo_send.at[rows(p)], lo_recv.at[rows(p)], p, 8 + p, i).wait_recv()
-
-        @pl.when(has_up)
-        def _():
-            remote(hi_send.at[rows(p)], hi_recv.at[rows(p)], 3 + p, 11 + p, i).wait_recv()
+    @pl.when(has_up)
+    def _():
+        remote(0, i + 1).start()
+
+    @pl.when(has_down)
+    def _():
+        remote(1, i - 1).start()
+
+    @pl.when(has_up)
+    def _():
+        remote(0, i + 1).wait_send()
+        remote(1, i).wait_recv()
+
+    @pl.when(has_down)
+    def _():
+        remote(1, i - 1).wait_send()
+        remote(0, i).wait_recv()
 
 
 def exchange(both, call_id):
     n = lax.axis_size("slab")
     shape = both.shape
     total = both[0].size // 128
-    part = total // 3 // 8 * 8
-    bounds = (0, part, 2 * part, total)
     vmem = pl.BlockSpec(memory_space=pltpu.VMEM)
     recv = pl.pallas_call(
-        functools.partial(halo_kernel, n, bounds),
+        functools.partial(halo_kernel, n),
         out_shape=jax.ShapeDtypeStruct((2, total, 128), jnp.float32),
         in_specs=[vmem],
         out_specs=vmem,
-        scratch_shapes=[
-            pltpu.VMEM((part, 128), jnp.float32),
-            pltpu.VMEM((total - 2 * part, 128), jnp.float32),
-            pltpu.VMEM((part, 128), jnp.float32),
-            pltpu.VMEM((total - 2 * part, 128), jnp.float32),
-            pltpu.SemaphoreType.DMA((16,)),
-        ],
+        scratch_shapes=[pltpu.SemaphoreType.DMA((4,))],
         compiler_params=pltpu.CompilerParams(collective_id=call_id, has_side_effects=True),
     )(both.reshape(2, total, 128))
     return recv.reshape(shape)

time: 131 us -> 127 us (0.969)
  Pallas kernels: 102 us -> 98.6 us
    pallas_call x2, Pallas kernels: 61.6 us -> 43.8 us  [exchange(): pl.pallas_call(functools.partial(halo_kernel, n), out_shape=jax.ShapeDtyp...]
    pallas_call x1, Pallas kernels: 40.4 us -> 54.8 us  [shots_sum(): pl.pallas_call(functools.partial(allreduce_kernel, chips), out_shape=jax....]
where the time goes in v12:
time: 127 us
  Pallas kernels  98.6 us (78%)
  other arithmetic  11.9 us (9%)
  local copies, waits for them, and re-layouts  8.42 us (7%)
  matrix products  6.63 us (5%)
    pallas_call x1, Pallas kernels, shots_sum(): pl.pallas_call(functools.partial(allreduce_kernel, chips), out_shape=jax....  54.8 us
    pallas_call x2, Pallas kernels, exchange(): pl.pallas_call(functools.partial(halo_kernel, n), out_shape=jax.ShapeDtyp...  43.8 us
    dot_general x8, matrix products, exact_einsum(): jnp.einsum(spec, a, b, precision=lax.Precision.HIGHEST, preferred_element...  5.11 us
    add x2, other arithmetic, laplace(): total = total + COEF[shift_k] * (side_y + side_x)  4.91 us
    reshape x2, local copies, waits for them, and re-layouts, exchange(): return recv.reshape(shape)  3.3 us
    reshape x2, local copies, waits for them, and re-layouts, exchange(): both.reshape(2, total, 128)  2.67 us

profile of v12, /device:TPU:25, one launch (start us, length us, event | category | flops | bytes accessed | tf_op | source)
XLA Modules:
  0.0 126.6 jit_solution(8894445191618128025)
XLA Ops:
  0.7 1.3 %fusion.73 = (f32[1,2,2,4,64,128]{5,4,3,2,1,0:T(8,128)S(1)}, f32[1,2,2,4,64,128]{5,4,3,2,1,0:T(8,128)S(1)}) fusion(f32[1,2,8,64,128]{4,3,2,1,0:T(8,128)} %bitcast.108, f32[1,2,8,64,128]{4,3,2,1,0:T(8,128)} %bitcast.111), kind=kLoop, calls=%fused_computation.140 | loop fusion | flops 262144 | bytes 2097152 | tf_op jit(solution)/shard_map/stack | solution.py:122
  2.1 0.7 convolution_bitcast_fusion.3
  2.9 0.6 convolution_bitcast_fusion.5
  3.5 1.3 %reshape.247.send_ref = f32[2,484,128]{2,1,0:T(8,128)} reshape(f32[2,2,2,4,44,88]{5,4,3,2,1,0:T(8,128)S(1)} %copy.22) | data formatting | bytes 991232 | tf_op jit(solution)/shard_map/reshape | solution.py:116
  4.9 24.4 %shard_map.148 = f32[2,484,128]{2,1,0:T(8,128)} custom-call(f32[2,484,128]{2,1,0:T(8,128)} %reshape.247.send_ref), custom_call_target="tpu_custom_call" | custom-call | tf_op jit(solution)/shard_map/pallas_call | solution.py:109
  29.3 1.7 %reshape.248 = f32[2,2,2,4,44,88]{5,4,3,2,1,0:T(8,128)S(1)} reshape(f32[2,484,128]{2,1,0:T(8,128)} %shard_map.148) | data formatting | bytes 991232 | tf_op jit(solution)/shard_map/reshape | solution.py:117
  31.0 0.1 pad_add_fusion
  31.0 0.6 convolution_bitcast_fusion.7
  31.7 0.7 convolution_bitcast_fusion.2
  32.4 0.1 slice_bitcast_fusion.7
  32.5 0.2 copy-done
  32.7 0.2 copy-done.1
  32.9 0.4 pad_maximum_fusion
  33.4 2.5 %fusion.6 = f32[2,2,8,64,128]{4,3,2,1,0:T(8,128)S(1)} fusion(f32[2,2,8,64,128]{4,3,2,1,0:T(8,128)S(1)} %pad_maximum_fusion.2, f32[2,2,12,64,128]{4,3,2,1,0:T(8,128)S(1)} %get-tuple-element.19, f32[2,2,12,64,128]{4,3,2,1,0:T(8,128)S(1)} %get-tuple-element.18), kind=kLoop, calls=%fused_computation.60 | loop fusion | flops 8650752 | bytes 10485760 | tf_op jit(solution)/shard_map/add | solution.py:161
  35.9 0.8 fusion.60
  37.0 0.1 and_convert_fusion
  37.1 1.7 %fusion.85 = (f32[2,8,64,128]{3,2,1,0:T(8,128)S(1)}, f32[2,8,64,128]{3,2,1,0:T(8,128)S(1)}) fusion(f32[2,8,64,128]{3,2,1,0:T(8,128)S(1)} %bitcast.122, f32[2,2,8,64,128]{4,3,2,1,0:T(8,128)S(1)} %fusion.6, f32[2,8,64,128]{3,2,1,0:T(8,128)} %param.15, f32[2,8,64,128]{3,2,1,0:T(8,128)S(1)} %copy-done.1, f32[8,64,128]{2,1,0:T(8,128)S(1)} %copy-done.3, ...), kind=kLoop, calls=%fused_computation.157 | loop fusion | flops 1835008 | bytes 5047560 | tf_op jit(solution)/shard_map/mul | solution.py:347
  38.9 0.6 convolution_bitcast_fusion.1
  39.6 0.6 convolution_bitcast_fusion.4
  40.2 1.3 %reshape.250.send_ref = f32[2,484,128]{2,1,0:T(8,128)} reshape(f32[2,2,2,4,44,88]{5,4,3,2,1,0:T(8,128)S(1)} %copy.25) | data formatting | bytes 991232 | tf_op jit(solution)/shard_map/reshape | solution.py:116
  41.6 19.3 %shard_map.149 = f32[2,484,128]{2,1,0:T(8,128)} custom-call(f32[2,484,128]{2,1,0:T(8,128)} %reshape.250.send_ref), custom_call_target="tpu_custom_call" | custom-call | tf_op jit(solution)/shard_map/pallas_call | solution.py:109
  60.9 1.7 %reshape.251 = f32[2,2,2,4,44,88]{5,4,3,2,1,0:T(8,128)S(1)} reshape(f32[2,484,128]{2,1,0:T(8,128)} %shard_map.149) | data formatting | bytes 991232 | tf_op jit(solution)/shard_map/reshape | solution.py:117
  62.6 0.6 convolution_bitcast_fusion.6
  63.2 0.7 convolution_bitcast_fusion
  63.9 0.1 slice_bitcast_fusion.3
  64.0 0.4 pad_maximum_fusion.1
  64.5 2.5 %fusion.26 = f32[2,2,8,64,128]{4,3,2,1,0:T(8,128)S(1)} fusion(f32[2,2,8,64,128]{4,3,2,1,0:T(8,128)S(1)} %pad_maximum_fusion.3, f32[2,2,12,64,128]{4,3,2,1,0:T(8,128)S(1)} %get-tuple-element.13, f32[2,2,12,64,128]{4,3,2,1,0:T(8,128)S(1)} %get-tuple-element.12), kind=kLoop, calls=%fused_computation.80 | loop fusion | flops 8650752 | bytes 10485760 | tf_op jit(solution)/shard_map/add | solution.py:161
  67.0 0.8 fusion.58
  67.7 1.7 %multiply_reduce_fusion = (f32[8,64,128]{2,1,0:T(8,128)S(1)}, f32[8,64,128]{2,1,0:T(8,128)S(1)}, f32[2,8,64,128]{3,2,1,0:T(8,128)}, f32[2,8,64,128]{3,2,1,0:T(8,128)}) fusion(f32[2,8,64,128]{3,2,1,0:T(8,128)S(1)} %copy-done, f32[2,8,64,128]{3,2,1,0:T(8,128)S(1)} %get-tuple-element.11, f32[2,8,64,128]{3,2,1,0:T(8,128)S(1)} %get-tuple-element.10, ...), kind=kLoop, calls=%fused_computation.163 | loop fusion | flops 2883584 | bytes 6096136 | tf_op jit(solution)/shard_map/reduce_sum | solution.py:348
  69.4 0.7 add.297
  70.1 54.8 %shard_map.150 = f32[512,128]{1,0:T(8,128)} custom-call(f32[512,128]{1,0:T(8,128)} %bitcast.120), custom_call_target="tpu_custom_call" | custom-call | tf_op jit(solution)/shard_map/pallas_call | solution.py:299
  125.0 1.7 %copy.51 = f32[8,64,128]{2,1,0:T(8,128)} copy(f32[8,64,128]{2,1,0:T(8,128)} %bitcast.121) | data formatting | bytes 524288
  (40 shorter events, 0.9 us)
Async XLA Ops:
  0.6 1.4 %copy-start.9 = (s32[2]{0:T(128)S(1)}, s32[2]{0:T(128)}, u32[]{:S(2)}) copy-start(s32[2]{0:T(128)} %param.22) | copy-start | bytes 28
  0.6 1.4 %copy-start.10 = (s32[2]{0:T(128)S(1)}, s32[2]{0:T(128)}, u32[]{:S(2)}) copy-start(s32[2]{0:T(128)} %param.24) | copy-start | bytes 28
  2.0 0.8 copy-start.7
  2.0 0.8 copy-start.8
  31.7 1.0 copy-start
  31.7 1.2 copy-start.1
  33.3 2.5 %copy-start.5 = (s32[2,256]{1,0:T(2,128)S(1)}, s32[2,256]{1,0:T(2,128)}, u32[]{:S(2)}) copy-start(s32[2,256]{1,0:T(2,128)} %param.25) | copy-start | bytes 6148
  33.4 2.6 %copy-start.4 = (f32[2,2,256]{2,1,0:T(2,128)S(1)}, f32[2,2,256]{2,1,0:T(2,128)}, u32[]{:S(2)}) copy-start(f32[2,2,256]{2,1,0:T(2,128)} %param.19) | copy-start | bytes 12292
  33.4 3.3 %copy-start.11 = (s32[2]{0:T(128)S(1)}, s32[2]{0:T(128)}, u32[]{:S(2)}) copy-start(s32[2]{0:T(128)} %param.20) | copy-start | bytes 28
  33.4 3.7 %copy-start.6 = (f32[2,2]{1,0:T(2,128)S(1)}, f32[2,2]{1,0:T(2,128)}, u32[]{:S(2)}) copy-start(f32[2,2]{1,0:T(2,128)} %param.18) | copy-start | bytes 52
  33.4 3.7 %copy-start.3 = (f32[8,64,128]{2,1,0:T(8,128)S(1)}, f32[8,64,128]{2,1,0:T(8,128)}, u32[]{:S(2)}) copy-start(f32[8,64,128]{2,1,0:T(8,128)} %param.17) | copy-start | bytes 786436
  64.5 3.2 %copy-start.2 = (f32[2,8,64,128]{3,2,1,0:T(8,128)S(1)}, f32[2,8,64,128]{3,2,1,0:T(8,128)}, u32[]{:S(2)}) copy-start(f32[2,8,64,128]{3,2,1,0:T(8,128)} %param.13) | copy-start | bytes 1572868

commit v13 on v12

--- a/solution.py
+++ b/solution.py
@@ -345,13 +345,13 @@
         rdelta = receiver_field(receiver_cell, residual_traces[step], start, depth, rows_y, cols_x)
         unew = mask * (2.0 * u - up + velocity * lap[0] + sdelta)
         vnew = mask * (2.0 * v - vp + velocity * lap[1] + rdelta)
-        terms.append(jnp.sum((unew - 2.0 * u + up) * vnew, axis=0))
+        terms.append((unew - 2.0 * u + up) * vnew)
         up, u, vp, v = (u, unew, v, vnew)
     src_last, rcv_last = (u, v)
     local_sum = terms[0]
     for extra in terms[1:]:
         local_sum = local_sum + extra
-    image = shots_sum(local_sum)
+    image = shots_sum(jnp.sum(local_sum, axis=0))
     return (src_last, rcv_last, image)
 
 

time: 127 us -> 131 us (1.031)
  local copies, waits for them, and re-layouts: 8.42 us -> 11.3 us
    mul x1 -> x0, other arithmetic: 1.68 us -> none  [per_device(): vnew = mask * (2.0 * v - vp + velocity * lap[1] + rdelta)]
    another operation x2 -> x3, other arithmetic: 0.14 us -> 1.82 us  [per_device(): stacked = jnp.stack([u, v])]
where the time goes in v13:
time: 131 us
  Pallas kernels  98.6 us (75%)
  other arithmetic  11.8 us (9%)
  local copies, waits for them, and re-layouts  11.3 us (9%)
  matrix products  7.75 us (6%)
    pallas_call x1, Pallas kernels, shots_sum(): pl.pallas_call(functools.partial(allreduce_kernel, chips), out_shape=jax....  54.8 us
    pallas_call x2, Pallas kernels, exchange(): pl.pallas_call(functools.partial(halo_kernel, n), out_shape=jax.ShapeDtyp...  43.8 us
    dot_general x8, matrix products, exact_einsum(): jnp.einsum(spec, a, b, precision=lax.Precision.HIGHEST, preferred_element...  6.23 us
    add x2, other arithmetic, laplace(): total = total + COEF[shift_k] * (side_y + side_x)  4.91 us
    reshape x2, local copies, waits for them, and re-layouts, exchange(): return recv.reshape(shape)  4.2 us
    reshape x2, local copies, waits for them, and re-layouts, exchange(): both.reshape(2, total, 128)  3.77 us

profile of v13, /device:TPU:25, one launch (start us, length us, event | category | flops | bytes accessed | tf_op | source)
XLA Modules:
  0.0 130.5 jit_solution(4829979623849828963)
XLA Ops:
  0.7 1.3 fusion.73
  2.1 0.7 convolution_bitcast_fusion.3
  2.9 0.6 convolution_bitcast_fusion.5
  3.5 1.3 %reshape.246.send_ref = f32[2,484,128]{2,1,0:T(8,128)} reshape(f32[2,2,2,4,44,88]{5,4,3,2,1,0:T(8,128)S(1)} %copy.22) | data formatting | bytes 991232 | tf_op jit(solution)/shard_map/reshape | solution.py:116
  4.9 24.4 %shard_map.148 = f32[2,484,128]{2,1,0:T(8,128)} custom-call(f32[2,484,128]{2,1,0:T(8,128)} %reshape.246.send_ref), custom_call_target="tpu_custom_call" | custom-call | tf_op jit(solution)/shard_map/pallas_call | solution.py:109
  29.3 1.7 %reshape.247 = f32[2,2,2,4,44,88]{5,4,3,2,1,0:T(8,128)S(1)} reshape(f32[2,484,128]{2,1,0:T(8,128)} %shard_map.148) | data formatting | bytes 991232 | tf_op jit(solution)/shard_map/reshape | solution.py:117
  31.0 0.1 pad_add_fusion
  31.0 0.6 convolution_bitcast_fusion.7
  31.7 0.7 convolution_bitcast_fusion.2
  32.4 0.1 slice_bitcast_fusion.7
  32.5 0.2 copy-done
  32.7 0.2 copy-done.1
  32.9 0.4 pad_maximum_fusion
  33.4 2.5 %fusion.6 = f32[2,2,8,64,128]{4,3,2,1,0:T(8,128)S(1)} fusion(f32[2,2,8,64,128]{4,3,2,1,0:T(8,128)S(1)} %pad_maximum_fusion.2, f32[2,2,12,64,128]{4,3,2,1,0:T(8,128)S(1)} %get-tuple-element.18, f32[2,2,12,64,128]{4,3,2,1,0:T(8,128)S(1)} %get-tuple-element.17), kind=kLoop, calls=%fused_computation.60 | loop fusion | flops 8650752 | bytes 10485760 | tf_op jit(solution)/shard_map/add | solution.py:161
  35.9 0.8 fusion.60
  37.0 0.1 and_convert_fusion
  37.1 1.7 %fusion.116 = (f32[1,2,8,64,128]{4,3,2,1,0:T(8,128)S(1)}, f32[2,8,64,128]{3,2,1,0:T(8,128)S(1)}) fusion(f32[2]{0:T(128)S(1)} %get-tuple-element.26, pred[2,128]{1,0:T(4,128)(4,1)S(1)} %get-tuple-element.29, pred[2,8,64]{2,1,0:T(8,128)(4,1)S(1)} %broadcast_and_fusion, f32[2,2,8,64,128]{4,3,2,1,0:T(8,128)S(1)} %fusion.6, f32[8,64,128]{2,1,0:T(8,128)S(1)} %copy-done.3, ...), kind=kLoop, calls=%fused_computation.217 | loop fusion | flops 1835008 | bytes 5047560 | tf_op jit(solution)/shard_map/stack | solution.py:339
  38.9 0.7 convolution_bitcast_fusion.1
  39.5 0.6 convolution_bitcast_fusion.4
  40.1 0.9 copy.25
  41.1 2.4 %reshape.249.send_ref = f32[2,484,128]{2,1,0:T(8,128)} reshape(f32[2,2,2,4,44,88]{5,4,3,2,1,0:T(8,128)} %copy.25) | data formatting | bytes 991232 | tf_op jit(solution)/shard_map/reshape | solution.py:116
  43.5 19.3 %shard_map.149 = f32[2,484,128]{2,1,0:T(8,128)} custom-call(f32[2,484,128]{2,1,0:T(8,128)} %reshape.249.send_ref), custom_call_target="tpu_custom_call" | custom-call | tf_op jit(solution)/shard_map/pallas_call | solution.py:109
  62.9 2.5 %reshape.250 = f32[2,2,2,4,44,88]{5,4,3,2,1,0:T(8,128)} reshape(f32[2,484,128]{2,1,0:T(8,128)} %shard_map.149) | data formatting | bytes 991232 | tf_op jit(solution)/shard_map/reshape | solution.py:117
  65.4 1.7 %convolution_bitcast_fusion.6 = f32[2,2,2,4,44,128]{5,4,3,1,0,2:T(8,128)S(1)} fusion(s32[2,88]{1,0:T(2,128)S(1)} %iota_add_fusion.1, f32[2,2,2,4,44,88]{5,4,3,2,1,0:T(8,128)} %reshape.250, pred[2]{0:T(512)(128)(4,1)S(1)} %pad_add_fusion), kind=kOutput, calls=%fused_computation.52 | convolution fusion | flops 190462976 | bytes 1217218 | tf_op jit(solution)/shard_map/zfsjab,sbx->zfsjax/dot_general | solution.py:38
  67.2 0.7 convolution_bitcast_fusion
  67.9 0.1 slice_bitcast_fusion.3
  68.0 0.4 pad_maximum_fusion.1
  68.4 2.5 %fusion.26 = f32[2,2,8,64,128]{4,3,2,1,0:T(8,128)S(1)} fusion(f32[2,2,8,64,128]{4,3,2,1,0:T(8,128)S(1)} %pad_maximum_fusion.3, f32[2,2,12,64,128]{4,3,2,1,0:T(8,128)S(1)} %get-tuple-element.12, f32[2,2,12,64,128]{4,3,2,1,0:T(8,128)S(1)} %get-tuple-element.11), kind=kLoop, calls=%fused_computation.80 | loop fusion | flops 8650752 | bytes 10485760 | tf_op jit(solution)/shard_map/add | solution.py:161
  70.9 0.8 fusion.58
  71.7 2.3 %add_reduce_fusion = (f32[8,64,128]{2,1,0:T(8,128)}, f32[2,8,64,128]{3,2,1,0:T(8,128)}, f32[2,8,64,128]{3,2,1,0:T(8,128)}) fusion(f32[2,8,64,128]{3,2,1,0:T(8,128)S(1)} %copy-done, f32[2,8,64,128]{3,2,1,0:T(8,128)S(1)} %get-tuple-element.10, f32[2,8,64,128]{3,2,1,0:T(8,128)S(1)} %copy-done.2, f32[2]{0:T(128)S(1)} %get-tuple-element.26, ...), kind=kLoop, calls=%fused_computation.163 | loop fusion | flops 3735552 | bytes 5834000 | tf_op jit(solution)/shard_map/reduce_sum | solution.py:354
  74.0 54.8 %shard_map.150 = f32[512,128]{1,0:T(8,128)} custom-call(f32[512,128]{1,0:T(8,128)} %bitcast.125), custom_call_target="tpu_custom_call" | custom-call | tf_op jit(solution)/shard_map/pallas_call | solution.py:299
  128.8 1.7 %copy.51 = f32[8,64,128]{2,1,0:T(8,128)} copy(f32[8,64,128]{2,1,0:T(8,128)} %bitcast.126) | data formatting | bytes 524288
  (39 shorter events, 0.8 us)
Async XLA Ops:
  0.6 1.4 %copy-start.9 = (s32[2]{0:T(128)S(1)}, s32[2]{0:T(128)}, u32[]{:S(2)}) copy-start(s32[2]{0:T(128)} %param.22) | copy-start | bytes 28
  0.6 1.4 %copy-start.10 = (s32[2]{0:T(128)S(1)}, s32[2]{0:T(128)}, u32[]{:S(2)}) copy-start(s32[2]{0:T(128)} %param.24) | copy-start | bytes 28
  2.0 0.8 copy-start.7
  2.0 0.8 copy-start.8
  31.7 1.0 copy-start
  31.7 1.2 copy-start.1
  33.3 2.5 %copy-start.5 = (s32[2,256]{1,0:T(2,128)S(1)}, s32[2,256]{1,0:T(2,128)}, u32[]{:S(2)}) copy-start(s32[2,256]{1,0:T(2,128)} %param.25) | copy-start | bytes 6148
  33.3 2.6 %copy-start.4 = (f32[2,2,256]{2,1,0:T(2,128)S(1)}, f32[2,2,256]{2,1,0:T(2,128)}, u32[]{:S(2)}) copy-start(f32[2,2,256]{2,1,0:T(2,128)} %param.19) | copy-start | bytes 12292
  33.3 3.3 %copy-start.11 = (s32[2]{0:T(128)S(1)}, s32[2]{0:T(128)}, u32[]{:S(2)}) copy-start(s32[2]{0:T(128)} %param.20) | copy-start | bytes 28
  33.4 3.7 %copy-start.6 = (f32[2,2]{1,0:T(2,128)S(1)}, f32[2,2]{1,0:T(2,128)}, u32[]{:S(2)}) copy-start(f32[2,2]{1,0:T(2,128)} %param.18) | copy-start | bytes 52
  33.4 3.7 %copy-start.3 = (f32[8,64,128]{2,1,0:T(8,128)S(1)}, f32[8,64,128]{2,1,0:T(8,128)}, u32[]{:S(2)}) copy-start(f32[8,64,128]{2,1,0:T(8,128)} %param.17) | copy-start | bytes 786436
  68.4 3.2 %copy-start.2 = (f32[2,8,64,128]{3,2,1,0:T(8,128)S(1)}, f32[2,8,64,128]{3,2,1,0:T(8,128)}, u32[]{:S(2)}) copy-start(f32[2,8,64,128]{3,2,1,0:T(8,128)} %param.13) | copy-start | bytes 1572868

commit v14 on v12

--- a/solution.py
+++ b/solution.py
@@ -241,9 +241,10 @@
     barrier = pltpu.get_barrier_semaphore()
     pl.semaphore_signal(barrier, inc=1, device_id=(slab, me + 1 - 2 * core), device_id_type=mesh_id)
     for k in range(1, chips):
-        peer = lax.rem(chip + k, chips) * 2 + core
-        pl.semaphore_signal(barrier, inc=1, device_id=(slab, peer), device_id_type=mesh_id)
-    pl.semaphore_wait(barrier, chips)
+        for side in (0, 1):
+            peer = lax.rem(chip + k, chips) * 2 + side
+            pl.semaphore_signal(barrier, inc=1, device_id=(slab, peer), device_id_type=mesh_id)
+    pl.semaphore_wait(barrier, 2 * chips - 1)
 
     def remote(src, dst, slot, target):
         return pltpu.make_async_remote_copy(
@@ -276,19 +277,28 @@
         total = total + gathered[k]
     out_ref[own] = total
     copies = []
-    for k in range(1, chips):
+    for k in range(chips):
         target = lax.rem(chip + k, chips)
-        copy = remote(out_ref.at[own], spread.at[k], chips + k, target * 2 + core)
-        copy.start()
-        copies.append(copy)
+        for other in (0, 1):
+            if k == 0 and other == 0:
+                continue
+            slot = k + chips * other
+            copy = remote(
+                out_ref.at[own], spread.at[slot], chips + slot, target * 2 + (core + other) % 2
+            )
+            copy.start()
+            copies.append(copy)
     for copy in copies:
         copy.wait()
-    for k in range(1, chips):
+    for k in range(chips):
         source = lax.rem(chip + chips - k, chips)
-        out_ref[pl.ds(pl.multiple_of(core * rows + source * chunk, 8), chunk)] = spread[k]
-    copy = remote(out_ref.at[mine], out_ref.at[mine], 2 * chips, me + 1 - 2 * core)
-    copy.start()
-    copy.wait()
+        for other in (0, 1):
+            if k == 0 and other == 0:
+                continue
+            half = (core + other) % 2
+            out_ref[pl.ds(pl.multiple_of(half * rows + source * chunk, 8), chunk)] = spread[
+                k + chips * other
+            ]
 
 
 def shots_sum(value):
@@ -304,9 +314,9 @@
         scratch_shapes=[
             pltpu.VMEM((rows // 2, 128), jnp.float32),
             pltpu.VMEM((chips, rows // 2 // chips, 128), jnp.float32),
-            pltpu.VMEM((chips, rows // 2 // chips, 128), jnp.float32),
-            pltpu.SemaphoreType.DMA((2 * chips + 1,)),
-            pltpu.SemaphoreType.DMA((2 * chips + 1,)),
+            pltpu.VMEM((2 * chips, rows // 2 // chips, 128), jnp.float32),
+            pltpu.SemaphoreType.DMA((3 * chips,)),
+            pltpu.SemaphoreType.DMA((3 * chips,)),
         ],
         compiler_params=pltpu.CompilerParams(collective_id=0, has_side_effects=True),
     )(chunks)

time: 127 us -> 130 us (1.024)
  Pallas kernels: 98.6 us -> 101 us
    pallas_call x1, Pallas kernels: 54.8 us -> 56.9 us  [shots_sum(): pl.pallas_call(functools.partial(allreduce_kernel, chips), out_shape=jax....]
where the time goes in v14:
time: 130 us; the launch traced here: 129 us
  Pallas kernels  101 us (78%)
  other arithmetic  11.9 us (9%)
  local copies, waits for them, and re-layouts  8.42 us (6%)
  matrix products  6.63 us (5%)
    pallas_call x1, Pallas kernels, shots_sum(): pl.pallas_call(functools.partial(allreduce_kernel, chips), out_shape=jax....  56.9 us
    pallas_call x2, Pallas kernels, exchange(): pl.pallas_call(functools.partial(halo_kernel, n), out_shape=jax.ShapeDtyp...  43.8 us
    dot_general x8, matrix products, exact_einsum(): jnp.einsum(spec, a, b, precision=lax.Precision.HIGHEST, preferred_element...  5.11 us
    add x2, other arithmetic, laplace(): total = total + COEF[shift_k] * (side_y + side_x)  4.91 us
    reshape x2, local copies, waits for them, and re-layouts, exchange(): return recv.reshape(shape)  3.3 us
    reshape x2, local copies, waits for them, and re-layouts, exchange(): both.reshape(2, total, 128)  2.67 us

profile of v14, /device:TPU:25, one launch (start us, length us, event | category | flops | bytes accessed | tf_op | source)
XLA Modules:
  0.0 128.8 jit_solution(8570418127656761239)
XLA Ops:
  0.7 1.3 %fusion.73 = (f32[1,2,2,4,64,128]{5,4,3,2,1,0:T(8,128)S(1)}, f32[1,2,2,4,64,128]{5,4,3,2,1,0:T(8,128)S(1)}) fusion(f32[1,2,8,64,128]{4,3,2,1,0:T(8,128)} %bitcast.108, f32[1,2,8,64,128]{4,3,2,1,0:T(8,128)} %bitcast.111), kind=kLoop, calls=%fused_computation.140 | loop fusion | flops 262144 | bytes 2097152 | tf_op jit(solution)/shard_map/stack | solution.py:122
  2.1 0.7 convolution_bitcast_fusion.3
  2.9 0.6 convolution_bitcast_fusion.5
  3.5 1.3 %reshape.247.send_ref = f32[2,484,128]{2,1,0:T(8,128)} reshape(f32[2,2,2,4,44,88]{5,4,3,2,1,0:T(8,128)S(1)} %copy.22) | data formatting | bytes 991232 | tf_op jit(solution)/shard_map/reshape | solution.py:116
  4.9 24.4 %shard_map.148 = f32[2,484,128]{2,1,0:T(8,128)} custom-call(f32[2,484,128]{2,1,0:T(8,128)} %reshape.247.send_ref), custom_call_target="tpu_custom_call" | custom-call | tf_op jit(solution)/shard_map/pallas_call | solution.py:109
  29.3 1.7 %reshape.248 = f32[2,2,2,4,44,88]{5,4,3,2,1,0:T(8,128)S(1)} reshape(f32[2,484,128]{2,1,0:T(8,128)} %shard_map.148) | data formatting | bytes 991232 | tf_op jit(solution)/shard_map/reshape | solution.py:117
  31.0 0.1 pad_add_fusion
  31.0 0.6 convolution_bitcast_fusion.7
  31.7 0.7 convolution_bitcast_fusion.2
  32.4 0.1 slice_bitcast_fusion.7
  32.5 0.2 copy-done
  32.7 0.2 copy-done.1
  32.9 0.4 pad_maximum_fusion
  33.4 2.5 %fusion.6 = f32[2,2,8,64,128]{4,3,2,1,0:T(8,128)S(1)} fusion(f32[2,2,8,64,128]{4,3,2,1,0:T(8,128)S(1)} %pad_maximum_fusion.2, f32[2,2,12,64,128]{4,3,2,1,0:T(8,128)S(1)} %get-tuple-element.19, f32[2,2,12,64,128]{4,3,2,1,0:T(8,128)S(1)} %get-tuple-element.18), kind=kLoop, calls=%fused_computation.60 | loop fusion | flops 8650752 | bytes 10485760 | tf_op jit(solution)/shard_map/add | solution.py:161
  35.9 0.8 fusion.60
  37.0 0.1 and_convert_fusion
  37.1 1.7 %fusion.85 = (f32[2,8,64,128]{3,2,1,0:T(8,128)S(1)}, f32[2,8,64,128]{3,2,1,0:T(8,128)S(1)}) fusion(f32[2,8,64,128]{3,2,1,0:T(8,128)S(1)} %bitcast.122, f32[2,2,8,64,128]{4,3,2,1,0:T(8,128)S(1)} %fusion.6, f32[2,8,64,128]{3,2,1,0:T(8,128)} %param.15, f32[2,8,64,128]{3,2,1,0:T(8,128)S(1)} %copy-done.1, f32[8,64,128]{2,1,0:T(8,128)S(1)} %copy-done.3, ...), kind=kLoop, calls=%fused_computation.157 | loop fusion | flops 1835008 | bytes 5047560 | tf_op jit(solution)/shard_map/mul | solution.py:357
  38.9 0.6 convolution_bitcast_fusion.1
  39.6 0.6 convolution_bitcast_fusion.4
  40.2 1.3 %reshape.250.send_ref = f32[2,484,128]{2,1,0:T(8,128)} reshape(f32[2,2,2,4,44,88]{5,4,3,2,1,0:T(8,128)S(1)} %copy.25) | data formatting | bytes 991232 | tf_op jit(solution)/shard_map/reshape | solution.py:116
  41.6 19.3 %shard_map.149 = f32[2,484,128]{2,1,0:T(8,128)} custom-call(f32[2,484,128]{2,1,0:T(8,128)} %reshape.250.send_ref), custom_call_target="tpu_custom_call" | custom-call | tf_op jit(solution)/shard_map/pallas_call | solution.py:109
  60.9 1.7 %reshape.251 = f32[2,2,2,4,44,88]{5,4,3,2,1,0:T(8,128)S(1)} reshape(f32[2,484,128]{2,1,0:T(8,128)} %shard_map.149) | data formatting | bytes 991232 | tf_op jit(solution)/shard_map/reshape | solution.py:117
  62.6 0.6 convolution_bitcast_fusion.6
  63.2 0.7 convolution_bitcast_fusion
  63.9 0.1 slice_bitcast_fusion.3
  64.0 0.4 pad_maximum_fusion.1
  64.5 2.5 %fusion.26 = f32[2,2,8,64,128]{4,3,2,1,0:T(8,128)S(1)} fusion(f32[2,2,8,64,128]{4,3,2,1,0:T(8,128)S(1)} %pad_maximum_fusion.3, f32[2,2,12,64,128]{4,3,2,1,0:T(8,128)S(1)} %get-tuple-element.13, f32[2,2,12,64,128]{4,3,2,1,0:T(8,128)S(1)} %get-tuple-element.12), kind=kLoop, calls=%fused_computation.80 | loop fusion | flops 8650752 | bytes 10485760 | tf_op jit(solution)/shard_map/add | solution.py:161
  67.0 0.8 fusion.58
  67.7 1.7 %multiply_reduce_fusion = (f32[8,64,128]{2,1,0:T(8,128)S(1)}, f32[8,64,128]{2,1,0:T(8,128)S(1)}, f32[2,8,64,128]{3,2,1,0:T(8,128)}, f32[2,8,64,128]{3,2,1,0:T(8,128)}) fusion(f32[2,8,64,128]{3,2,1,0:T(8,128)S(1)} %copy-done, f32[2,8,64,128]{3,2,1,0:T(8,128)S(1)} %get-tuple-element.11, f32[2,8,64,128]{3,2,1,0:T(8,128)S(1)} %get-tuple-element.10, ...), kind=kLoop, calls=%fused_computation.163 | loop fusion | flops 2883584 | bytes 6096136 | tf_op jit(solution)/shard_map/reduce_sum | solution.py:358
  69.4 0.7 add.297
  70.1 56.9 %shard_map.150 = f32[512,128]{1,0:T(8,128)} custom-call(f32[512,128]{1,0:T(8,128)} %bitcast.120), custom_call_target="tpu_custom_call" | custom-call | tf_op jit(solution)/shard_map/pallas_call | solution.py:309
  127.1 1.7 %copy.51 = f32[8,64,128]{2,1,0:T(8,128)} copy(f32[8,64,128]{2,1,0:T(8,128)} %bitcast.121) | data formatting | bytes 524288
  (40 shorter events, 0.9 us)
Async XLA Ops:
  0.6 1.4 %copy-start.9 = (s32[2]{0:T(128)S(1)}, s32[2]{0:T(128)}, u32[]{:S(2)}) copy-start(s32[2]{0:T(128)} %param.22) | copy-start | bytes 28
  0.6 1.4 %copy-start.10 = (s32[2]{0:T(128)S(1)}, s32[2]{0:T(128)}, u32[]{:S(2)}) copy-start(s32[2]{0:T(128)} %param.24) | copy-start | bytes 28
  2.0 0.8 copy-start.7
  2.0 0.8 copy-start.8
  31.7 1.0 copy-start
  31.7 1.2 copy-start.1
  33.3 2.5 %copy-start.5 = (s32[2,256]{1,0:T(2,128)S(1)}, s32[2,256]{1,0:T(2,128)}, u32[]{:S(2)}) copy-start(s32[2,256]{1,0:T(2,128)} %param.25) | copy-start | bytes 6148
  33.4 2.6 %copy-start.4 = (f32[2,2,256]{2,1,0:T(2,128)S(1)}, f32[2,2,256]{2,1,0:T(2,128)}, u32[]{:S(2)}) copy-start(f32[2,2,256]{2,1,0:T(2,128)} %param.19) | copy-start | bytes 12292
  33.4 3.3 %copy-start.11 = (s32[2]{0:T(128)S(1)}, s32[2]{0:T(128)}, u32[]{:S(2)}) copy-start(s32[2]{0:T(128)} %param.20) | copy-start | bytes 28
  33.4 3.7 %copy-start.6 = (f32[2,2]{1,0:T(2,128)S(1)}, f32[2,2]{1,0:T(2,128)}, u32[]{:S(2)}) copy-start(f32[2,2]{1,0:T(2,128)} %param.18) | copy-start | bytes 52
  33.4 3.7 %copy-start.3 = (f32[8,64,128]{2,1,0:T(8,128)S(1)}, f32[8,64,128]{2,1,0:T(8,128)}, u32[]{:S(2)}) copy-start(f32[8,64,128]{2,1,0:T(8,128)} %param.17) | copy-start | bytes 786436
  64.5 3.2 %copy-start.2 = (f32[2,8,64,128]{3,2,1,0:T(8,128)S(1)}, f32[2,8,64,128]{3,2,1,0:T(8,128)}, u32[]{:S(2)}) copy-start(f32[2,8,64,128]{3,2,1,0:T(8,128)} %param.13) | copy-start | bytes 1572868

commit v15 on v12

--- a/solution.py
+++ b/solution.py
@@ -105,7 +105,7 @@
     n = lax.axis_size("slab")
     shape = both.shape
     total = both[0].size // 128
-    vmem = pl.BlockSpec(memory_space=pltpu.VMEM)
+    vmem = pl.BlockSpec(memory_space=pl.ANY)
     recv = pl.pallas_call(
         functools.partial(halo_kernel, n),
         out_shape=jax.ShapeDtypeStruct((2, total, 128), jnp.float32),

time: 127 us -> 124 us (0.976)
  Pallas kernels: 98.6 us -> 95.6 us
    pallas_call x2, Pallas kernels: 43.8 us -> 40.8 us  [exchange(): pl.pallas_call(functools.partial(halo_kernel, n), out_shape=jax.ShapeDtyp...]
where the time goes in v15:
time: 124 us
  Pallas kernels  95.6 us (77%)
  other arithmetic  11.9 us (10%)
  local copies, waits for them, and re-layouts  8.42 us (7%)
  matrix products  6.63 us (5%)
    pallas_call x1, Pallas kernels, shots_sum(): pl.pallas_call(functools.partial(allreduce_kernel, chips), out_shape=jax....  54.8 us
    pallas_call x2, Pallas kernels, exchange(): pl.pallas_call(functools.partial(halo_kernel, n), out_shape=jax.ShapeDtyp...  40.8 us
    dot_general x8, matrix products, exact_einsum(): jnp.einsum(spec, a, b, precision=lax.Precision.HIGHEST, preferred_element...  5.11 us
    add x2, other arithmetic, laplace(): total = total + COEF[shift_k] * (side_y + side_x)  4.91 us
    reshape x2, local copies, waits for them, and re-layouts, exchange(): return recv.reshape(shape)  3.3 us
    reshape x2, local copies, waits for them, and re-layouts, exchange(): both.reshape(2, total, 128)  2.67 us

profile of v15, /device:TPU:25, one launch (start us, length us, event | category | flops | bytes accessed | tf_op | source)
XLA Modules:
  0.0 123.7 jit_solution(4416057032475430962)
XLA Ops:
  0.7 1.3 %fusion.73 = (f32[1,2,2,4,64,128]{5,4,3,2,1,0:T(8,128)S(1)}, f32[1,2,2,4,64,128]{5,4,3,2,1,0:T(8,128)S(1)}) fusion(f32[1,2,8,64,128]{4,3,2,1,0:T(8,128)} %bitcast.108, f32[1,2,8,64,128]{4,3,2,1,0:T(8,128)} %bitcast.111), kind=kLoop, calls=%fused_computation.140 | loop fusion | flops 262144 | bytes 2097152 | tf_op jit(solution)/shard_map/stack | solution.py:122
  2.1 0.7 convolution_bitcast_fusion.3
  2.9 0.6 convolution_bitcast_fusion.5
  3.5 1.3 %reshape.247.send_ref = f32[2,484,128]{2,1,0:T(8,128)} reshape(f32[2,2,2,4,44,88]{5,4,3,2,1,0:T(8,128)S(1)} %copy.22) | data formatting | bytes 991232 | tf_op jit(solution)/shard_map/reshape | solution.py:116
  4.9 22.9 %shard_map.148 = f32[2,484,128]{2,1,0:T(8,128)} custom-call(f32[2,484,128]{2,1,0:T(8,128)} %reshape.247.send_ref), custom_call_target="tpu_custom_call" | custom-call | tf_op jit(solution)/shard_map/pallas_call | solution.py:109
  27.8 1.7 %reshape.248 = f32[2,2,2,4,44,88]{5,4,3,2,1,0:T(8,128)S(1)} reshape(f32[2,484,128]{2,1,0:T(8,128)} %shard_map.148) | data formatting | bytes 991232 | tf_op jit(solution)/shard_map/reshape | solution.py:117
  29.5 0.1 pad_add_fusion
  29.5 0.6 convolution_bitcast_fusion.7
  30.2 0.7 convolution_bitcast_fusion.2
  30.9 0.1 slice_bitcast_fusion.7
  31.0 0.2 copy-done
  31.2 0.2 copy-done.1
  31.4 0.4 pad_maximum_fusion
  31.9 2.5 %fusion.6 = f32[2,2,8,64,128]{4,3,2,1,0:T(8,128)S(1)} fusion(f32[2,2,8,64,128]{4,3,2,1,0:T(8,128)S(1)} %pad_maximum_fusion.2, f32[2,2,12,64,128]{4,3,2,1,0:T(8,128)S(1)} %get-tuple-element.19, f32[2,2,12,64,128]{4,3,2,1,0:T(8,128)S(1)} %get-tuple-element.18), kind=kLoop, calls=%fused_computation.60 | loop fusion | flops 8650752 | bytes 10485760 | tf_op jit(solution)/shard_map/add | solution.py:161
  34.4 0.8 fusion.60
  35.5 0.1 and_convert_fusion
  35.6 1.7 %fusion.85 = (f32[2,8,64,128]{3,2,1,0:T(8,128)S(1)}, f32[2,8,64,128]{3,2,1,0:T(8,128)S(1)}) fusion(f32[2,8,64,128]{3,2,1,0:T(8,128)S(1)} %bitcast.122, f32[2,2,8,64,128]{4,3,2,1,0:T(8,128)S(1)} %fusion.6, f32[2,8,64,128]{3,2,1,0:T(8,128)} %param.15, f32[2,8,64,128]{3,2,1,0:T(8,128)S(1)} %copy-done.1, f32[8,64,128]{2,1,0:T(8,128)S(1)} %copy-done.3, ...), kind=kLoop, calls=%fused_computation.157 | loop fusion | flops 1835008 | bytes 5047560 | tf_op jit(solution)/shard_map/mul | solution.py:347
  37.4 0.6 convolution_bitcast_fusion.1
  38.1 0.6 convolution_bitcast_fusion.4
  38.7 1.3 %reshape.250.send_ref = f32[2,484,128]{2,1,0:T(8,128)} reshape(f32[2,2,2,4,44,88]{5,4,3,2,1,0:T(8,128)S(1)} %copy.25) | data formatting | bytes 991232 | tf_op jit(solution)/shard_map/reshape | solution.py:116
  40.1 17.9 %shard_map.149 = f32[2,484,128]{2,1,0:T(8,128)} custom-call(f32[2,484,128]{2,1,0:T(8,128)} %reshape.250.send_ref), custom_call_target="tpu_custom_call" | custom-call | tf_op jit(solution)/shard_map/pallas_call | solution.py:109
  57.9 1.7 %reshape.251 = f32[2,2,2,4,44,88]{5,4,3,2,1,0:T(8,128)S(1)} reshape(f32[2,484,128]{2,1,0:T(8,128)} %shard_map.149) | data formatting | bytes 991232 | tf_op jit(solution)/shard_map/reshape | solution.py:117
  59.6 0.6 convolution_bitcast_fusion.6
  60.2 0.7 convolution_bitcast_fusion
  60.9 0.1 slice_bitcast_fusion.3
  61.0 0.4 pad_maximum_fusion.1
  61.5 2.5 %fusion.26 = f32[2,2,8,64,128]{4,3,2,1,0:T(8,128)S(1)} fusion(f32[2,2,8,64,128]{4,3,2,1,0:T(8,128)S(1)} %pad_maximum_fusion.3, f32[2,2,12,64,128]{4,3,2,1,0:T(8,128)S(1)} %get-tuple-element.13, f32[2,2,12,64,128]{4,3,2,1,0:T(8,128)S(1)} %get-tuple-element.12), kind=kLoop, calls=%fused_computation.80 | loop fusion | flops 8650752 | bytes 10485760 | tf_op jit(solution)/shard_map/add | solution.py:161
  64.0 0.8 fusion.58
  64.7 1.7 %multiply_reduce_fusion = (f32[8,64,128]{2,1,0:T(8,128)S(1)}, f32[8,64,128]{2,1,0:T(8,128)S(1)}, f32[2,8,64,128]{3,2,1,0:T(8,128)}, f32[2,8,64,128]{3,2,1,0:T(8,128)}) fusion(f32[2,8,64,128]{3,2,1,0:T(8,128)S(1)} %copy-done, f32[2,8,64,128]{3,2,1,0:T(8,128)S(1)} %get-tuple-element.11, f32[2,8,64,128]{3,2,1,0:T(8,128)S(1)} %get-tuple-element.10, ...), kind=kLoop, calls=%fused_computation.163 | loop fusion | flops 2883584 | bytes 6096136 | tf_op jit(solution)/shard_map/reduce_sum | solution.py:348
  66.4 0.7 add.297
  67.1 54.8 %shard_map.150 = f32[512,128]{1,0:T(8,128)} custom-call(f32[512,128]{1,0:T(8,128)} %bitcast.120), custom_call_target="tpu_custom_call" | custom-call | tf_op jit(solution)/shard_map/pallas_call | solution.py:299
  122.0 1.7 %copy.51 = f32[8,64,128]{2,1,0:T(8,128)} copy(f32[8,64,128]{2,1,0:T(8,128)} %bitcast.121) | data formatting | bytes 524288
  (40 shorter events, 0.9 us)
Async XLA Ops:
  0.6 1.4 %copy-start.9 = (s32[2]{0:T(128)S(1)}, s32[2]{0:T(128)}, u32[]{:S(2)}) copy-start(s32[2]{0:T(128)} %param.22) | copy-start | bytes 28
  0.6 1.4 %copy-start.10 = (s32[2]{0:T(128)S(1)}, s32[2]{0:T(128)}, u32[]{:S(2)}) copy-start(s32[2]{0:T(128)} %param.24) | copy-start | bytes 28
  2.0 0.8 copy-start.7
  2.0 0.8 copy-start.8
  30.2 1.0 copy-start
  30.2 1.2 copy-start.1
  31.8 2.5 %copy-start.5 = (s32[2,256]{1,0:T(2,128)S(1)}, s32[2,256]{1,0:T(2,128)}, u32[]{:S(2)}) copy-start(s32[2,256]{1,0:T(2,128)} %param.25) | copy-start | bytes 6148
  31.9 2.6 %copy-start.4 = (f32[2,2,256]{2,1,0:T(2,128)S(1)}, f32[2,2,256]{2,1,0:T(2,128)}, u32[]{:S(2)}) copy-start(f32[2,2,256]{2,1,0:T(2,128)} %param.19) | copy-start | bytes 12292
  31.9 3.3 %copy-start.11 = (s32[2]{0:T(128)S(1)}, s32[2]{0:T(128)}, u32[]{:S(2)}) copy-start(s32[2]{0:T(128)} %param.20) | copy-start | bytes 28
  31.9 3.7 %copy-start.6 = (f32[2,2]{1,0:T(2,128)S(1)}, f32[2,2]{1,0:T(2,128)}, u32[]{:S(2)}) copy-start(f32[2,2]{1,0:T(2,128)} %param.18) | copy-start | bytes 52
  31.9 3.7 %copy-start.3 = (f32[8,64,128]{2,1,0:T(8,128)S(1)}, f32[8,64,128]{2,1,0:T(8,128)}, u32[]{:S(2)}) copy-start(f32[8,64,128]{2,1,0:T(8,128)} %param.17) | copy-start | bytes 786436
  61.5 3.2 %copy-start.2 = (f32[2,8,64,128]{3,2,1,0:T(8,128)S(1)}, f32[2,8,64,128]{3,2,1,0:T(8,128)}, u32[]{:S(2)}) copy-start(f32[2,8,64,128]{3,2,1,0:T(8,128)} %param.13) | copy-start | bytes 1572868

commit v16 on v15

--- a/solution.py
+++ b/solution.py
@@ -230,7 +230,7 @@
     return piece.reshape(shape)
 
 
-def allreduce_kernel(chips, local_ref, out_ref, half_in, gathered, spread, send_sems, recv_sems):
+def allreduce_kernel(chips, local_ref, out_ref, half_in, own_half, gathered, spread, send_sems, recv_sems, local_sem):
     me = lax.axis_index("shots")
     slab = lax.axis_index("slab")
     core = me % 2
@@ -257,10 +257,13 @@
 
     mine = pl.ds(pl.multiple_of(core * rows, 8), rows)
     theirs = pl.ds(pl.multiple_of((1 - core) * rows, 8), rows)
+    fetch = pltpu.make_async_copy(local_ref.at[mine], own_half, local_sem)
+    fetch.start()
     copy = remote(local_ref.at[theirs], half_in, 0, me + 1 - 2 * core)
     copy.start()
+    fetch.wait()
     copy.wait()
-    out_ref[mine] = local_ref[mine] + half_in[...]
+    out_ref[mine] = own_half[...] + half_in[...]
     copies = []
     for k in range(1, chips):
         target = lax.rem(chip + k, chips)
@@ -299,14 +302,16 @@
     out = pl.pallas_call(
         functools.partial(allreduce_kernel, chips),
         out_shape=jax.ShapeDtypeStruct(chunks.shape, jnp.float32),
-        in_specs=[pl.BlockSpec(memory_space=pltpu.VMEM)],
+        in_specs=[pl.BlockSpec(memory_space=pl.ANY)],
         out_specs=pl.BlockSpec(memory_space=pltpu.VMEM),
         scratch_shapes=[
+            pltpu.VMEM((rows // 2, 128), jnp.float32),
             pltpu.VMEM((rows // 2, 128), jnp.float32),
             pltpu.VMEM((chips, rows // 2 // chips, 128), jnp.float32),
             pltpu.VMEM((chips, rows // 2 // chips, 128), jnp.float32),
             pltpu.SemaphoreType.DMA((2 * chips + 1,)),
             pltpu.SemaphoreType.DMA((2 * chips + 1,)),
+            pltpu.SemaphoreType.DMA(()),
         ],
         compiler_params=pltpu.CompilerParams(collective_id=0, has_side_effects=True),
     )(chunks)

time: 124 us -> 124 us (level)
  no operation moved by 1% of the time
where the time goes in v16:
time: 124 us; the launch traced here: 123 us
  Pallas kernels  94.9 us (77%)
  other arithmetic  11.9 us (10%)
  local copies, waits for them, and re-layouts  8.42 us (7%)
  matrix products  6.63 us (5%)
    pallas_call x1, Pallas kernels, shots_sum(): pl.pallas_call(functools.partial(allreduce_kernel, chips), out_shape=jax....  54.1 us
    pallas_call x2, Pallas kernels, exchange(): pl.pallas_call(functools.partial(halo_kernel, n), out_shape=jax.ShapeDtyp...  40.8 us
    dot_general x8, matrix products, exact_einsum(): jnp.einsum(spec, a, b, precision=lax.Precision.HIGHEST, preferred_element...  5.11 us
    add x2, other arithmetic, laplace(): total = total + COEF[shift_k] * (side_y + side_x)  4.91 us
    reshape x2, local copies, waits for them, and re-layouts, exchange(): return recv.reshape(shape)  3.3 us
    reshape x2, local copies, waits for them, and re-layouts, exchange(): both.reshape(2, total, 128)  2.67 us

profile of v16, /device:TPU:25, one launch (start us, length us, event | category | flops | bytes accessed | tf_op | source)
XLA Modules:
  0.0 123.0 jit_solution(15427996861513629255)
XLA Ops:
  0.7 1.3 %fusion.73 = (f32[1,2,2,4,64,128]{5,4,3,2,1,0:T(8,128)S(1)}, f32[1,2,2,4,64,128]{5,4,3,2,1,0:T(8,128)S(1)}) fusion(f32[1,2,8,64,128]{4,3,2,1,0:T(8,128)} %bitcast.108, f32[1,2,8,64,128]{4,3,2,1,0:T(8,128)} %bitcast.111), kind=kLoop, calls=%fused_computation.140 | loop fusion | flops 262144 | bytes 2097152 | tf_op jit(solution)/shard_map/stack | solution.py:122
  2.1 0.7 convolution_bitcast_fusion.3
  2.9 0.6 convolution_bitcast_fusion.5
  3.5 1.3 %reshape.247.send_ref = f32[2,484,128]{2,1,0:T(8,128)} reshape(f32[2,2,2,4,44,88]{5,4,3,2,1,0:T(8,128)S(1)} %copy.22) | data formatting | bytes 991232 | tf_op jit(solution)/shard_map/reshape | solution.py:116
  4.9 22.9 %shard_map.148 = f32[2,484,128]{2,1,0:T(8,128)} custom-call(f32[2,484,128]{2,1,0:T(8,128)} %reshape.247.send_ref), custom_call_target="tpu_custom_call" | custom-call | tf_op jit(solution)/shard_map/pallas_call | solution.py:109
  27.8 1.7 %reshape.248 = f32[2,2,2,4,44,88]{5,4,3,2,1,0:T(8,128)S(1)} reshape(f32[2,484,128]{2,1,0:T(8,128)} %shard_map.148) | data formatting | bytes 991232 | tf_op jit(solution)/shard_map/reshape | solution.py:117
  29.5 0.1 pad_add_fusion
  29.5 0.6 convolution_bitcast_fusion.7
  30.2 0.7 convolution_bitcast_fusion.2
  30.9 0.1 slice_bitcast_fusion.7
  31.0 0.2 copy-done
  31.2 0.2 copy-done.1
  31.4 0.4 pad_maximum_fusion
  31.9 2.5 %fusion.6 = f32[2,2,8,64,128]{4,3,2,1,0:T(8,128)S(1)} fusion(f32[2,2,8,64,128]{4,3,2,1,0:T(8,128)S(1)} %pad_maximum_fusion.2, f32[2,2,12,64,128]{4,3,2,1,0:T(8,128)S(1)} %get-tuple-element.19, f32[2,2,12,64,128]{4,3,2,1,0:T(8,128)S(1)} %get-tuple-element.18), kind=kLoop, calls=%fused_computation.60 | loop fusion | flops 8650752 | bytes 10485760 | tf_op jit(solution)/shard_map/add | solution.py:161
  34.4 0.8 fusion.60
  35.5 0.1 and_convert_fusion
  35.6 1.7 %fusion.85 = (f32[2,8,64,128]{3,2,1,0:T(8,128)S(1)}, f32[2,8,64,128]{3,2,1,0:T(8,128)S(1)}) fusion(f32[2,8,64,128]{3,2,1,0:T(8,128)S(1)} %bitcast.122, f32[2,2,8,64,128]{4,3,2,1,0:T(8,128)S(1)} %fusion.6, f32[2,8,64,128]{3,2,1,0:T(8,128)} %param.15, f32[2,8,64,128]{3,2,1,0:T(8,128)S(1)} %copy-done.1, f32[8,64,128]{2,1,0:T(8,128)S(1)} %copy-done.3, ...), kind=kLoop, calls=%fused_computation.157 | loop fusion | flops 1835008 | bytes 5047560 | tf_op jit(solution)/shard_map/mul | solution.py:352
  37.4 0.6 convolution_bitcast_fusion.1
  38.1 0.6 convolution_bitcast_fusion.4
  38.7 1.3 %reshape.250.send_ref = f32[2,484,128]{2,1,0:T(8,128)} reshape(f32[2,2,2,4,44,88]{5,4,3,2,1,0:T(8,128)S(1)} %copy.25) | data formatting | bytes 991232 | tf_op jit(solution)/shard_map/reshape | solution.py:116
  40.1 17.9 %shard_map.149 = f32[2,484,128]{2,1,0:T(8,128)} custom-call(f32[2,484,128]{2,1,0:T(8,128)} %reshape.250.send_ref), custom_call_target="tpu_custom_call" | custom-call | tf_op jit(solution)/shard_map/pallas_call | solution.py:109
  57.9 1.7 %reshape.251 = f32[2,2,2,4,44,88]{5,4,3,2,1,0:T(8,128)S(1)} reshape(f32[2,484,128]{2,1,0:T(8,128)} %shard_map.149) | data formatting | bytes 991232 | tf_op jit(solution)/shard_map/reshape | solution.py:117
  59.6 0.6 convolution_bitcast_fusion.6
  60.2 0.7 convolution_bitcast_fusion
  60.9 0.1 slice_bitcast_fusion.3
  61.0 0.4 pad_maximum_fusion.1
  61.5 2.5 %fusion.26 = f32[2,2,8,64,128]{4,3,2,1,0:T(8,128)S(1)} fusion(f32[2,2,8,64,128]{4,3,2,1,0:T(8,128)S(1)} %pad_maximum_fusion.3, f32[2,2,12,64,128]{4,3,2,1,0:T(8,128)S(1)} %get-tuple-element.13, f32[2,2,12,64,128]{4,3,2,1,0:T(8,128)S(1)} %get-tuple-element.12), kind=kLoop, calls=%fused_computation.80 | loop fusion | flops 8650752 | bytes 10485760 | tf_op jit(solution)/shard_map/add | solution.py:161
  64.0 0.8 fusion.58
  64.7 1.7 %multiply_reduce_fusion = (f32[8,64,128]{2,1,0:T(8,128)S(1)}, f32[8,64,128]{2,1,0:T(8,128)S(1)}, f32[2,8,64,128]{3,2,1,0:T(8,128)}, f32[2,8,64,128]{3,2,1,0:T(8,128)}) fusion(f32[2,8,64,128]{3,2,1,0:T(8,128)S(1)} %copy-done, f32[2,8,64,128]{3,2,1,0:T(8,128)S(1)} %get-tuple-element.11, f32[2,8,64,128]{3,2,1,0:T(8,128)S(1)} %get-tuple-element.10, ...), kind=kLoop, calls=%fused_computation.163 | loop fusion | flops 2883584 | bytes 6096136 | tf_op jit(solution)/shard_map/reduce_sum | solution.py:353
  66.4 0.7 add.297
  67.1 54.1 %shard_map.150 = f32[512,128]{1,0:T(8,128)} custom-call(f32[512,128]{1,0:T(8,128)} %bitcast.120), custom_call_target="tpu_custom_call" | custom-call | tf_op jit(solution)/shard_map/pallas_call | solution.py:302
  121.3 1.7 %copy.51 = f32[8,64,128]{2,1,0:T(8,128)} copy(f32[8,64,128]{2,1,0:T(8,128)} %bitcast.121) | data formatting | bytes 524288
  (40 shorter events, 0.9 us)
Async XLA Ops:
  0.6 1.4 %copy-start.9 = (s32[2]{0:T(128)S(1)}, s32[2]{0:T(128)}, u32[]{:S(2)}) copy-start(s32[2]{0:T(128)} %param.22) | copy-start | bytes 28
  0.6 1.4 %copy-start.10 = (s32[2]{0:T(128)S(1)}, s32[2]{0:T(128)}, u32[]{:S(2)}) copy-start(s32[2]{0:T(128)} %param.24) | copy-start | bytes 28
  2.0 0.8 copy-start.7
  2.0 0.8 copy-start.8
  30.2 1.0 copy-start
  30.2 1.2 copy-start.1
  31.8 2.5 %copy-start.5 = (s32[2,256]{1,0:T(2,128)S(1)}, s32[2,256]{1,0:T(2,128)}, u32[]{:S(2)}) copy-start(s32[2,256]{1,0:T(2,128)} %param.25) | copy-start | bytes 6148
  31.9 2.6 %copy-start.4 = (f32[2,2,256]{2,1,0:T(2,128)S(1)}, f32[2,2,256]{2,1,0:T(2,128)}, u32[]{:S(2)}) copy-start(f32[2,2,256]{2,1,0:T(2,128)} %param.19) | copy-start | bytes 12292
  31.9 3.3 %copy-start.11 = (s32[2]{0:T(128)S(1)}, s32[2]{0:T(128)}, u32[]{:S(2)}) copy-start(s32[2]{0:T(128)} %param.20) | copy-start | bytes 28
  31.9 3.7 %copy-start.6 = (f32[2,2]{1,0:T(2,128)S(1)}, f32[2,2]{1,0:T(2,128)}, u32[]{:S(2)}) copy-start(f32[2,2]{1,0:T(2,128)} %param.18) | copy-start | bytes 52
  31.9 3.7 %copy-start.3 = (f32[8,64,128]{2,1,0:T(8,128)S(1)}, f32[8,64,128]{2,1,0:T(8,128)}, u32[]{:S(2)}) copy-start(f32[8,64,128]{2,1,0:T(8,128)} %param.17) | copy-start | bytes 786436
  61.5 3.2 %copy-start.2 = (f32[2,8,64,128]{3,2,1,0:T(8,128)S(1)}, f32[2,8,64,128]{3,2,1,0:T(8,128)}, u32[]{:S(2)}) copy-start(f32[2,8,64,128]{3,2,1,0:T(8,128)} %param.13) | copy-start | bytes 1572868
